TPU v7x, 32 devices: a whole 2x2x4 slice. The times are simulated.
32 devices in a mesh: space: 16 (over z, x, core), chan: 2 (over y).
Axes of the slice: x: 2, y: 2, z: 4, core: 2. Of those that a mesh axis runs over, the one named last changes fastest.
Arguments:
- volume: bfloat16 [256, 16, 8, 128], P('chan', 'space'), may hold values from -6 to 6
- w_first: bfloat16 [256, 27, 256], P(None, None, 'chan'), may hold values from -0.078125 to 0.078125
- b_first: float32 [256], P('chan'), may hold values from -1.8 to 1.8
- w_second: bfloat16 [256, 27, 256], P('chan'), may hold values from -0.125 to 0.125
- b_second: float32 [256], P('chan'), may hold values from -1.8 to 1.8
Outputs:
- result: bfloat16 [256, 16, 8, 128], P('chan', 'space')
All inputs are finite; a program needn't handle non-finite values.
Results may differ from a plain program's by a relative error of at most 0.011.
Values may be sent and summed in bfloat16 or wider, within the bound.
No kernel may reach another device: no remote copies, remote signals or barrier semaphores. Data moves between devices by JAX's collectives and lax.ppermute only.
A program may use at most 64 MiB of HBM per device.

v0:
```python
import jax
import jax.numpy as jnp
from jax import lax
from jax.sharding import PartitionSpec as P


def with_halo(cells, sides, width):
    for axis, dim in sides:
        count = lax.axis_size(axis)
        ends = count - 1
        head = lax.slice_in_dim(cells, 0, width, axis=dim)
        tail = lax.slice_in_dim(cells, cells.shape[dim] - width, cells.shape[dim], axis=dim)
        cells = jnp.concatenate(
            [
                lax.ppermute(tail, axis, [(i, (i + 1) % count) for i in range(ends)]),
                cells,
                lax.ppermute(head, axis, [((i + 1) % count, i) for i in range(ends)]),
            ],
            axis=dim,
        )
    return cells


def apply_taps(slab, weights, row_pad):
    kernel = weights.reshape(weights.shape[0], 3, 3, 3, weights.shape[2])
    summed = lax.conv_general_dilated(
        slab[None],
        kernel,
        (1, 1, 1),
        [(0, 0), (row_pad, row_pad), (1, 1)],
        dimension_numbers=("NCDHW", "IDHWO", "NCDHW"),
        preferred_element_type=jnp.float32,
    )
    return summed[0]


def per_device(volume, w_first, b_first, w_second, b_second):
    gathered = lax.all_gather(volume, "chan", axis=0, tiled=True)
    framed = with_halo(gathered, (("space", 1),), 1)
    first_sum = apply_taps(framed, w_first, 1)
    hidden = jax.nn.relu(first_sum + b_first[:, None, None, None]).astype(jnp.bfloat16)
    beside_all = with_halo(hidden, (("space", 1),), 1)
    second_sum = lax.psum_scatter(
        apply_taps(beside_all, w_second, 1).astype(jnp.bfloat16),
        "chan",
        scatter_dimension=0,
        tiled=True,
    ).astype(jnp.float32)
    return jax.nn.relu(second_sum + b_second[:, None, None, None]).astype(jnp.bfloat16)


def solution(mesh):
    in_specs = (
        P("chan", "space", None, None),
        P(None, None, "chan"),
        P("chan"),
        P("chan", None, None),
        P("chan"),
    )
    out_specs = P("chan", "space", None, None)
    return jax.shard_map(
        per_device, mesh=mesh, in_specs=in_specs, out_specs=out_specs, check_vma=False
    )
```

profile of v0, /device:TPU:9, one launch (start us, length us, event | category | flops | bytes accessed | tf_op | source)
XLA Modules:
  0.0 112.4 jit_solution(8084966245108863844)
XLA Ops:
  6.5 0.0 copy-start
  6.5 0.0 reduce-scatter.4.cloned.1.call-start
  6.5 1.3 %copy.15 = bf16[128,1,8,128]{0,2,3,1:T(8,128)(2,1)S(1)} copy(bf16[128,1,8,128]{3,2,1,0:T(8,128)(2,1)} %param.5) | data formatting | bytes 524288 | tf_op args[0]
  7.9 7.9 %all_gather.3 = bf16[256,1,8,128]{0,2,3,1:T(8,128)(2,1)S(1)} all-gather(bf16[128,1,8,128]{0,2,3,1:T(8,128)(2,1)S(1)} %copy.15), channel_id=1, replica_groups=mesh['space'=16,'chan'=2] {'chan'}, dimensions={0}, use_global_device_ids=true | all-gather | bytes 786432 | tf_op jit(solution)/shard_map/all_gather | solution.py:38
  15.8 3.4 %collective-permute-start.1 = (bf16[256,1,8,128]{0,2,3,1:T(8,128)(2,1)S(1)}, bf16[256,1,8,128]{0,2,3,1:T(8,128)(2,1)S(1)}, u32[]{:S(2)}, u32[]{:S(2)}) collective-permute-start(bf16[256,1,8,128]{0,2,3,1:T(8,128)(2,1)S(1)} %all_gather.3), channel_id=1, source_target_pairs={{2,0},{4,2},{6,4},{8,6},{10,8},{12,10},{14,12},{16,14},{18,16},{20... | collective-permute-start | bytes 1572872 | tf_op jit(solution)/shard_map/ppermute | solution.py:17
  19.2 3.0 %collective-permute-start = (bf16[256,1,8,128]{0,2,3,1:T(8,128)(2,1)S(1)}, bf16[256,1,8,128]{0,2,3,1:T(8,128)(2,1)S(1)}, u32[]{:S(2)}, u32[]{:S(2)}) collective-permute-start(bf16[256,1,8,128]{0,2,3,1:T(8,128)(2,1)S(1)} %all_gather.3), channel_id=1, source_target_pairs={{0,2},{2,4},{4,6},{6,8},{8,10},{10,12},{12,14},{14,16},{16,18},{18... | collective-permute-start | bytes 1572872 | tf_op jit(solution)/shard_map/ppermute | solution.py:15
  22.2 10.5 %collective-permute-done.1 = bf16[256,1,8,128]{0,2,3,1:T(8,128)(2,1)S(1)} collective-permute-done((bf16[256,1,8,128]{0,2,3,1:T(8,128)(2,1)S(1)}, bf16[256,1,8,128]{0,2,3,1:T(8,128)(2,1)S(1)}, u32[]{:S(2)}, u32[]{:S(2)}) %collective-permute-start.1) | collective-permute-done | bytes 524320 | tf_op jit(solution)/shard_map/ppermute | solution.py:17
  32.8 0.0 collective-permute-done
  32.8 0.2 maximum_bitcast_fusion
  32.9 0.1 pad
  33.1 0.0 copy-start.3
  33.1 0.0 copy-start.4
  33.1 0.3 copy.17
  33.5 1.1 copy-done.3
  34.5 0.0 copy-done.4
  34.5 0.0 copy-start.2
  34.5 4.1 %fusion.10 = f32[1,8,8,17,128]{4,2,3,1,0:T(8,128)S(1)} fusion(bf16[256,3,3,3,128]{4,0,3,2,1:T(8,128)(2,1)S(1)} %bitcast.46, bf16[256,3,8,1,7,2]{0,4,5,2,1,3:T(8,128)(2,1)S(1)} %slice.4, bf16[256,3,8,1,8,17]{0,4,5,2,1,3:T(8,128)(2,1)S(1)} %copy.17, pred[8,17]{0,1:T(8,128)(4,1)S(1)} %copy-done.4), kind=kOutput, calls=%fused_computation.13 | convolution fusion | flops 1770496000 | bytes 4169864 | tf_op jit(solution)/shard_map/conv_general_dilated | solution.py:26
  38.7 0.1 copy.18
  38.8 0.0 copy-done.2
  38.8 0.1 fusion.22
  38.8 1.9 %collective-permute-start.3 = (bf16[128,1,8,128]{0,2,3,1:T(8,128)(2,1)S(1)}, bf16[128,1,8,128]{0,2,3,1:T(8,128)(2,1)S(1)}, u32[]{:S(2)}, u32[]{:S(2)}) collective-permute-start(bf16[128,1,8,128]{0,2,3,1:T(8,128)(2,1)S(1)} %fusion.22), channel_id=1, source_target_pairs={{2,0},{4,2},{6,4},{8,6},{10,8},{12,10},{14,12},{16,14},{18,16},{20... | collective-permute-start | bytes 786440 | tf_op jit(solution)/shard_map/ppermute | solution.py:17
  40.8 3.9 %collective-permute-start.2 = (bf16[128,1,8,128]{0,2,3,1:T(8,128)(2,1)S(1)}, bf16[128,1,8,128]{0,2,3,1:T(8,128)(2,1)S(1)}, u32[]{:S(2)}, u32[]{:S(2)}) collective-permute-start(bf16[128,1,8,128]{0,2,3,1:T(8,128)(2,1)S(1)} %fusion.22), channel_id=1, source_target_pairs={{0,2},{2,4},{4,6},{6,8},{8,10},{10,12},{12,14},{14,16},{16,18},{18... | collective-permute-start | bytes 786440 | tf_op jit(solution)/shard_map/ppermute | solution.py:15
  44.7 4.7 %collective-permute-done.3 = bf16[128,1,8,128]{0,2,3,1:T(8,128)(2,1)S(1)} collective-permute-done((bf16[128,1,8,128]{0,2,3,1:T(8,128)(2,1)S(1)}, bf16[128,1,8,128]{0,2,3,1:T(8,128)(2,1)S(1)}, u32[]{:S(2)}, u32[]{:S(2)}) %collective-permute-start.3) | collective-permute-done | bytes 262176 | tf_op jit(solution)/shard_map/ppermute | solution.py:17
  49.5 0.0 collective-permute-done.2
  49.5 0.1 maximum_bitcast_fusion.1
  49.6 0.1 pad.2
  49.6 0.1 copy.20
  49.8 0.0 copy-done
  49.8 2.2 %fusion.9 = bf16[1,8,8,17,256]{4,2,3,1,0:T(8,128)(2,1)S(1)} fusion(bf16[128,3,3,3,256]{4,0,3,2,1:T(8,128)(2,1)S(1)} %bitcast.39, bf16[128,3,8,1,7,2]{0,4,5,2,1,3:T(8,128)(2,1)S(1)} %slice.6, bf16[128,3,8,1,8,17]{0,4,5,2,1,3:T(8,128)(2,1)S(1)} %copy.20, pred[8,17]{0,1:T(8,128)(4,1)S(1)} %copy-done.4), kind=kOutput, calls=%fused_computation.12 | convolution fusion | flops 1768112128 | bytes 3248264 | tf_op jit(solution)/shard_map/conv_general_dilated | solution.py:26
  52.0 0.1 copy.21
  52.2 11.8 %copy.23 = bf16[256,1,8,128]{2,3,1,0:T(8,128)(2,1)} copy(bf16[256,1,8,128]{0,2,3,1:T(8,128)(2,1)S(1)} %slice_bitcast_fusion) | data formatting | bytes 1048576
  63.9 13.5 %reshape.71 = bf16[256,1024]{1,0:T(8,128)(2,1)} reshape(bf16[256,1,128,8]{3,2,1,0:T(8,128)(2,1)} %bitcast.40) | data formatting | bytes 1048576
  77.4 0.0 reduce-scatter.4.cloned.1.call-update
  77.4 14.8 %reduce-scatter.4.cloned.1.call-done = bf16[128,1024]{1,0:T(8,128)(2,1)} async-done(((bf16[256,1024]{1,0:T(8,128)(2,1)}), bf16[128,1024]{1,0:T(8,128)(2,1)}) %reduce-scatter.4.cloned.1.call-update) | async-done | bytes 262160
  92.3 6.8 %reshape.72 = bf16[128,1,128,8]{3,2,1,0:T(8,128)(2,1)} reshape(bf16[128,1024]{1,0:T(8,128)(2,1)} %reduce-scatter.4.cloned.1.call-done) | data formatting | bytes 524288
  99.1 0.0 copy-start.1
  99.1 5.5 %copy.24 = bf16[128,1,8,128]{0,2,3,1:T(8,128)(2,1)S(1)} copy(bf16[128,1,8,128]{2,3,1,0:T(8,128)(2,1)} %bitcast.41) | data formatting | bytes 524288
  104.6 0.0 copy-done.1
  104.6 0.1 maximum_convert_fusion
  104.6 0.9 copy.22
  (3 shorter events, 0.1 us)
Async XLA Ops:
  6.5 43.3 %copy-start = (bf16[128,27,256]{2,0,1:T(8,128)(2,1)S(1)}, bf16[128,27,256]{2,0,1:T(8,128)(2,1)}, u32[]{:S(2)}) copy-start(bf16[128,27,256]{2,0,1:T(8,128)(2,1)} %param.8) | copy-start | bytes 5308420
  6.5 85.7 %reduce-scatter.4.cloned.1.call-start = ((), (), s32[]{:S(2)}) async-start(), calls=%async_computation.1 | async-start | bytes 786432
  15.8 16.9 %collective-permute-start.1 = (bf16[256,1,8,128]{0,2,3,1:T(8,128)(2,1)S(1)}, bf16[256,1,8,128]{0,2,3,1:T(8,128)(2,1)S(1)}, u32[]{:S(2)}, u32[]{:S(2)}) collective-permute-start(bf16[256,1,8,128]{0,2,3,1:T(8,128)(2,1)S(1)} %all_gather.3), channel_id=1, source_target_pairs={{2,0},{4,2},{6,4},{8,6},{10,8},{12,10},{14,12},{16,14},{18,16},{20... | collective-permute-start | bytes 1572872 | tf_op jit(solution)/shard_map/ppermute | solution.py:17
  19.2 13.6 %collective-permute-start = (bf16[256,1,8,128]{0,2,3,1:T(8,128)(2,1)S(1)}, bf16[256,1,8,128]{0,2,3,1:T(8,128)(2,1)S(1)}, u32[]{:S(2)}, u32[]{:S(2)}) collective-permute-start(bf16[256,1,8,128]{0,2,3,1:T(8,128)(2,1)S(1)} %all_gather.3), channel_id=1, source_target_pairs={{0,2},{2,4},{4,6},{6,8},{8,10},{10,12},{12,14},{14,16},{16,18},{18... | collective-permute-start | bytes 1572872 | tf_op jit(solution)/shard_map/ppermute | solution.py:15
  33.1 1.5 %copy-start.3 = (bf16[256,27,128]{2,0,1:T(8,128)(2,1)S(1)}, bf16[256,27,128]{2,0,1:T(8,128)(2,1)}, u32[]{:S(2)}) copy-start(bf16[256,27,128]{2,0,1:T(8,128)(2,1)} %param.6) | copy-start | bytes 5308420
  33.1 1.5 %copy-start.4 = (pred[8,17]{0,1:T(8,128)(4,1)S(1)}, pred[8,17]{0,1:T(8,128)(4,1)}, u32[]{:S(2)}) copy-start(pred[8,17]{0,1:T(8,128)(4,1)} %constant.13) | copy-start | bytes 412
  34.5 4.2 %copy-start.2 = (f32[128]{0:T(128)S(1)}, f32[128]{0:T(128)}, u32[]{:S(2)}) copy-start(f32[128]{0:T(128)} %param.7) | copy-start | bytes 1540
  38.8 10.6 %collective-permute-start.3 = (bf16[128,1,8,128]{0,2,3,1:T(8,128)(2,1)S(1)}, bf16[128,1,8,128]{0,2,3,1:T(8,128)(2,1)S(1)}, u32[]{:S(2)}, u32[]{:S(2)}) collective-permute-start(bf16[128,1,8,128]{0,2,3,1:T(8,128)(2,1)S(1)} %fusion.22), channel_id=1, source_target_pairs={{2,0},{4,2},{6,4},{8,6},{10,8},{12,10},{14,12},{16,14},{18,16},{20... | collective-permute-start | bytes 786440 | tf_op jit(solution)/shard_map/ppermute | solution.py:17
  40.8 8.7 %collective-permute-start.2 = (bf16[128,1,8,128]{0,2,3,1:T(8,128)(2,1)S(1)}, bf16[128,1,8,128]{0,2,3,1:T(8,128)(2,1)S(1)}, u32[]{:S(2)}, u32[]{:S(2)}) collective-permute-start(bf16[128,1,8,128]{0,2,3,1:T(8,128)(2,1)S(1)} %fusion.22), channel_id=1, source_target_pairs={{0,2},{2,4},{4,6},{6,8},{8,10},{10,12},{12,14},{14,16},{16,18},{18... | collective-permute-start | bytes 786440 | tf_op jit(solution)/shard_map/ppermute | solution.py:15
  99.1 5.5 %copy-start.1 = (f32[128]{0:T(128)S(1)}, f32[128]{0:T(128)}, u32[]{:S(2)}) copy-start(f32[128]{0:T(128)} %param.9) | copy-start | bytes 1540
Sparse Core Ops, SparseCore 0:
  77.6 14.6 reduce-scatter.3
where the time goes:
time: 114 us; the launch traced here: 112 us
  local copies, waits for them, and re-layouts  41.9 us (37%)
  waiting for transfers between devices  30.1 us (26%)
  between operations  13.6 us (12%)
  starting transfers between devices  12.2 us (11%)
  blocking collectives  7.94 us (7%)
  matrix products  6.29 us (6%)
    unnamed x15, local copies, waits for them, and re-layouts  40 us
    ppermute x2, waiting for transfers between devices, with_halo(): lax.ppermute(head, axis, [((i + 1) % count, i) for i in range(ends)])  15.3 us
    unnamed x2, waiting for transfers between devices  14.8 us
    all_gather x1, blocking collectives, per_device(): gathered = lax.all_gather(volume, 'chan', axis=0, tiled=True)  7.94 us
    ppermute x2, starting transfers between devices, with_halo(): lax.ppermute(tail, axis, [(i, (i + 1) % count) for i in range(ends)])  6.96 us
    conv_general_dilated x2, matrix products, apply_taps(): lax.conv_general_dilated(slab[None], kernel, (1, 1, 1), [(0, 0), (row_pad...  6.29 us
    ppermute x2, starting transfers between devices, with_halo(): lax.ppermute(head, axis, [((i + 1) % count, i) for i in range(ends)])  5.29 us
  transfers between devices with their start and end apart: 5, of which 3 were waited for; matrix products, arithmetic and copies ran while one was open for 0% of the time, Pallas kernels for 0%

commit v1 on v0

v1 whole, which is shorter than its diff:
```python
import functools

import jax
import jax.numpy as jnp
from jax import lax
from jax.experimental import pallas as pl
from jax.experimental.pallas import tpu as pltpu
from jax.sharding import PartitionSpec as P

F32 = jnp.float32
BF16 = jnp.bfloat16
VMEM_LIMIT = 20 << 20


def sds(shape, dtype):
    return jax.ShapeDtypeStruct(shape, dtype)


def run(kernel, outs, args, scratch=(), flops=0):
    moved = sum(a.size * a.dtype.itemsize for a in args)
    return pl.pallas_call(
        kernel,
        out_shape=outs,
        scratch_shapes=scratch,
        compiler_params=pltpu.CompilerParams(vmem_limit_bytes=VMEM_LIMIT),
        cost_estimate=pl.CostEstimate(
            flops=flops, bytes_accessed=moved, transcendentals=0
        ),
    )(*args)


def rows_last(block):
    c, h, w = block.shape
    planes = jnp.transpose(block, (1, 0, 2))
    return jnp.concatenate([planes[i].T for i in range(h)], axis=0).astype(F32)


def channels_first(cells, h, w):
    planes = jnp.stack([cells[i * w : (i + 1) * w].T for i in range(h)])
    return jnp.transpose(planes, (1, 0, 2))


def lay_columns(cells, framed, h, w):
    c = cells.shape[1]
    hw = h * w
    column = lax.broadcasted_iota(jnp.int32, (hw, 1), 0) % w
    left = jnp.where(column == 0, 0.0, pltpu.roll(cells, 1, 0))
    right = jnp.where(column == w - 1, 0.0, pltpu.roll(cells, hw - 1, 0))
    blank = jnp.zeros((w, 3 * c), BF16)
    framed[0:w] = blank
    framed[w + hw : 2 * w + hw] = blank
    framed[w : w + hw, 0:c] = left.astype(BF16)
    framed[w : w + hw, c : 2 * c] = cells.astype(BF16)
    framed[w : w + hw, 2 * c : 3 * c] = right.astype(BF16)


def nine_taps(framed, weights, h, w):
    hw = h * w
    _, c, n = weights.shape
    if c % 128 == 0:
        lhs = jnp.concatenate([framed[b * w : b * w + hw] for b in range(3)], axis=1)
        return jnp.dot(lhs, weights.reshape(9 * c, n), preferred_element_type=F32)
    total = None
    for b in range(3):
        term = jnp.dot(
            framed[b * w : b * w + hw],
            weights[3 * b : 3 * b + 3].reshape(3 * c, n),
            preferred_element_type=F32,
        )
        total = term if total is None else total + term
    return total


def depth_taps(where, weights, rows=None):
    return weights[pl.ds(where * 9, 9)] if rows is None else weights[pl.ds(where * 9, 9), rows]


def per_device(ns, nc, volume, w_first, b_first, w_second, b_second):
    cb, _, h, w = volume.shape
    hw = h * w
    ob = w_first.shape[2]
    full = w_second.shape[2]
    own_out = full // nc
    framed_in = sds(((h + 2) * w, 3 * cb), BF16)
    framed_mid = sds(((h + 2) * w, 3 * ob), BF16)
    volume = volume.reshape(cb, h, w)
    w_first = jnp.transpose(w_first, (1, 0, 2))
    w_second = jnp.transpose(w_second, (1, 0, 2))
    b_first = b_first.reshape(1, ob)
    b_second = b_second.reshape(own_out, 1, 1)

    pairs = [(i, i ^ 1) for i in range(ns)]
    beside = [(i, i + 1) for i in range(1, ns - 1, 2)]
    beside = beside + [(j, i) for i, j in beside]
    in_chip = lambda x: lax.ppermute(x, "space", pairs)
    next_chip = lambda x: lax.ppermute(x, "space", beside)
    round_chan = lambda x, k: lax.ppermute(
        x, "chan", [(i, (i + k) % nc) for i in range(nc)]
    )

    def odd():
        return lax.rem(lax.axis_index("space"), 2)

    def chan_rows(k, size):
        owner = lax.rem(lax.axis_index("chan") + nc - k, nc)
        return pl.ds(pl.multiple_of(owner * size, size), size)

    to_pair = lambda: 2 * odd()
    to_next = lambda: 2 - 2 * odd()

    def first_own(vol, wt, next_ref, pair_ref, mid_ref, framed):
        lay_columns(rows_last(vol[...]), framed, h, w)
        block = chan_rows(0, cb)
        next_ref[...] = nine_taps(framed, depth_taps(to_next(), wt, block), h, w)
        pair_ref[...] = nine_taps(framed, depth_taps(to_pair(), wt, block), h, w)
        mid_ref[...] = nine_taps(framed, depth_taps(1, wt, block), h, w)

    part = sds((hw, ob), F32)
    half = sds((hw, ob), BF16)
    arrived = [round_chan(volume, k) for k in range(1, nc)]
    own_next, own_pair, own_mid = run(
        first_own,
        [part, part, part],
        (volume, w_first),
        [pltpu.VMEM(framed_in.shape, BF16)],
        flops=54 * hw * cb * ob,
    )

    def first_sides(*refs):
        vols, (wt, next_ref, pair_ref) = refs[: nc - 1], refs[nc - 1 : nc + 2]
        to_next_ref, to_pair_ref = refs[nc + 2 : nc + 4]
        frames = refs[nc + 4 :]
        onward, across = next_ref[...], pair_ref[...]
        for k in range(1, nc):
            lay_columns(rows_last(vols[k - 1][...]), frames[k - 1], h, w)
            block = chan_rows(k, cb)
            onward += nine_taps(frames[k - 1], depth_taps(to_next(), wt, block), h, w)
            across += nine_taps(frames[k - 1], depth_taps(to_pair(), wt, block), h, w)
        to_next_ref[...] = onward.astype(BF16)
        to_pair_ref[...] = across.astype(BF16)

    to_next_part, to_pair_part, *frames = run(
        first_sides,
        [half, half] + [framed_in] * (nc - 1),
        (*arrived, w_first, own_next, own_pair),
        flops=36 * hw * cb * ob * (nc - 1),
    )
    pair_part = in_chip(to_pair_part)
    next_part = next_chip(to_next_part)

    def first_mid(*refs):
        blocks, (wt, mid_ref, pair_ref, sum_ref, edge_ref) = refs[: nc - 1], refs[nc - 1 :]
        total = mid_ref[...] + pair_ref[...].astype(F32)
        for k in range(1, nc):
            taps = depth_taps(1, wt, chan_rows(k, cb))
            total += nine_taps(blocks[k - 1], taps, h, w)
        sum_ref[...] = total
        edge_ref[...] = total.astype(BF16)

    so_far, edge_sum = run(
        first_mid,
        [part, half],
        (*frames, w_first, own_mid, pair_part),
        flops=18 * hw * cb * ob * (nc - 1),
    )
    next_edge = next_chip(edge_sum)

    def hidden_own(sum_ref, side_ref, b, out):
        total = sum_ref[...] + side_ref[...].astype(F32) + b[...]
        out[...] = jnp.maximum(total, 0.0).astype(BF16)

    hidden = run(hidden_own, half, (so_far, next_part, b_first), flops=3 * hw * ob)
    pair_hidden = in_chip(hidden)

    def second_own(cells, wt, out, framed):
        lay_columns(cells[...].astype(F32), framed, h, w)
        out[...] = nine_taps(framed, depth_taps(1, wt), h, w)

    def second_pair(cells, wt, before, out, framed):
        lay_columns(cells[...].astype(F32), framed, h, w)
        out[...] = before[...] + nine_taps(framed, depth_taps(2 - 2 * odd(), wt), h, w)

    scratch_mid = [pltpu.VMEM(framed_mid.shape, BF16)]
    whole = sds((hw, full), F32)
    second = run(second_own, whole, (hidden, w_second), scratch_mid, 18 * hw * ob * full)
    second = run(
        second_pair, whole, (pair_hidden, w_second, second), scratch_mid, 18 * hw * ob * full
    )

    def wanted(k):
        owner = lax.rem(lax.axis_index("chan") + k, nc)
        return pl.ds(pl.multiple_of(owner * own_out, own_out), own_out)

    def taps_for(wt, where, k):
        if own_out % 128 == 0:
            return wt[pl.ds(where * 9, 9), :, wanted(k)]
        owner = lax.rem(lax.axis_index("chan") + k, nc)
        taps = wt[pl.ds(where * 9, 9)]
        picked = taps[:, :, 0:own_out]
        for i in range(1, nc):
            picked = jnp.where(owner == i, taps[:, :, i * own_out : (i + 1) * own_out], picked)
        return picked

    def columns_for(ref, k):
        if own_out % 128 == 0:
            return ref[:, wanted(k)]
        owner = lax.rem(lax.axis_index("chan") + k, nc)
        cells = ref[...]
        picked = cells[:, 0:own_out]
        for i in range(1, nc):
            picked = jnp.where(owner == i, cells[:, i * own_out : (i + 1) * own_out], picked)
        return picked

    def second_send(edge_ref, mine_ref, b, wt, before, *refs):
        outs, framed = refs[:-1], refs[-1]
        place = lax.axis_index("space")
        inside = jnp.logical_and(place > 0, place < ns - 1)
        total = edge_ref[...].astype(F32) + mine_ref[...].astype(F32) + b[...]
        cells = jnp.where(inside, jnp.maximum(total, 0.0), 0.0)
        lay_columns(cells, framed, h, w)
        for k in range(1, nc):
            taps = taps_for(wt, 2 * odd(), k)
            sums = columns_for(before, k) + nine_taps(framed, taps, h, w)
            outs[k - 1][...] = channels_first(sums, h, w).astype(BF16)

    *sends, framed_edge = run(
        second_send,
        [sds((own_out, h, w), BF16)] * (nc - 1) + [framed_mid],
        (next_edge, to_next_part, b_first, w_second, second),
        flops=18 * hw * ob * own_out * (nc - 1),
    )
    parts = [round_chan(sends[k - 1], k) for k in range(1, nc)]

    def second_keep(framed, wt, before, b, out):
        taps = taps_for(wt, 2 * odd(), 0)
        sums = columns_for(before, 0) + nine_taps(framed, taps, h, w)
        out[...] = channels_first(sums, h, w) + b[...]

    kept = run(
        second_keep,
        sds((own_out, h, w), F32),
        (framed_edge, w_second, second, b_second),
        flops=18 * hw * ob * own_out,
    )

    def finish(kept_ref, *refs):
        total = kept_ref[...]
        for ref in refs[:-1]:
            total += ref[...].astype(F32)
        refs[-1][...] = jnp.maximum(total, 0.0).astype(BF16)

    result = run(finish, sds((own_out, h, w), BF16), (kept, *parts), flops=2 * hw * own_out)
    return result.reshape(own_out, 1, h, w)


def solution(mesh):
    in_specs = (
        P("chan", "space", None, None),
        P(None, None, "chan"),
        P("chan"),
        P("chan", None, None),
        P("chan"),
    )
    return jax.shard_map(
        functools.partial(per_device, mesh.shape["space"], mesh.shape["chan"]),
        mesh=mesh,
        in_specs=in_specs,
        out_specs=P("chan", "space", None, None),
        check_vma=False,
    )
```

time: 114 us -> 41.7 us (0.37); the launches traced: 112 us -> 41.5 us
  local copies, waits for them, and re-layouts: 41.9 us -> 4.7 us
  between operations: 13.6 us -> 0.14 us
  waiting for transfers between devices: 30.1 us -> 17.6 us
  Pallas kernels: 0 us -> 8.88 us
  blocking collectives: 7.94 us -> 0 us
  matrix products: 6.29 us -> 0 us
  starting transfers between devices: 12.2 us -> 10.2 us
    unnamed x15 -> x16, local copies, waits for them, and re-layouts: 40 us -> 4.59 us
    unnamed x2 -> x0, waiting for transfers between devices: 14.8 us -> none
    pallas_call x0 -> x9, Pallas kernels: none -> 8.88 us  [run(): pl.pallas_call(kernel, out_shape=outs, scratch_shapes=scratch, compiler_p...]
    all_gather x1 -> x0, blocking collectives: 7.94 us -> none  [per_device(): gathered = lax.all_gather(volume, 'chan', axis=0, tiled=True)]
    conv_general_dilated x2 -> x0, matrix products: 6.29 us -> none  [apply_taps(): lax.conv_general_dilated(slab[None], kernel, (1, 1, 1), [(0, 0), (row_pad...]
    ppermute x4 -> x6, waiting for transfers between devices: 15.3 us -> 17.6 us  [the longest x2 12.3 us: per_device(): next_chip = lambda x: lax.ppermute(x, 'space', beside)]
    ppermute x4 -> x6, starting transfers between devices: 12.2 us -> 10.2 us  [the longest x2 6.05 us: per_device(): next_chip = lambda x: lax.ppermute(x, 'space', beside)]
  transfers between devices with their start and end apart: 5 -> 6, of which waited for: 3 -> 4; matrix products, arithmetic and copies ran while one was open for 0% -> 0% of each run, Pallas kernels for 0% -> 13%
where the time goes in v1:
time: 41.7 us; the launch traced here: 41.5 us
  waiting for transfers between devices  17.6 us (42%)
  starting transfers between devices  10.2 us (24%)
  Pallas kernels  8.88 us (21%)
  local copies, waits for them, and re-layouts  4.7 us (11%)
    ppermute x2, waiting for transfers between devices, per_device(): next_chip = lambda x: lax.ppermute(x, 'space', beside)  12.3 us
    pallas_call x9, Pallas kernels, run(): pl.pallas_call(kernel, out_shape=outs, scratch_shapes=scratch, compiler_p...  8.88 us
    ppermute x2, starting transfers between devices, per_device(): next_chip = lambda x: lax.ppermute(x, 'space', beside)  6.05 us
    ppermute x2, waiting for transfers between devices, per_device(): lax.ppermute(x, 'chan', [(i, (i + k) % nc) for i in range(nc)])  5.28 us
    unnamed x16, local copies, waits for them, and re-layouts  4.59 us
    ppermute x2, starting transfers between devices, per_device(): lax.ppermute(x, 'chan', [(i, (i + k) % nc) for i in range(nc)])  2.47 us
    ppermute x2, starting transfers between devices, per_device(): in_chip = lambda x: lax.ppermute(x, 'space', pairs)  1.68 us
  transfers between devices with their start and end apart: 6, of which 4 were waited for; matrix products, arithmetic and copies ran while one was open for 0% of the time, Pallas kernels for 13%

profile of v1, /device:TPU:9, one launch (start us, length us, event | category | flops | bytes accessed | tf_op | source)
XLA Modules:
  0.0 41.5 jit_solution(9029796178877523727)
XLA Ops:
  0.0 1.2 %collective-permute-start = (bf16[128,8,128]{2,1,0:T(8,128)(2,1)}, bf16[128,8,128]{2,1,0:T(8,128)(2,1)S(1)}, u32[]{:S(2)}, u32[]{:S(2)}) collective-permute-start(bf16[128,8,128]{2,1,0:T(8,128)(2,1)} %bitcast.17), channel_id=1, source_target_pairs={{0,1},{1,0},{2,3},{3,2},{4,5},{5,4},{6,7},{7,6},{8,9},{9,8},{10,11... | collective-permute-start | bytes 786440 | tf_op jit(solution)/shard_map/ppermute | solution.py:97
  1.2 0.0 copy-start.1
  1.2 1.5 %copy-done.1 = bf16[256,27,128]{2,0,1:T(8,128)(2,1)S(1)} copy-done((bf16[256,27,128]{2,0,1:T(8,128)(2,1)S(1)}, bf16[256,27,128]{2,0,1:T(8,128)(2,1)}, u32[]{:S(2)}) %copy-start.1) | copy-done | bytes 1769496
  2.7 0.0 copy-start.6
  2.7 0.9 %copy-done.6 = bf16[128,1,8,128]{3,2,1,0:T(8,128)(2,1)S(1)} copy-done((bf16[128,1,8,128]{3,2,1,0:T(8,128)(2,1)S(1)}, bf16[128,1,8,128]{3,2,1,0:T(8,128)(2,1)}, u32[]{:S(2)}) %copy-start.6) | copy-done | bytes 262168
  3.7 0.0 copy-start.2
  3.7 2.1 %shard_map.55 = (f32[1024,128]{1,0:T(8,128)S(1)}, f32[1024,128]{1,0:T(8,128)S(1)}, f32[1024,128]{1,0:T(8,128)S(1)}) custom-call(bf16[128,8,128]{2,1,0:T(8,128)(2,1)S(1)} %bitcast.18, bf16[27,256,128]{2,1,0:T(8,128)(2,1)S(1)} %bitcast.12), custom_call_target="tpu_custom_call" | custom-call | flops 905969664 | bytes 2031616 | tf_op jit(solution)/shard_map/pallas_call | solution.py:21
  5.8 1.6 %collective-permute-done.refs_0_ = bf16[128,8,128]{2,1,0:T(8,128)(2,1)S(1)} collective-permute-done((bf16[128,8,128]{2,1,0:T(8,128)(2,1)}, bf16[128,8,128]{2,1,0:T(8,128)(2,1)S(1)}, u32[]{:S(2)}, u32[]{:S(2)}) %collective-permute-start) | collective-permute-done | bytes 262176 | tf_op jit(solution)/shard_map/ppermute | solution.py:97
  7.4 0.0 copy-done.2
  7.4 1.5 %shard_map.56 = (bf16[1024,128]{1,0:T(8,128)(2,1)S(1)}, bf16[1024,128]{1,0:T(8,128)(2,1)S(1)}, bf16[1280,384]{1,0:T(8,128)(2,1)S(1)}) custom-call(bf16[128,8,128]{2,1,0:T(8,128)(2,1)S(1)} %collective-permute-done.refs_0_, bf16[27,256,128]{2,1,0:T(8,128)(2,1)S(1)} %bitcast.13, f32[1024,128]{1,0:T(8,128)S(1)} %get-tuple-element.15.refs_2_, ...), custom_call_target="tpu_custom_call" | custom-call | flops 603979776 | bytes 3080192 | tf_op jit(solution)/shard_map/pallas_call | solution.py:21
  8.9 1.6 %collective-permute-start.1 = (bf16[1024,128]{1,0:T(8,128)(2,1)S(1)}, bf16[1024,128]{1,0:T(8,128)(2,1)S(1)}, u32[]{:S(2)}, u32[]{:S(2)}) collective-permute-start(bf16[1024,128]{1,0:T(8,128)(2,1)S(1)} %get-tuple-element.19), channel_id=1, source_target_pairs={{0,2},{2,0},{4,6},{6,4},{8,10},{10,8},{12,14},{14,12},{16,18},{18,... | collective-permute-start | bytes 786440 | tf_op jit(solution)/shard_map/ppermute | solution.py:95
  10.5 3.0 %collective-permute-start.3 = (bf16[1024,128]{1,0:T(8,128)(2,1)S(1)}, bf16[1024,128]{1,0:T(8,128)(2,1)S(1)}, u32[]{:S(2)}, u32[]{:S(2)}) collective-permute-start(bf16[1024,128]{1,0:T(8,128)(2,1)S(1)} %get-tuple-element.21.mine_ref), channel_id=1, source_target_pairs={{2,4},{6,8},{10,12},{14,16},{18,20},{22,24},{26,28},{4,2},{8,6},{1... | collective-permute-start | bytes 786440 | tf_op jit(solution)/shard_map/ppermute | solution.py:96
  13.5 0.0 collective-permute-done.1.refs_3_
  13.6 0.0 copy-start.5
  13.6 0.0 copy-start
  13.6 0.8 %shard_map.57 = (f32[1024,128]{1,0:T(8,128)S(1)}, bf16[1024,128]{1,0:T(8,128)(2,1)S(1)}) custom-call(bf16[1280,384]{1,0:T(8,128)(2,1)S(1)} %get-tuple-element.17.refs_0_, bf16[27,256,128]{2,1,0:T(8,128)(2,1)S(1)} %bitcast.14, f32[1024,128]{1,0:T(8,128)S(1)} %get-tuple-element.18.refs_2_, bf16[1024,128]{1,0:T(8,128)(2,1)S(1)} %collective-permute-done.1.refs_3_), custom_call_target="tpu_custom_call" | custom-call | flops 301989888 | bytes 3538944 | tf_op jit(solution)/shard_map/pallas_call | solution.py:21
  14.4 6.6 %collective-permute-done.3.side_ref = bf16[1024,128]{1,0:T(8,128)(2,1)S(1)} collective-permute-done((bf16[1024,128]{1,0:T(8,128)(2,1)S(1)}, bf16[1024,128]{1,0:T(8,128)(2,1)S(1)}, u32[]{:S(2)}, u32[]{:S(2)}) %collective-permute-start.3) | collective-permute-done | bytes 262176 | tf_op jit(solution)/shard_map/ppermute | solution.py:96
  21.0 0.0 copy-done.5
  21.0 0.1 shard_map.58.cells
  21.1 0.1 collective-permute-start.4
  21.2 3.0 %collective-permute-start.2 = (bf16[1024,128]{1,0:T(8,128)(2,1)S(1)}, bf16[1024,128]{1,0:T(8,128)(2,1)S(1)}, u32[]{:S(2)}, u32[]{:S(2)}) collective-permute-start(bf16[1024,128]{1,0:T(8,128)(2,1)S(1)} %get-tuple-element.20), channel_id=1, source_target_pairs={{2,4},{6,8},{10,12},{14,16},{18,20},{22,24},{26,28},{4,2},{8,6},{1... | collective-permute-start | bytes 786440 | tf_op jit(solution)/shard_map/ppermute | solution.py:96
  24.2 0.0 copy-done
  24.2 0.9 %shard_map.59.before = f32[1024,256]{1,0:T(8,128)S(1)} custom-call(bf16[1024,128]{1,0:T(8,128)(2,1)S(1)} %shard_map.58.cells, bf16[27,128,256]{2,1,0:T(8,128)(2,1)S(1)} %bitcast.8), custom_call_target="tpu_custom_call" | custom-call | flops 603979776 | bytes 2031616 | tf_op jit(solution)/shard_map/pallas_call | solution.py:21
  25.1 0.0 collective-permute-done.4.cells
  25.1 0.9 %shard_map.60.before = f32[1024,256]{1,0:T(8,128)S(1)} custom-call(bf16[1024,128]{1,0:T(8,128)(2,1)S(1)} %collective-permute-done.4.cells, bf16[27,128,256]{2,1,0:T(8,128)(2,1)S(1)} %bitcast.9, f32[1024,256]{1,0:T(8,128)S(1)} %shard_map.59.before), custom_call_target="tpu_custom_call" | custom-call | flops 603979776 | bytes 3080192 | tf_op jit(solution)/shard_map/pallas_call | solution.py:21
  26.0 0.0 copy-start.7
  26.0 5.7 %collective-permute-done.2.edge_ref = bf16[1024,128]{1,0:T(8,128)(2,1)S(1)} collective-permute-done((bf16[1024,128]{1,0:T(8,128)(2,1)S(1)}, bf16[1024,128]{1,0:T(8,128)(2,1)S(1)}, u32[]{:S(2)}, u32[]{:S(2)}) %collective-permute-start.2) | collective-permute-done | bytes 262176 | tf_op jit(solution)/shard_map/ppermute | solution.py:96
  31.7 0.9 %shard_map.61 = (bf16[128,8,128]{2,1,0:T(8,128)(2,1)S(1)}, bf16[1280,384]{1,0:T(8,128)(2,1)S(1)}) custom-call(bf16[1024,128]{1,0:T(8,128)(2,1)S(1)} %collective-permute-done.2.edge_ref, bf16[1024,128]{1,0:T(8,128)(2,1)S(1)} %get-tuple-element.21.mine_ref, f32[1,128]{1,0:T(1,128)S(1)} %bitcast.16, bf16[27,128,256]{2,1,0:T(8,128)(2,1)S(1)} %bitcast.10, ...), custom_call_target="tpu_custom_call" | custom-call | flops 301989888 | bytes 3342848 | tf_op jit(solution)/shard_map/pallas_call | solution.py:21
  32.6 0.0 copy-start.3
  32.6 0.9 %copy-done.3 = bf16[1280,384]{1,0:T(8,128)(2,1)} copy-done((bf16[1280,384]{1,0:T(8,128)(2,1)}, bf16[1280,384]{1,0:T(8,128)(2,1)S(1)}, u32[]{:S(2)}) %copy-start.3) | copy-done | bytes 983064
  33.6 1.2 %collective-permute-start.5 = (bf16[128,8,128]{2,1,0:T(8,128)(2,1)S(1)}, bf16[128,8,128]{2,1,0:T(8,128)(2,1)S(1)}, u32[]{:S(2)}, u32[]{:S(2)}) collective-permute-start(bf16[128,8,128]{2,1,0:T(8,128)(2,1)S(1)} %get-tuple-element.24), channel_id=1, source_target_pairs={{0,1},{1,0},{2,3},{3,2},{4,5},{5,4},{6,7},{7,6},{8,9},{9,8},{10,11... | collective-permute-start | bytes 786440 | tf_op jit(solution)/shard_map/ppermute | solution.py:97
  34.8 0.0 copy-done.7
  34.8 0.1 copy.6.b
  34.9 0.0 copy-start.4
  34.9 1.2 %copy-done.4 = bf16[1280,384]{1,0:T(8,128)(2,1)S(1)} copy-done((bf16[1280,384]{1,0:T(8,128)(2,1)S(1)}, bf16[1280,384]{1,0:T(8,128)(2,1)}, u32[]{:S(2)}) %copy-start.4) | copy-done | bytes 983064
  36.1 0.9 %shard_map.62.kept_ref = f32[128,8,128]{2,1,0:T(8,128)S(1)} custom-call(bf16[1280,384]{1,0:T(8,128)(2,1)S(1)} %copy-done.4, bf16[27,128,256]{2,1,0:T(8,128)(2,1)S(1)} %bitcast.11, f32[1024,256]{1,0:T(8,128)S(1)} %shard_map.60.before, f32[128,1,1]{2,1,0:T(1,128)S(1)} %copy.6.b), custom_call_target="tpu_custom_call" | custom-call | flops 301989888 | bytes 3801600 | tf_op jit(solution)/shard_map/pallas_call | solution.py:21
  37.1 3.7 %collective-permute-done.5.refs_0_ = bf16[128,8,128]{2,1,0:T(8,128)(2,1)S(1)} collective-permute-done((bf16[128,8,128]{2,1,0:T(8,128)(2,1)S(1)}, bf16[128,8,128]{2,1,0:T(8,128)(2,1)S(1)}, u32[]{:S(2)}, u32[]{:S(2)}) %collective-permute-start.5) | collective-permute-done | bytes 262176 | tf_op jit(solution)/shard_map/ppermute | solution.py:97
  40.8 0.8 %shard_map.63 = bf16[128,8,128]{2,1,0:T(8,128)(2,1)} custom-call(f32[128,8,128]{2,1,0:T(8,128)S(1)} %shard_map.62.kept_ref, bf16[128,8,128]{2,1,0:T(8,128)(2,1)S(1)} %collective-permute-done.5.refs_0_), custom_call_target="tpu_custom_call" | custom-call | flops 262144 | bytes 786432 | tf_op jit(solution)/shard_map/pallas_call | solution.py:21
Async XLA Ops:
  0.0 7.4 %collective-permute-start = (bf16[128,8,128]{2,1,0:T(8,128)(2,1)}, bf16[128,8,128]{2,1,0:T(8,128)(2,1)S(1)}, u32[]{:S(2)}, u32[]{:S(2)}) collective-permute-start(bf16[128,8,128]{2,1,0:T(8,128)(2,1)} %bitcast.17), channel_id=1, source_target_pairs={{0,1},{1,0},{2,3},{3,2},{4,5},{5,4},{6,7},{7,6},{8,9},{9,8},{10,11... | collective-permute-start | bytes 786440 | tf_op jit(solution)/shard_map/ppermute | solution.py:97
  1.2 1.5 %copy-start.1 = (bf16[256,27,128]{2,0,1:T(8,128)(2,1)S(1)}, bf16[256,27,128]{2,0,1:T(8,128)(2,1)}, u32[]{:S(2)}) copy-start(bf16[256,27,128]{2,0,1:T(8,128)(2,1)} %param.6) | copy-start | bytes 5308420
  2.7 0.9 %copy-start.6 = (bf16[128,1,8,128]{3,2,1,0:T(8,128)(2,1)S(1)}, bf16[128,1,8,128]{3,2,1,0:T(8,128)(2,1)}, u32[]{:S(2)}) copy-start(bf16[128,1,8,128]{3,2,1,0:T(8,128)(2,1)} %param.5) | copy-start | bytes 786436
  3.7 3.7 %copy-start.2 = (bf16[256,27,128]{2,0,1:T(8,128)(2,1)S(1)}, bf16[256,27,128]{2,0,1:T(8,128)(2,1)}, u32[]{:S(2)}) copy-start(bf16[256,27,128]{2,0,1:T(8,128)(2,1)} %param.6) | copy-start | bytes 5308420
  8.9 4.6 %collective-permute-start.1 = (bf16[1024,128]{1,0:T(8,128)(2,1)S(1)}, bf16[1024,128]{1,0:T(8,128)(2,1)S(1)}, u32[]{:S(2)}, u32[]{:S(2)}) collective-permute-start(bf16[1024,128]{1,0:T(8,128)(2,1)S(1)} %get-tuple-element.19), channel_id=1, source_target_pairs={{0,2},{2,0},{4,6},{6,4},{8,10},{10,8},{12,14},{14,12},{16,18},{18,... | collective-permute-start | bytes 786440 | tf_op jit(solution)/shard_map/ppermute | solution.py:95
  10.5 10.5 %collective-permute-start.3 = (bf16[1024,128]{1,0:T(8,128)(2,1)S(1)}, bf16[1024,128]{1,0:T(8,128)(2,1)S(1)}, u32[]{:S(2)}, u32[]{:S(2)}) collective-permute-start(bf16[1024,128]{1,0:T(8,128)(2,1)S(1)} %get-tuple-element.21.mine_ref), channel_id=1, source_target_pairs={{2,4},{6,8},{10,12},{14,16},{18,20},{22,24},{26,28},{4,2},{8,6},{1... | collective-permute-start | bytes 786440 | tf_op jit(solution)/shard_map/ppermute | solution.py:96
  13.6 7.5 %copy-start.5 = (f32[128]{0:T(128)S(1)}, f32[128]{0:T(128)}, u32[]{:S(2)}) copy-start(f32[128]{0:T(128)} %param.7) | copy-start | bytes 1540
  13.6 10.6 %copy-start = (bf16[128,27,256]{2,0,1:T(8,128)(2,1)S(1)}, bf16[128,27,256]{2,0,1:T(8,128)(2,1)}, u32[]{:S(2)}) copy-start(bf16[128,27,256]{2,0,1:T(8,128)(2,1)} %param.8) | copy-start | bytes 5308420
  21.1 4.0 %collective-permute-start.4 = (bf16[1024,128]{1,0:T(8,128)(2,1)S(1)}, bf16[1024,128]{1,0:T(8,128)(2,1)S(1)}, u32[]{:S(2)}, u32[]{:S(2)}) collective-permute-start(bf16[1024,128]{1,0:T(8,128)(2,1)S(1)} %shard_map.58.cells), channel_id=1, source_target_pairs={{0,2},{2,0},{4,6},{6,4},{8,10},{10,8},{12,14},{14,12},{16,18},{18,... | collective-permute-start | bytes 786440 | tf_op jit(solution)/shard_map/ppermute | solution.py:95
  21.2 10.5 %collective-permute-start.2 = (bf16[1024,128]{1,0:T(8,128)(2,1)S(1)}, bf16[1024,128]{1,0:T(8,128)(2,1)S(1)}, u32[]{:S(2)}, u32[]{:S(2)}) collective-permute-start(bf16[1024,128]{1,0:T(8,128)(2,1)S(1)} %get-tuple-element.20), channel_id=1, source_target_pairs={{2,4},{6,8},{10,12},{14,16},{18,20},{22,24},{26,28},{4,2},{8,6},{1... | collective-permute-start | bytes 786440 | tf_op jit(solution)/shard_map/ppermute | solution.py:96
  26.0 8.8 %copy-start.7 = (f32[128]{0:T(128)S(1)}, f32[128]{0:T(128)}, u32[]{:S(2)}) copy-start(f32[128]{0:T(128)} %param.9) | copy-start | bytes 1540
  32.6 1.0 %copy-start.3 = (bf16[1280,384]{1,0:T(8,128)(2,1)}, bf16[1280,384]{1,0:T(8,128)(2,1)S(1)}, u32[]{:S(2)}) copy-start(bf16[1280,384]{1,0:T(8,128)(2,1)S(1)} %get-tuple-element.23.framed) | copy-start | bytes 2949124
  33.6 7.2 %collective-permute-start.5 = (bf16[128,8,128]{2,1,0:T(8,128)(2,1)S(1)}, bf16[128,8,128]{2,1,0:T(8,128)(2,1)S(1)}, u32[]{:S(2)}, u32[]{:S(2)}) collective-permute-start(bf16[128,8,128]{2,1,0:T(8,128)(2,1)S(1)} %get-tuple-element.24), channel_id=1, source_target_pairs={{0,1},{1,0},{2,3},{3,2},{4,5},{5,4},{6,7},{7,6},{8,9},{9,8},{10,11... | collective-permute-start | bytes 786440 | tf_op jit(solution)/shard_map/ppermute | solution.py:97
  34.9 1.2 %copy-start.4 = (bf16[1280,384]{1,0:T(8,128)(2,1)S(1)}, bf16[1280,384]{1,0:T(8,128)(2,1)}, u32[]{:S(2)}) copy-start(bf16[1280,384]{1,0:T(8,128)(2,1)} %copy-done.3) | copy-start | bytes 2949124

commit v2 on v1

--- a/solution.py
+++ b/solution.py
@@ -17,7 +17,7 @@
 
 
 def run(kernel, outs, args, scratch=(), flops=0):
-    moved = sum(a.size * a.dtype.itemsize for a in args)
+    moved = sum(a.size * a.dtype.itemsize for a in args) if flops else 0
     return pl.pallas_call(
         kernel,
         out_shape=outs,
@@ -81,13 +81,12 @@
     ob = w_first.shape[2]
     full = w_second.shape[2]
     own_out = full // nc
-    framed_in = sds(((h + 2) * w, 3 * cb), BF16)
     framed_mid = sds(((h + 2) * w, 3 * ob), BF16)
     volume = volume.reshape(cb, h, w)
     w_first = jnp.transpose(w_first, (1, 0, 2))
     w_second = jnp.transpose(w_second, (1, 0, 2))
     b_first = b_first.reshape(1, ob)
-    b_second = b_second.reshape(own_out, 1, 1)
+    b_second = b_second.reshape(1, own_out)
 
     pairs = [(i, i ^ 1) for i in range(ns)]
     beside = [(i, i + 1) for i in range(1, ns - 1, 2)]
@@ -97,6 +96,11 @@
     round_chan = lambda x, k: lax.ppermute(
         x, "chan", [(i, (i + k) % nc) for i in range(nc)]
     )
+    across = lambda x, k: lax.ppermute(
+        x,
+        ("space", "chan"),
+        [(i * nc + c, j * nc + (c + k) % nc) for i, j in beside for c in range(nc)],
+    )
 
     def odd():
         return lax.rem(lax.axis_index("space"), 2)
@@ -105,87 +109,111 @@
         owner = lax.rem(lax.axis_index("chan") + nc - k, nc)
         return pl.ds(pl.multiple_of(owner * size, size), size)
 
-    to_pair = lambda: 2 * odd()
+    from_pair = lambda: 2 - 2 * odd()
+    from_next = lambda: 2 * odd()
     to_next = lambda: 2 - 2 * odd()
-
-    def first_own(vol, wt, next_ref, pair_ref, mid_ref, framed):
-        lay_columns(rows_last(vol[...]), framed, h, w)
-        block = chan_rows(0, cb)
-        next_ref[...] = nine_taps(framed, depth_taps(to_next(), wt, block), h, w)
-        pair_ref[...] = nine_taps(framed, depth_taps(to_pair(), wt, block), h, w)
-        mid_ref[...] = nine_taps(framed, depth_taps(1, wt, block), h, w)
 
     part = sds((hw, ob), F32)
     half = sds((hw, ob), BF16)
-    arrived = [round_chan(volume, k) for k in range(1, nc)]
-    own_next, own_pair, own_mid = run(
+    scratch_in = [pltpu.VMEM(((h + 2) * w, 3 * cb), BF16)]
+    others = list(range(1, nc))
+
+    arrived = [round_chan(volume, k) for k in others]
+    partner = in_chip(volume)
+    beyond = next_chip(volume)
+    beyond_rest = [across(volume, k) for k in others]
+    pieces = 2
+
+    def spread(framed, vol, wt, offsets, k):
+        lay_columns(rows_last(vol), framed, h, w)
+        taps = [depth_taps(offset(), wt, chan_rows(k, cb)) for offset in offsets]
+        if ob % 128 == 0:
+            return nine_taps(framed, jnp.concatenate(taps, axis=2), h, w)
+        return jnp.concatenate([nine_taps(framed, t, h, w) for t in taps], axis=1)
+
+    def first_own(vol_hbm, wt_hbm, both_ref, wt, framed, vol, sems):
+        get_vol = pltpu.make_async_copy(vol_hbm, vol, sems.at[0])
+        get_wt = pltpu.make_async_copy(wt_hbm, wt, sems.at[1])
+        get_vol.start()
+        get_wt.start()
+        get_vol.wait()
+        get_wt.wait()
+        both_ref[...] = spread(framed, vol[...], wt, (lambda: 1, to_next), 0)
+
+    hbm = pl.BlockSpec(memory_space=pltpu.HBM)
+    vmem = pl.BlockSpec(memory_space=pltpu.VMEM)
+    both, taps_first = pl.pallas_call(
         first_own,
-        [part, part, part],
-        (volume, w_first),
-        [pltpu.VMEM(framed_in.shape, BF16)],
-        flops=54 * hw * cb * ob,
-    )
-
-    def first_sides(*refs):
-        vols, (wt, next_ref, pair_ref) = refs[: nc - 1], refs[nc - 1 : nc + 2]
-        to_next_ref, to_pair_ref = refs[nc + 2 : nc + 4]
-        frames = refs[nc + 4 :]
-        onward, across = next_ref[...], pair_ref[...]
-        for k in range(1, nc):
-            lay_columns(rows_last(vols[k - 1][...]), frames[k - 1], h, w)
-            block = chan_rows(k, cb)
-            onward += nine_taps(frames[k - 1], depth_taps(to_next(), wt, block), h, w)
-            across += nine_taps(frames[k - 1], depth_taps(to_pair(), wt, block), h, w)
-        to_next_ref[...] = onward.astype(BF16)
-        to_pair_ref[...] = across.astype(BF16)
-
-    to_next_part, to_pair_part, *frames = run(
-        first_sides,
-        [half, half] + [framed_in] * (nc - 1),
-        (*arrived, w_first, own_next, own_pair),
-        flops=36 * hw * cb * ob * (nc - 1),
-    )
-    pair_part = in_chip(to_pair_part)
-    next_part = next_chip(to_next_part)
-
-    def first_mid(*refs):
-        blocks, (wt, mid_ref, pair_ref, sum_ref, edge_ref) = refs[: nc - 1], refs[nc - 1 :]
-        total = mid_ref[...] + pair_ref[...].astype(F32)
-        for k in range(1, nc):
-            taps = depth_taps(1, wt, chan_rows(k, cb))
-            total += nine_taps(blocks[k - 1], taps, h, w)
+        out_shape=[sds((hw, 2 * ob), F32), sds(w_first.shape, BF16)],
+        in_specs=[hbm, hbm],
+        out_specs=[vmem, vmem],
+        scratch_shapes=[
+            *scratch_in,
+            pltpu.VMEM(volume.shape, BF16),
+            pltpu.SemaphoreType.DMA((2,)),
+        ],
+        compiler_params=pltpu.CompilerParams(vmem_limit_bytes=VMEM_LIMIT),
+        cost_estimate=pl.CostEstimate(
+            flops=36 * hw * cb * ob, bytes_accessed=2 * w_first.size, transcendentals=0
+        ),
+    )(volume, w_first)
+
+    def first_rest(*refs):
+        vols, (wt, both_ref, mid_ref, onward_ref, framed) = refs[: nc - 1], refs[nc - 1 :]
+        total = both_ref[...]
+        for vol, k in zip(vols, others):
+            total += spread(framed, vol[...], wt, (lambda: 1, to_next), k)
+        mid_ref[...] = total[:, :ob]
+        onward_ref[...] = total[:, ob:]
+
+    both, arrived = lax.optimization_barrier((both, arrived))
+    partner_rest = [in_chip(q) for x in arrived for q in jnp.split(x, pieces)]
+    mid, onward = run(first_rest, [part, part], (*arrived, taps_first, both), scratch_in, 36 * hw * cb * ob)
+
+    def first_pair(*refs):
+        whole_ref, refs = refs[0], refs[1:]
+        count = (nc - 1) * pieces
+        parts_in, (wt, mid_ref, sum_ref, edge_ref, framed) = refs[:count], refs[count:]
+        total = mid_ref[...] + spread(framed, whole_ref[...], wt, (from_pair,), 0)
+        for k in others:
+            vol = jnp.concatenate([r[...] for r in parts_in[(k - 1) * pieces : k * pieces]])
+            total += spread(framed, vol, wt, (from_pair,), k)
         sum_ref[...] = total
         edge_ref[...] = total.astype(BF16)
 
     so_far, edge_sum = run(
-        first_mid,
-        [part, half],
-        (*frames, w_first, own_mid, pair_part),
-        flops=18 * hw * cb * ob * (nc - 1),
+        first_pair, [part, half], (partner, *partner_rest, taps_first, mid), scratch_in, 36 * hw * cb * ob
     )
     next_edge = next_chip(edge_sum)
 
-    def hidden_own(sum_ref, side_ref, b, out):
-        total = sum_ref[...] + side_ref[...].astype(F32) + b[...]
-        out[...] = jnp.maximum(total, 0.0).astype(BF16)
-
-    hidden = run(hidden_own, half, (so_far, next_part, b_first), flops=3 * hw * ob)
-    pair_hidden = in_chip(hidden)
+    def first_next(vol, wt, sum_ref, out, framed):
+        out[...] = sum_ref[...] + spread(framed, vol[...], wt, (from_next,), 0)
+
+    side = run(first_next, part, (beyond, taps_first, so_far), scratch_in, 18 * hw * cb * ob)
+
+    def hidden_own(*refs):
+        vols, (wt, side_ref, b, out, framed) = refs[: nc - 1], refs[nc - 1 :]
+        total = side_ref[...]
+        for vol, k in zip(vols, others):
+            total += spread(framed, vol[...], wt, (from_next,), k)
+        out[...] = jnp.maximum(total + b[...], 0.0).astype(BF16)
+
+    hidden = run(hidden_own, half, (*beyond_rest, taps_first, side, b_first), scratch_in, 18 * hw * cb * ob)
+    pair_hidden = [in_chip(hidden[: hw // 2]), in_chip(hidden[hw // 2 :])]
 
     def second_own(cells, wt, out, framed):
         lay_columns(cells[...].astype(F32), framed, h, w)
         out[...] = nine_taps(framed, depth_taps(1, wt), h, w)
 
-    def second_pair(cells, wt, before, out, framed):
-        lay_columns(cells[...].astype(F32), framed, h, w)
+    def second_pair(top, bottom, wt, before, out, framed):
+        cells = jnp.concatenate([top[...], bottom[...]], axis=0)
+        lay_columns(cells.astype(F32), framed, h, w)
         out[...] = before[...] + nine_taps(framed, depth_taps(2 - 2 * odd(), wt), h, w)
 
     scratch_mid = [pltpu.VMEM(framed_mid.shape, BF16)]
     whole = sds((hw, full), F32)
-    second = run(second_own, whole, (hidden, w_second), scratch_mid, 18 * hw * ob * full)
-    second = run(
-        second_pair, whole, (pair_hidden, w_second, second), scratch_mid, 18 * hw * ob * full
-    )
+    second = run(second_own, whole, (hidden, w_second), scratch_mid)
+    second = run(second_pair, whole, (*pair_hidden, w_second, second), scratch_mid)
 
     def wanted(k):
         owner = lax.rem(lax.axis_index("chan") + k, nc)
@@ -211,35 +239,41 @@
             picked = jnp.where(owner == i, cells[:, i * own_out : (i + 1) * own_out], picked)
         return picked
 
+    def lay_edge(edge_ref, mine_ref, b, framed):
+        place = lax.axis_index("space")
+        inside = jnp.logical_and(place > 0, place < ns - 1)
+        total = edge_ref[...].astype(F32) + mine_ref[...] + b[...]
+        cells = jnp.where(inside, jnp.maximum(total, 0.0), 0.0)
+        lay_columns(cells.astype(BF16).astype(F32), framed, h, w)
+
     def second_send(edge_ref, mine_ref, b, wt, before, *refs):
         outs, framed = refs[:-1], refs[-1]
-        place = lax.axis_index("space")
-        inside = jnp.logical_and(place > 0, place < ns - 1)
-        total = edge_ref[...].astype(F32) + mine_ref[...].astype(F32) + b[...]
-        cells = jnp.where(inside, jnp.maximum(total, 0.0), 0.0)
-        lay_columns(cells, framed, h, w)
+        lay_edge(edge_ref, mine_ref, b, framed)
         for k in range(1, nc):
             taps = taps_for(wt, 2 * odd(), k)
             sums = columns_for(before, k) + nine_taps(framed, taps, h, w)
             outs[k - 1][...] = channels_first(sums, h, w).astype(BF16)
 
-    *sends, framed_edge = run(
+    sends = run(
         second_send,
-        [sds((own_out, h, w), BF16)] * (nc - 1) + [framed_mid],
-        (next_edge, to_next_part, b_first, w_second, second),
+        [sds((own_out, h, w), BF16)] * (nc - 1),
+        (next_edge, onward, b_first, w_second, second),
+        scratch_mid,
         flops=18 * hw * ob * own_out * (nc - 1),
     )
     parts = [round_chan(sends[k - 1], k) for k in range(1, nc)]
 
-    def second_keep(framed, wt, before, b, out):
+    def second_keep(edge_ref, mine_ref, b_mid, wt, before, b, out, framed):
+        lay_edge(edge_ref, mine_ref, b_mid, framed)
         taps = taps_for(wt, 2 * odd(), 0)
         sums = columns_for(before, 0) + nine_taps(framed, taps, h, w)
-        out[...] = channels_first(sums, h, w) + b[...]
+        out[...] = channels_first(sums + b[...], h, w)
 
     kept = run(
         second_keep,
         sds((own_out, h, w), F32),
-        (framed_edge, w_second, second, b_second),
+        (next_edge, onward, b_first, w_second, second, b_second),
+        scratch_mid,
         flops=18 * hw * ob * own_out,
     )
 

time: 41.7 us -> 35.1 us (0.84)
  waiting for transfers between devices: 17.6 us -> 7.83 us
  starting transfers between devices: 10.2 us -> 14.1 us
  local copies, waits for them, and re-layouts: 4.7 us -> 2.47 us
  Pallas kernels: 8.88 us -> 10.1 us
    ppermute x2, waiting for transfers between devices: 12.3 us -> 2.65 us  [per_device(): next_chip = lambda x: lax.ppermute(x, 'space', beside)]
    ppermute x0 -> x1, starting transfers between devices: none -> 2.5 us  [per_device(): lax.ppermute(x, ('space', 'chan'), [(i * nc + c, j * nc + (c + k) % nc) f...]
    unnamed x16 -> x10, local copies, waits for them, and re-layouts: 4.59 us -> 2.44 us
    pallas_call x0 -> x1, Pallas kernels: none -> 1.41 us  [per_device(): pl.pallas_call(first_own, out_shape=[sds((hw, 2 * ob), F32), sds(w_first....]
    ppermute x2 -> x5, starting transfers between devices: 1.68 us -> 2.57 us  [per_device(): in_chip = lambda x: lax.ppermute(x, 'space', pairs)]
    ppermute x2, waiting for transfers between devices: 5.28 us -> 4.74 us  [per_device(): lax.ppermute(x, 'chan', [(i, (i + k) % nc) for i in range(nc)])]
    ppermute x2, starting transfers between devices: 6.05 us -> 6.51 us  [per_device(): next_chip = lambda x: lax.ppermute(x, 'space', beside)]
    ppermute x2 -> x5, waiting for transfers between devices: 0.01 us -> 0.44 us  [per_device(): in_chip = lambda x: lax.ppermute(x, 'space', pairs)]
  transfers between devices with their start and end apart: 6 -> 10, of which waited for: 4 -> 4; matrix products, arithmetic and copies ran while one was open for 0% -> 0% of each run, Pallas kernels for 13% -> 24%
where the time goes in v2:
time: 35.1 us; the launch traced here: 34.7 us
  starting transfers between devices  14.1 us (40%)
  Pallas kernels  10.1 us (29%)
  waiting for transfers between devices  7.83 us (22%)
  local copies, waits for them, and re-layouts  2.47 us (7%)
    pallas_call x9, Pallas kernels, run(): pl.pallas_call(kernel, out_shape=outs, scratch_shapes=scratch, compiler_p...  8.67 us
    ppermute x2, starting transfers between devices, per_device(): next_chip = lambda x: lax.ppermute(x, 'space', beside)  6.51 us
    ppermute x2, waiting for transfers between devices, per_device(): lax.ppermute(x, 'chan', [(i, (i + k) % nc) for i in range(nc)])  4.74 us
    ppermute x2, waiting for transfers between devices, per_device(): next_chip = lambda x: lax.ppermute(x, 'space', beside)  2.65 us
    ppermute x5, starting transfers between devices, per_device(): in_chip = lambda x: lax.ppermute(x, 'space', pairs)  2.57 us
    ppermute x2, starting transfers between devices, per_device(): lax.ppermute(x, 'chan', [(i, (i + k) % nc) for i in range(nc)])  2.54 us
    ppermute x1, starting transfers between devices, per_device(): lax.ppermute(x, ('space', 'chan'), [(i * nc + c, j * nc + (c + k) % nc) f...  2.5 us
    unnamed x10, local copies, waits for them, and re-layouts  2.44 us
  transfers between devices with their start and end apart: 10, of which 4 were waited for; matrix products, arithmetic and copies ran while one was open for 0% of the time, Pallas kernels for 24%

profile of v2, /device:TPU:9, one launch (start us, length us, event | category | flops | bytes accessed | tf_op | source)
XLA Modules:
  0.0 34.7 jit_solution(1830800584337287059)
XLA Ops:
  0.0 1.2 %collective-permute-start.1 = (bf16[128,8,128]{2,1,0:T(8,128)(2,1)}, bf16[128,8,128]{2,1,0:T(8,128)(2,1)S(1)}, u32[]{:S(2)}, u32[]{:S(2)}) collective-permute-start(bf16[128,8,128]{2,1,0:T(8,128)(2,1)} %bitcast.17), channel_id=1, source_target_pairs={{0,1},{1,0},{2,3},{3,2},{4,5},{5,4},{6,7},{7,6},{8,9},{9,8},{10,11... | collective-permute-start | bytes 786440 | tf_op jit(solution)/shard_map/ppermute | solution.py:96
  1.2 1.0 %collective-permute-start = (bf16[128,8,128]{2,1,0:T(8,128)(2,1)}, bf16[128,8,128]{2,1,0:T(8,128)(2,1)S(1)}, u32[]{:S(2)}, u32[]{:S(2)}) collective-permute-start(bf16[128,8,128]{2,1,0:T(8,128)(2,1)} %bitcast.18), channel_id=1, source_target_pairs={{0,2},{2,0},{4,6},{6,4},{8,10},{10,8},{12,14},{14,12},{16,18},{18,... | collective-permute-start | bytes 786440 | tf_op jit(solution)/shard_map/ppermute | solution.py:94
  2.2 3.0 %collective-permute-start.6 = (bf16[128,8,128]{2,1,0:T(8,128)(2,1)}, bf16[128,8,128]{2,1,0:T(8,128)(2,1)S(1)}, u32[]{:S(2)}, u32[]{:S(2)}) collective-permute-start(bf16[128,8,128]{2,1,0:T(8,128)(2,1)} %bitcast.19), channel_id=1, source_target_pairs={{2,4},{6,8},{10,12},{14,16},{18,20},{22,24},{26,28},{4,2},{8,6},{1... | collective-permute-start | bytes 786440 | tf_op jit(solution)/shard_map/ppermute | solution.py:95
  5.2 2.5 %collective-permute-start.5 = (bf16[128,8,128]{2,1,0:T(8,128)(2,1)}, bf16[128,8,128]{2,1,0:T(8,128)(2,1)S(1)}, u32[]{:S(2)}, u32[]{:S(2)}) collective-permute-start(bf16[128,8,128]{2,1,0:T(8,128)(2,1)} %bitcast.20), channel_id=1, source_target_pairs={{2,5},{3,4},{6,9},{7,8},{10,13},{11,12},{14,17},{15,16},{18,21},{1... | collective-permute-start | bytes 786440 | tf_op jit(solution)/shard_map/ppermute | solution.py:99
  7.7 0.0 copy-start.3
  7.7 1.5 %copy-done.3 = bf16[256,27,128]{2,0,1:T(8,128)(2,1)S(1)} copy-done((bf16[256,27,128]{2,0,1:T(8,128)(2,1)S(1)}, bf16[256,27,128]{2,0,1:T(8,128)(2,1)}, u32[]{:S(2)}) %copy-start.3) | copy-done | bytes 1769496
  9.2 0.0 copy-start.4
  9.2 0.9 %copy-done.4 = bf16[128,1,8,128]{3,2,1,0:T(8,128)(2,1)S(1)} copy-done((bf16[128,1,8,128]{3,2,1,0:T(8,128)(2,1)S(1)}, bf16[128,1,8,128]{3,2,1,0:T(8,128)(2,1)}, u32[]{:S(2)}) %copy-start.4) | copy-done | bytes 262168
  10.1 1.4 %shard_map.55 = (f32[1024,256]{1,0:T(8,128)S(1)}, bf16[27,256,128]{2,1,0:T(8,128)(2,1)S(1)}) custom-call(bf16[128,8,128]{2,1,0:T(8,128)(2,1)S(1)} %bitcast.21, bf16[27,256,128]{2,1,0:T(8,128)(2,1)S(1)} %bitcast.16), custom_call_target="tpu_custom_call" | custom-call | flops 603979776 | bytes 1769472 | tf_op jit(solution)/shard_map/pallas_call | solution.py:145
  11.6 0.0 collective-permute-done.1.refs_0_
  11.6 1.0 %collective-permute-start.2 = (bf16[64,8,128]{2,1,0:T(8,128)(2,1)S(1)}, bf16[64,8,128]{2,1,0:T(8,128)(2,1)S(1)}, u32[]{:S(2)}, u32[]{:S(2)}) collective-permute-start(bf16[64,8,128]{2,1,0:T(8,128)(2,1)S(1)} %get-tuple-element.24), channel_id=1, source_target_pairs={{0,2},{2,0},{4,6},{6,4},{8,10},{10,8},{12,14},{14,12},{16,18},{18,... | collective-permute-start | bytes 393224 | tf_op jit(solution)/shard_map/ppermute | solution.py:94
  12.6 0.1 collective-permute-start.3
  12.6 0.9 %shard_map.56 = (f32[1024,128]{1,0:T(8,128)S(1)}, f32[1024,128]{1,0:T(8,128)S(1)}) custom-call(bf16[128,8,128]{2,1,0:T(8,128)(2,1)S(1)} %collective-permute-done.1.refs_0_, bf16[27,256,128]{2,1,0:T(8,128)(2,1)S(1)} %get-tuple-element.15.refs_1_.refs_3_.wt, f32[1024,256]{1,0:T(8,128)S(1)} %get-tuple-element.16.refs_2_), custom_call_target="tpu_custom_call" | custom-call | flops 603979776 | bytes 3080192 | tf_op jit(solution)/shard_map/pallas_call | solution.py:21
  13.6 0.0 collective-permute-done.refs_0_
  13.6 0.0 collective-permute-done.2.refs_1_
  13.6 0.3 collective-permute-done.3.refs_2_
  13.9 1.6 %shard_map.57 = (f32[1024,128]{1,0:T(8,128)S(1)}, bf16[1024,128]{1,0:T(8,128)(2,1)S(1)}) custom-call(bf16[128,8,128]{2,1,0:T(8,128)(2,1)S(1)} %collective-permute-done.refs_0_, bf16[64,8,128]{2,1,0:T(8,128)(2,1)S(1)} %collective-permute-done.2.refs_1_, bf16[64,8,128]{2,1,0:T(8,128)(2,1)S(1)} %collective-permute-done.3.refs_2_, ...), custom_call_target="tpu_custom_call" | custom-call | flops 603979776 | bytes 2818048 | tf_op jit(solution)/shard_map/pallas_call | solution.py:21
  15.5 0.0 copy-start.1
  15.5 3.5 %collective-permute-start.4 = (bf16[1024,128]{1,0:T(8,128)(2,1)S(1)}, bf16[1024,128]{1,0:T(8,128)(2,1)S(1)}, u32[]{:S(2)}, u32[]{:S(2)}) collective-permute-start(bf16[1024,128]{1,0:T(8,128)(2,1)S(1)} %get-tuple-element.18), channel_id=1, source_target_pairs={{2,4},{6,8},{10,12},{14,16},{18,20},{22,24},{26,28},{4,2},{8,6},{1... | collective-permute-start | bytes 786440 | tf_op jit(solution)/shard_map/ppermute | solution.py:95
  19.1 0.0 collective-permute-done.6.vol
  19.1 0.9 %shard_map.58.refs_2_ = f32[1024,128]{1,0:T(8,128)S(1)} custom-call(bf16[128,8,128]{2,1,0:T(8,128)(2,1)S(1)} %collective-permute-done.6.vol, bf16[27,256,128]{2,1,0:T(8,128)(2,1)S(1)} %get-tuple-element.15.refs_1_.refs_3_.wt, f32[1024,128]{1,0:T(8,128)S(1)} %get-tuple-element.20.sum_ref), custom_call_target="tpu_custom_call" | custom-call | flops 301989888 | bytes 2555904 | tf_op jit(solution)/shard_map/pallas_call | solution.py:21
  19.9 0.0 copy-start
  20.0 0.0 collective-permute-done.5.refs_0_
  20.0 0.0 copy-done.1
  20.0 0.9 %shard_map.59.cells = bf16[1024,128]{1,0:T(8,128)(2,1)S(1)} custom-call(bf16[128,8,128]{2,1,0:T(8,128)(2,1)S(1)} %collective-permute-done.5.refs_0_, bf16[27,256,128]{2,1,0:T(8,128)(2,1)S(1)} %get-tuple-element.15.refs_1_.refs_3_.wt, f32[1024,128]{1,0:T(8,128)S(1)} %shard_map.58.refs_2_, f32[1,128]{1,0:T(1,128)S(1)} %bitcast.12), custom_call_target="tpu_custom_call" | custom-call | flops 301989888 | bytes 2556416 | tf_op jit(solution)/shard_map/pallas_call | solution.py:21
  20.9 0.1 collective-permute-start.7
  21.0 0.4 %collective-permute-start.8 = (bf16[512,128]{1,0:T(8,128)(2,1)S(1)}, bf16[512,128]{1,0:T(8,128)(2,1)S(1)}, u32[]{:S(2)}, u32[]{:S(2)}) collective-permute-start(bf16[512,128]{1,0:T(8,128)(2,1)S(1)} %get-tuple-element.21), channel_id=1, source_target_pairs={{0,2},{2,0},{4,6},{6,4},{8,10},{10,8},{12,14},{14,12},{16,18},{18,... | collective-permute-start | bytes 393224 | tf_op jit(solution)/shard_map/ppermute | solution.py:94
  21.5 0.0 copy-done
  21.5 0.9 %shard_map.60.before = f32[1024,256]{1,0:T(8,128)S(1)} custom-call(bf16[1024,128]{1,0:T(8,128)(2,1)S(1)} %shard_map.59.cells, bf16[27,128,256]{2,1,0:T(8,128)(2,1)S(1)} %bitcast.8), custom_call_target="tpu_custom_call" | custom-call | tf_op jit(solution)/shard_map/pallas_call | solution.py:21
  22.3 0.0 collective-permute-done.7.top
  22.3 0.1 collective-permute-done.8.bottom
  22.5 0.9 %shard_map.61.before = f32[1024,256]{1,0:T(8,128)S(1)} custom-call(bf16[512,128]{1,0:T(8,128)(2,1)S(1)} %collective-permute-done.7.top, bf16[512,128]{1,0:T(8,128)(2,1)S(1)} %collective-permute-done.8.bottom, bf16[27,128,256]{2,1,0:T(8,128)(2,1)S(1)} %bitcast.9, f32[1024,256]{1,0:T(8,128)S(1)} %shard_map.60.before), custom_call_target="tpu_custom_call" | custom-call | tf_op jit(solution)/shard_map/pallas_call | solution.py:21
  23.4 2.6 %collective-permute-done.4.edge_ref = bf16[1024,128]{1,0:T(8,128)(2,1)S(1)} collective-permute-done((bf16[1024,128]{1,0:T(8,128)(2,1)S(1)}, bf16[1024,128]{1,0:T(8,128)(2,1)S(1)}, u32[]{:S(2)}, u32[]{:S(2)}) %collective-permute-start.4) | collective-permute-done | bytes 262176 | tf_op jit(solution)/shard_map/ppermute | solution.py:95
  26.0 0.0 copy-start.2
  26.0 0.9 %shard_map.63 = bf16[128,8,128]{2,1,0:T(8,128)(2,1)S(1)} custom-call(bf16[1024,128]{1,0:T(8,128)(2,1)S(1)} %collective-permute-done.4.edge_ref, f32[1024,128]{1,0:T(8,128)S(1)} %get-tuple-element.19.mine_ref, f32[1,128]{1,0:T(1,128)S(1)} %bitcast.13, bf16[27,128,256]{2,1,0:T(8,128)(2,1)S(1)} %bitcast.10, f32[1024,256]{1,0:T(8,128)S(1)} %shard_map.61.before), custom_call_target="tpu_custom_call" | custom-call | flops 301989888 | bytes 3604992 | tf_op jit(solution)/shard_map/pallas_call | solution.py:21
  27.0 1.3 %collective-permute-start.9 = (bf16[128,8,128]{2,1,0:T(8,128)(2,1)S(1)}, bf16[128,8,128]{2,1,0:T(8,128)(2,1)S(1)}, u32[]{:S(2)}, u32[]{:S(2)}) collective-permute-start(bf16[128,8,128]{2,1,0:T(8,128)(2,1)S(1)} %shard_map.63), channel_id=1, source_target_pairs={{0,1},{1,0},{2,3},{3,2},{4,5},{5,4},{6,7},{7,6},{8,9},{9,8},{10,11... | collective-permute-start | bytes 786440 | tf_op jit(solution)/shard_map/ppermute | solution.py:96
  28.3 0.0 copy-done.2
  28.3 0.9 %shard_map.62.kept_ref = f32[128,8,128]{2,1,0:T(8,128)S(1)} custom-call(bf16[1024,128]{1,0:T(8,128)(2,1)S(1)} %collective-permute-done.4.edge_ref, f32[1024,128]{1,0:T(8,128)S(1)} %get-tuple-element.19.mine_ref, f32[1,128]{1,0:T(1,128)S(1)} %bitcast.14, bf16[27,128,256]{2,1,0:T(8,128)(2,1)S(1)} %bitcast.11, f32[1024,256]{1,0:T(8,128)S(1)} %shard_map.61.before, ...), custom_call_target="tpu_custom_call" | custom-call | flops 301989888 | bytes 3605504 | tf_op jit(solution)/shard_map/pallas_call | solution.py:21
  29.2 4.7 %collective-permute-done.9.refs_0_ = bf16[128,8,128]{2,1,0:T(8,128)(2,1)S(1)} collective-permute-done((bf16[128,8,128]{2,1,0:T(8,128)(2,1)S(1)}, bf16[128,8,128]{2,1,0:T(8,128)(2,1)S(1)}, u32[]{:S(2)}, u32[]{:S(2)}) %collective-permute-start.9) | collective-permute-done | bytes 262176 | tf_op jit(solution)/shard_map/ppermute | solution.py:96
  33.9 0.8 %shard_map.64 = bf16[128,8,128]{2,1,0:T(8,128)(2,1)} custom-call(f32[128,8,128]{2,1,0:T(8,128)S(1)} %shard_map.62.kept_ref, bf16[128,8,128]{2,1,0:T(8,128)(2,1)S(1)} %collective-permute-done.9.refs_0_), custom_call_target="tpu_custom_call" | custom-call | flops 262144 | bytes 786432 | tf_op jit(solution)/shard_map/pallas_call | solution.py:21
  (2 shorter events, 0.0 us)
Async XLA Ops:
  0.0 11.6 %collective-permute-start.1 = (bf16[128,8,128]{2,1,0:T(8,128)(2,1)}, bf16[128,8,128]{2,1,0:T(8,128)(2,1)S(1)}, u32[]{:S(2)}, u32[]{:S(2)}) collective-permute-start(bf16[128,8,128]{2,1,0:T(8,128)(2,1)} %bitcast.17), channel_id=1, source_target_pairs={{0,1},{1,0},{2,3},{3,2},{4,5},{5,4},{6,7},{7,6},{8,9},{9,8},{10,11... | collective-permute-start | bytes 786440 | tf_op jit(solution)/shard_map/ppermute | solution.py:96
  1.2 12.3 %collective-permute-start = (bf16[128,8,128]{2,1,0:T(8,128)(2,1)}, bf16[128,8,128]{2,1,0:T(8,128)(2,1)S(1)}, u32[]{:S(2)}, u32[]{:S(2)}) collective-permute-start(bf16[128,8,128]{2,1,0:T(8,128)(2,1)} %bitcast.18), channel_id=1, source_target_pairs={{0,2},{2,0},{4,6},{6,4},{8,10},{10,8},{12,14},{14,12},{16,18},{18,... | collective-permute-start | bytes 786440 | tf_op jit(solution)/shard_map/ppermute | solution.py:94
  2.2 16.9 %collective-permute-start.6 = (bf16[128,8,128]{2,1,0:T(8,128)(2,1)}, bf16[128,8,128]{2,1,0:T(8,128)(2,1)S(1)}, u32[]{:S(2)}, u32[]{:S(2)}) collective-permute-start(bf16[128,8,128]{2,1,0:T(8,128)(2,1)} %bitcast.19), channel_id=1, source_target_pairs={{2,4},{6,8},{10,12},{14,16},{18,20},{22,24},{26,28},{4,2},{8,6},{1... | collective-permute-start | bytes 786440 | tf_op jit(solution)/shard_map/ppermute | solution.py:95
  5.2 14.8 %collective-permute-start.5 = (bf16[128,8,128]{2,1,0:T(8,128)(2,1)}, bf16[128,8,128]{2,1,0:T(8,128)(2,1)S(1)}, u32[]{:S(2)}, u32[]{:S(2)}) collective-permute-start(bf16[128,8,128]{2,1,0:T(8,128)(2,1)} %bitcast.20), channel_id=1, source_target_pairs={{2,5},{3,4},{6,9},{7,8},{10,13},{11,12},{14,17},{15,16},{18,21},{1... | collective-permute-start | bytes 786440 | tf_op jit(solution)/shard_map/ppermute | solution.py:99
  7.7 1.5 %copy-start.3 = (bf16[256,27,128]{2,0,1:T(8,128)(2,1)S(1)}, bf16[256,27,128]{2,0,1:T(8,128)(2,1)}, u32[]{:S(2)}) copy-start(bf16[256,27,128]{2,0,1:T(8,128)(2,1)} %param.6) | copy-start | bytes 5308420
  9.2 0.9 %copy-start.4 = (bf16[128,1,8,128]{3,2,1,0:T(8,128)(2,1)S(1)}, bf16[128,1,8,128]{3,2,1,0:T(8,128)(2,1)}, u32[]{:S(2)}) copy-start(bf16[128,1,8,128]{3,2,1,0:T(8,128)(2,1)} %param.5) | copy-start | bytes 786436
  11.6 2.0 %collective-permute-start.2 = (bf16[64,8,128]{2,1,0:T(8,128)(2,1)S(1)}, bf16[64,8,128]{2,1,0:T(8,128)(2,1)S(1)}, u32[]{:S(2)}, u32[]{:S(2)}) collective-permute-start(bf16[64,8,128]{2,1,0:T(8,128)(2,1)S(1)} %get-tuple-element.24), channel_id=1, source_target_pairs={{0,2},{2,0},{4,6},{6,4},{8,10},{10,8},{12,14},{14,12},{16,18},{18,... | collective-permute-start | bytes 393224 | tf_op jit(solution)/shard_map/ppermute | solution.py:94
  12.6 1.3 %collective-permute-start.3 = (bf16[64,8,128]{2,1,0:T(8,128)(2,1)S(1)}, bf16[64,8,128]{2,1,0:T(8,128)(2,1)S(1)}, u32[]{:S(2)}, u32[]{:S(2)}) collective-permute-start(bf16[64,8,128]{2,1,0:T(8,128)(2,1)S(1)} %get-tuple-element.23), channel_id=1, source_target_pairs={{0,2},{2,0},{4,6},{6,4},{8,10},{10,8},{12,14},{14,12},{16,18},{18,... | collective-permute-start | bytes 393224 | tf_op jit(solution)/shard_map/ppermute | solution.py:94
  15.5 4.4 %copy-start.1 = (f32[128]{0:T(128)S(1)}, f32[128]{0:T(128)}, u32[]{:S(2)}) copy-start(f32[128]{0:T(128)} %param.7) | copy-start | bytes 1540
  15.5 10.5 %collective-permute-start.4 = (bf16[1024,128]{1,0:T(8,128)(2,1)S(1)}, bf16[1024,128]{1,0:T(8,128)(2,1)S(1)}, u32[]{:S(2)}, u32[]{:S(2)}) collective-permute-start(bf16[1024,128]{1,0:T(8,128)(2,1)S(1)} %get-tuple-element.18), channel_id=1, source_target_pairs={{2,4},{6,8},{10,12},{14,16},{18,20},{22,24},{26,28},{4,2},{8,6},{1... | collective-permute-start | bytes 786440 | tf_op jit(solution)/shard_map/ppermute | solution.py:95
  19.9 1.5 %copy-start = (bf16[128,27,256]{2,0,1:T(8,128)(2,1)S(1)}, bf16[128,27,256]{2,0,1:T(8,128)(2,1)}, u32[]{:S(2)}) copy-start(bf16[128,27,256]{2,0,1:T(8,128)(2,1)} %param.8) | copy-start | bytes 5308420
  20.9 1.5 %collective-permute-start.7 = (bf16[512,128]{1,0:T(8,128)(2,1)S(1)}, bf16[512,128]{1,0:T(8,128)(2,1)S(1)}, u32[]{:S(2)}, u32[]{:S(2)}) collective-permute-start(bf16[512,128]{1,0:T(8,128)(2,1)S(1)} %get-tuple-element.22), channel_id=1, source_target_pairs={{0,2},{2,0},{4,6},{6,4},{8,10},{10,8},{12,14},{14,12},{16,18},{18,... | collective-permute-start | bytes 393224 | tf_op jit(solution)/shard_map/ppermute | solution.py:94
  21.0 1.5 %collective-permute-start.8 = (bf16[512,128]{1,0:T(8,128)(2,1)S(1)}, bf16[512,128]{1,0:T(8,128)(2,1)S(1)}, u32[]{:S(2)}, u32[]{:S(2)}) collective-permute-start(bf16[512,128]{1,0:T(8,128)(2,1)S(1)} %get-tuple-element.21), channel_id=1, source_target_pairs={{0,2},{2,0},{4,6},{6,4},{8,10},{10,8},{12,14},{14,12},{16,18},{18,... | collective-permute-start | bytes 393224 | tf_op jit(solution)/shard_map/ppermute | solution.py:94
  26.0 2.2 %copy-start.2 = (f32[128]{0:T(128)S(1)}, f32[128]{0:T(128)}, u32[]{:S(2)}) copy-start(f32[128]{0:T(128)} %param.9) | copy-start | bytes 1540
  27.0 6.9 %collective-permute-start.9 = (bf16[128,8,128]{2,1,0:T(8,128)(2,1)S(1)}, bf16[128,8,128]{2,1,0:T(8,128)(2,1)S(1)}, u32[]{:S(2)}, u32[]{:S(2)}) collective-permute-start(bf16[128,8,128]{2,1,0:T(8,128)(2,1)S(1)} %shard_map.63), channel_id=1, source_target_pairs={{0,1},{1,0},{2,3},{3,2},{4,5},{5,4},{6,7},{7,6},{8,9},{9,8},{10,11... | collective-permute-start | bytes 786440 | tf_op jit(solution)/shard_map/ppermute | solution.py:96

commit v3 on v2

--- a/solution.py
+++ b/solution.py
@@ -10,6 +10,8 @@
 F32 = jnp.float32
 BF16 = jnp.bfloat16
 VMEM_LIMIT = 20 << 20
+FRAME_COST = 1 << 30
+PAIR_COST = 1 << 28
 
 
 def sds(shape, dtype):
@@ -96,11 +98,6 @@
     round_chan = lambda x, k: lax.ppermute(
         x, "chan", [(i, (i + k) % nc) for i in range(nc)]
     )
-    across = lambda x, k: lax.ppermute(
-        x,
-        ("space", "chan"),
-        [(i * nc + c, j * nc + (c + k) % nc) for i, j in beside for c in range(nc)],
-    )
 
     def odd():
         return lax.rem(lax.axis_index("space"), 2)
@@ -121,60 +118,62 @@
     arrived = [round_chan(volume, k) for k in others]
     partner = in_chip(volume)
     beyond = next_chip(volume)
-    beyond_rest = [across(volume, k) for k in others]
-    pieces = 2
-
-    def spread(framed, vol, wt, offsets, k):
-        lay_columns(rows_last(vol), framed, h, w)
+
+    def frame_own(vol, framed):
+        lay_columns(rows_last(vol[...]), framed, h, w)
+
+    framed_in = sds(((h + 2) * w, 3 * cb), BF16)
+    framed_own = run(frame_own, framed_in, (volume,), (), FRAME_COST)
+    pieces = 1
+
+    def side_by_side(framed, wt, offsets, k):
         taps = [depth_taps(offset(), wt, chan_rows(k, cb)) for offset in offsets]
         if ob % 128 == 0:
             return nine_taps(framed, jnp.concatenate(taps, axis=2), h, w)
         return jnp.concatenate([nine_taps(framed, t, h, w) for t in taps], axis=1)
 
-    def first_own(vol_hbm, wt_hbm, both_ref, wt, framed, vol, sems):
-        get_vol = pltpu.make_async_copy(vol_hbm, vol, sems.at[0])
-        get_wt = pltpu.make_async_copy(wt_hbm, wt, sems.at[1])
-        get_vol.start()
-        get_wt.start()
-        get_vol.wait()
-        get_wt.wait()
-        both_ref[...] = spread(framed, vol[...], wt, (lambda: 1, to_next), 0)
-
-    hbm = pl.BlockSpec(memory_space=pltpu.HBM)
-    vmem = pl.BlockSpec(memory_space=pltpu.VMEM)
-    both, taps_first = pl.pallas_call(
-        first_own,
-        out_shape=[sds((hw, 2 * ob), F32), sds(w_first.shape, BF16)],
-        in_specs=[hbm, hbm],
-        out_specs=[vmem, vmem],
-        scratch_shapes=[
-            *scratch_in,
-            pltpu.VMEM(volume.shape, BF16),
-            pltpu.SemaphoreType.DMA((2,)),
-        ],
-        compiler_params=pltpu.CompilerParams(vmem_limit_bytes=VMEM_LIMIT),
-        cost_estimate=pl.CostEstimate(
-            flops=36 * hw * cb * ob, bytes_accessed=2 * w_first.size, transcendentals=0
-        ),
-    )(volume, w_first)
+    def spread(framed, vol, wt, offsets, k):
+        lay_columns(rows_last(vol), framed, h, w)
+        return side_by_side(framed, wt, offsets, k)
+
+    def first_own(framed, wt, both_ref):
+        both_ref[...] = side_by_side(framed, wt, (lambda: 1, to_next), 0)
+
+    both = run(
+        first_own, sds((hw, 2 * ob), F32), (framed_own, w_first), (), 36 * hw * cb * ob
+    )
+    taps_first = w_first
+
+    def pair_own(vol, wt, out, framed):
+        out[...] = spread(framed, vol[...], wt, (from_pair,), 0)
+
+    pair_part = run(pair_own, part, (partner, taps_first), scratch_in, 18 * hw * cb * ob)
 
     def first_rest(*refs):
-        vols, (wt, both_ref, mid_ref, onward_ref, framed) = refs[: nc - 1], refs[nc - 1 :]
+        vols, refs = refs[: nc - 1], refs[nc - 1 :]
+        wt, both_ref, pair_ref, mid_ref, onward_ref, framed = refs
         total = both_ref[...]
         for vol, k in zip(vols, others):
             total += spread(framed, vol[...], wt, (lambda: 1, to_next), k)
-        mid_ref[...] = total[:, :ob]
+        mid_ref[...] = total[:, :ob] + pair_ref[...]
         onward_ref[...] = total[:, ob:]
 
-    both, arrived = lax.optimization_barrier((both, arrived))
+    both, pair_part, arrived = lax.optimization_barrier((both, pair_part, arrived))
+    mid, onward = run(
+        first_rest,
+        [part, part],
+        (*arrived, taps_first, both, pair_part),
+        scratch_in,
+        36 * hw * cb * ob,
+    )
+    mid, onto_chan = lax.optimization_barrier((mid, beyond))
+    beyond_rest = [round_chan(onto_chan, k) for k in others]
     partner_rest = [in_chip(q) for x in arrived for q in jnp.split(x, pieces)]
-    mid, onward = run(first_rest, [part, part], (*arrived, taps_first, both), scratch_in, 36 * hw * cb * ob)
 
     def first_pair(*refs):
-        whole_ref, refs = refs[0], refs[1:]
         count = (nc - 1) * pieces
         parts_in, (wt, mid_ref, sum_ref, edge_ref, framed) = refs[:count], refs[count:]
-        total = mid_ref[...] + spread(framed, whole_ref[...], wt, (from_pair,), 0)
+        total = mid_ref[...]
         for k in others:
             vol = jnp.concatenate([r[...] for r in parts_in[(k - 1) * pieces : k * pieces]])
             total += spread(framed, vol, wt, (from_pair,), k)
@@ -182,14 +181,14 @@
         edge_ref[...] = total.astype(BF16)
 
     so_far, edge_sum = run(
-        first_pair, [part, half], (partner, *partner_rest, taps_first, mid), scratch_in, 36 * hw * cb * ob
+        first_pair, [part, half], (*partner_rest, taps_first, mid), scratch_in, PAIR_COST
     )
     next_edge = next_chip(edge_sum)
 
     def first_next(vol, wt, sum_ref, out, framed):
         out[...] = sum_ref[...] + spread(framed, vol[...], wt, (from_next,), 0)
 
-    side = run(first_next, part, (beyond, taps_first, so_far), scratch_in, 18 * hw * cb * ob)
+    side = run(first_next, part, (beyond, taps_first, so_far), scratch_in)
 
     def hidden_own(*refs):
         vols, (wt, side_ref, b, out, framed) = refs[: nc - 1], refs[nc - 1 :]
@@ -198,23 +197,16 @@
             total += spread(framed, vol[...], wt, (from_next,), k)
         out[...] = jnp.maximum(total + b[...], 0.0).astype(BF16)
 
-    hidden = run(hidden_own, half, (*beyond_rest, taps_first, side, b_first), scratch_in, 18 * hw * cb * ob)
+    hidden = run(hidden_own, half, (*beyond_rest, taps_first, side, b_first), scratch_in)
     pair_hidden = [in_chip(hidden[: hw // 2]), in_chip(hidden[hw // 2 :])]
 
     def second_own(cells, wt, out, framed):
         lay_columns(cells[...].astype(F32), framed, h, w)
         out[...] = nine_taps(framed, depth_taps(1, wt), h, w)
 
-    def second_pair(top, bottom, wt, before, out, framed):
-        cells = jnp.concatenate([top[...], bottom[...]], axis=0)
-        lay_columns(cells.astype(F32), framed, h, w)
-        out[...] = before[...] + nine_taps(framed, depth_taps(2 - 2 * odd(), wt), h, w)
-
     scratch_mid = [pltpu.VMEM(framed_mid.shape, BF16)]
     whole = sds((hw, full), F32)
     second = run(second_own, whole, (hidden, w_second), scratch_mid)
-    second = run(second_pair, whole, (*pair_hidden, w_second, second), scratch_mid)
-
     def wanted(k):
         owner = lax.rem(lax.axis_index("chan") + k, nc)
         return pl.ds(pl.multiple_of(owner * own_out, own_out), own_out)
@@ -239,49 +231,46 @@
             picked = jnp.where(owner == i, cells[:, i * own_out : (i + 1) * own_out], picked)
         return picked
 
-    def lay_edge(edge_ref, mine_ref, b, framed):
+    def beside(top, low, edge, mine, b, wt, before, frames, ks):
         place = lax.axis_index("space")
         inside = jnp.logical_and(place > 0, place < ns - 1)
-        total = edge_ref[...].astype(F32) + mine_ref[...] + b[...]
-        cells = jnp.where(inside, jnp.maximum(total, 0.0), 0.0)
-        lay_columns(cells.astype(BF16).astype(F32), framed, h, w)
-
-    def second_send(edge_ref, mine_ref, b, wt, before, *refs):
-        outs, framed = refs[:-1], refs[-1]
-        lay_edge(edge_ref, mine_ref, b, framed)
-        for k in range(1, nc):
-            taps = taps_for(wt, 2 * odd(), k)
-            sums = columns_for(before, k) + nine_taps(framed, taps, h, w)
-            outs[k - 1][...] = channels_first(sums, h, w).astype(BF16)
-
-    sends = run(
-        second_send,
-        [sds((own_out, h, w), BF16)] * (nc - 1),
-        (next_edge, onward, b_first, w_second, second),
-        scratch_mid,
-        flops=18 * hw * ob * own_out * (nc - 1),
-    )
-    parts = [round_chan(sends[k - 1], k) for k in range(1, nc)]
-
-    def second_keep(edge_ref, mine_ref, b_mid, wt, before, b, out, framed):
-        lay_edge(edge_ref, mine_ref, b_mid, framed)
-        taps = taps_for(wt, 2 * odd(), 0)
-        sums = columns_for(before, 0) + nine_taps(framed, taps, h, w)
-        out[...] = channels_first(sums + b[...], h, w)
-
+        total = edge[...].astype(F32) + mine[...] + b[...]
+        edge_cells = jnp.where(inside, jnp.maximum(total, 0.0), 0.0)
+        pair_cells = jnp.concatenate([top[...], low[...]], axis=0).astype(F32)
+        lay_columns(pair_cells, frames.at[0], h, w)
+        lay_columns(edge_cells, frames.at[1], h, w)
+        for k in ks:
+            sums = nine_taps(frames.at[0], taps_for(wt, 2 - 2 * odd(), k), h, w)
+            sums += nine_taps(frames.at[1], taps_for(wt, 2 * odd(), k), h, w)
+            yield sums + columns_for(before, k)
+
+    def second_send(*refs):
+        ins, outs, frames = refs[:7], refs[7:-1], refs[-1]
+        for out, sums in zip(outs, beside(*ins, frames, others)):
+            out[...] = sums.astype(BF16)
+
+    def second_keep(*refs):
+        ins, (b, out, frames) = refs[:7], refs[7:]
+        for sums in beside(*ins, frames, [0]):
+            out[...] = sums + b[...]
+
+    two_frames = [pltpu.VMEM((2, (h + 2) * w, 3 * ob), BF16)]
+    beside_in = (*pair_hidden, next_edge, onward, b_first, w_second, second)
+    sends = run(second_send, [sds((hw, own_out), BF16)] * (nc - 1), beside_in, two_frames)
+    parts = [round_chan(sends[k - 1], k) for k in others]
     kept = run(
         second_keep,
-        sds((own_out, h, w), F32),
-        (next_edge, onward, b_first, w_second, second, b_second),
-        scratch_mid,
-        flops=18 * hw * ob * own_out,
+        sds((hw, own_out), F32),
+        (*beside_in, b_second),
+        two_frames,
+        flops=36 * hw * ob * own_out,
     )
 
     def finish(kept_ref, *refs):
-        total = kept_ref[...]
+        total, out = kept_ref[...], refs[-1]
         for ref in refs[:-1]:
             total += ref[...].astype(F32)
-        refs[-1][...] = jnp.maximum(total, 0.0).astype(BF16)
+        out[...] = channels_first(jnp.maximum(total, 0.0), h, w).astype(BF16)
 
     result = run(finish, sds((own_out, h, w), BF16), (kept, *parts), flops=2 * hw * own_out)
     return result.reshape(own_out, 1, h, w)

time: 35.1 us -> 34 us (0.969)
  waiting for transfers between devices: 7.83 us -> 11 us
  starting transfers between devices: 14.1 us -> 11.3 us
  local copies, waits for them, and re-layouts: 2.47 us -> 0.99 us
    ppermute x2 -> x3, waiting for transfers between devices: 4.74 us -> 7.49 us  [per_device(): lax.ppermute(x, 'chan', [(i, (i + k) % nc) for i in range(nc)])]
    ppermute x1 -> x0, starting transfers between devices: 2.5 us -> none  [per_device(): lax.ppermute(x, ('space', 'chan'), [(i * nc + c, j * nc + (c + k) % nc) f...]
    pallas_call x9 -> x11, Pallas kernels: 8.67 us -> 10.3 us  [run(): pl.pallas_call(kernel, out_shape=outs, scratch_shapes=scratch, compiler_p...]
    unnamed x10, local copies, waits for them, and re-layouts: 2.44 us -> 0.97 us
    pallas_call x1 -> x0, Pallas kernels: 1.41 us -> none  [per_device(): pl.pallas_call(first_own, out_shape=[sds((hw, 2 * ob), F32), sds(w_first....]
    ppermute x2, waiting for transfers between devices: 2.65 us -> 3.36 us  [per_device(): next_chip = lambda x: lax.ppermute(x, 'space', beside)]
    ppermute x5 -> x4, starting transfers between devices: 2.57 us -> 2.09 us  [per_device(): in_chip = lambda x: lax.ppermute(x, 'space', pairs)]
    ppermute x2, starting transfers between devices: 6.51 us -> 6.96 us  [per_device(): next_chip = lambda x: lax.ppermute(x, 'space', beside)]
  transfers between devices with their start and end apart: 10 -> 9, of which waited for: 4 -> 6; matrix products, arithmetic and copies ran while one was open for 0% -> 0% of each run, Pallas kernels for 24% -> 23%
where the time goes in v3:
time: 34 us; the launch traced here: 33.8 us
  starting transfers between devices  11.3 us (33%)
  waiting for transfers between devices  11 us (32%)
  Pallas kernels  10.3 us (30%)
  local copies, waits for them, and re-layouts  0.99 us (3%)
    pallas_call x11, Pallas kernels, run(): pl.pallas_call(kernel, out_shape=outs, scratch_shapes=scratch, compiler_p...  10.3 us
    ppermute x3, waiting for transfers between devices, per_device(): lax.ppermute(x, 'chan', [(i, (i + k) % nc) for i in range(nc)])  7.49 us
    ppermute x2, starting transfers between devices, per_device(): next_chip = lambda x: lax.ppermute(x, 'space', beside)  6.96 us
    ppermute x2, waiting for transfers between devices, per_device(): next_chip = lambda x: lax.ppermute(x, 'space', beside)  3.36 us
    ppermute x3, starting transfers between devices, per_device(): lax.ppermute(x, 'chan', [(i, (i + k) % nc) for i in range(nc)])  2.28 us
    ppermute x4, starting transfers between devices, per_device(): in_chip = lambda x: lax.ppermute(x, 'space', pairs)  2.09 us
    unnamed x10, local copies, waits for them, and re-layouts  0.97 us
  transfers between devices with their start and end apart: 9, of which 6 were waited for; matrix products, arithmetic and copies ran while one was open for 0% of the time, Pallas kernels for 23%

profile of v3, /device:TPU:9, one launch (start us, length us, event | category | flops | bytes accessed | tf_op | source)
XLA Modules:
  0.0 33.8 jit_solution(17367296484950601221)
XLA Ops:
  0.0 0.0 copy-start
  0.0 0.7 %collective-permute-start = (bf16[128,8,128]{2,1,0:T(8,128)(2,1)}, bf16[128,8,128]{2,1,0:T(8,128)(2,1)S(1)}, u32[]{:S(2)}, u32[]{:S(2)}) collective-permute-start(bf16[128,8,128]{2,1,0:T(8,128)(2,1)} %bitcast.21), channel_id=1, source_target_pairs={{0,2},{2,0},{4,6},{6,4},{8,10},{10,8},{12,14},{14,12},{16,18},{18,... | collective-permute-start | bytes 786440 | tf_op jit(solution)/shard_map/ppermute | solution.py:96
  0.7 1.2 %collective-permute-start.1 = (bf16[128,8,128]{2,1,0:T(8,128)(2,1)}, bf16[128,8,128]{2,1,0:T(8,128)(2,1)S(1)}, u32[]{:S(2)}, u32[]{:S(2)}) collective-permute-start(bf16[128,8,128]{2,1,0:T(8,128)(2,1)} %bitcast.22), channel_id=1, source_target_pairs={{0,1},{1,0},{2,3},{3,2},{4,5},{5,4},{6,7},{7,6},{8,9},{9,8},{10,11... | collective-permute-start | bytes 786440 | tf_op jit(solution)/shard_map/ppermute | solution.py:98
  1.9 3.3 %collective-permute-start.2 = (bf16[128,8,128]{2,1,0:T(8,128)(2,1)}, bf16[128,8,128]{2,1,0:T(8,128)(2,1)S(1)}, u32[]{:S(2)}, u32[]{:S(2)}) collective-permute-start(bf16[128,8,128]{2,1,0:T(8,128)(2,1)} %bitcast.23), channel_id=1, source_target_pairs={{2,4},{6,8},{10,12},{14,16},{18,20},{22,24},{26,28},{4,2},{8,6},{1... | collective-permute-start | bytes 786440 | tf_op jit(solution)/shard_map/ppermute | solution.py:97
  5.3 0.0 copy-start.4
  5.3 1.0 %copy-done.4 = bf16[128,1,8,128]{3,2,1,0:T(8,128)(2,1)S(1)} copy-done((bf16[128,1,8,128]{3,2,1,0:T(8,128)(2,1)S(1)}, bf16[128,1,8,128]{3,2,1,0:T(8,128)(2,1)}, u32[]{:S(2)}) %copy-start.4) | copy-done | bytes 262168
  6.2 0.2 shard_map.55.framed
  6.4 0.0 copy-done
  6.5 0.9 %shard_map.56.refs_2_ = f32[1024,256]{1,0:T(8,128)S(1)} custom-call(bf16[1280,384]{1,0:T(8,128)(2,1)S(1)} %shard_map.55.framed, bf16[27,256,128]{2,1,0:T(8,128)(2,1)S(1)} %bitcast.8), custom_call_target="tpu_custom_call" | custom-call | flops 603979776 | bytes 2752512 | tf_op jit(solution)/shard_map/pallas_call | solution.py:23
  7.3 0.0 collective-permute-done.vol
  7.3 0.9 %shard_map.57.refs_3_ = f32[1024,128]{1,0:T(8,128)S(1)} custom-call(bf16[128,8,128]{2,1,0:T(8,128)(2,1)S(1)} %collective-permute-done.vol, bf16[27,256,128]{2,1,0:T(8,128)(2,1)S(1)} %bitcast.9), custom_call_target="tpu_custom_call" | custom-call | flops 301989888 | bytes 2031616 | tf_op jit(solution)/shard_map/pallas_call | solution.py:23
  8.2 0.6 %collective-permute-done.1.refs_0_ = bf16[128,8,128]{2,1,0:T(8,128)(2,1)S(1)} collective-permute-done((bf16[128,8,128]{2,1,0:T(8,128)(2,1)}, bf16[128,8,128]{2,1,0:T(8,128)(2,1)S(1)}, u32[]{:S(2)}, u32[]{:S(2)}) %collective-permute-start.1) | collective-permute-done | bytes 262176 | tf_op jit(solution)/shard_map/ppermute | solution.py:98
  8.8 0.8 %collective-permute-start.4 = (bf16[128,8,128]{2,1,0:T(8,128)(2,1)S(1)}, bf16[128,8,128]{2,1,0:T(8,128)(2,1)S(1)}, u32[]{:S(2)}, u32[]{:S(2)}) collective-permute-start(bf16[128,8,128]{2,1,0:T(8,128)(2,1)S(1)} %collective-permute-done.1.refs_0_), channel_id=1, source_target_pairs={{0,2},{2,0},{4,6},{6,4},{8,10},{10,8},{12,14},{14,12},{16,18},{18,... | collective-permute-start | bytes 786440 | tf_op jit(solution)/shard_map/ppermute | solution.py:96
  9.6 0.9 %shard_map.58 = (f32[1024,128]{1,0:T(8,128)S(1)}, f32[1024,128]{1,0:T(8,128)S(1)}) custom-call(bf16[128,8,128]{2,1,0:T(8,128)(2,1)S(1)} %collective-permute-done.1.refs_0_, bf16[27,256,128]{2,1,0:T(8,128)(2,1)S(1)} %bitcast.10, f32[1024,256]{1,0:T(8,128)S(1)} %shard_map.56.refs_2_, f32[1024,128]{1,0:T(8,128)S(1)} %shard_map.57.refs_3_), custom_call_target="tpu_custom_call" | custom-call | flops 603979776 | bytes 3604480 | tf_op jit(solution)/shard_map/pallas_call | solution.py:23
  10.6 2.1 %collective-permute-done.2.vol = bf16[128,8,128]{2,1,0:T(8,128)(2,1)S(1)} collective-permute-done((bf16[128,8,128]{2,1,0:T(8,128)(2,1)}, bf16[128,8,128]{2,1,0:T(8,128)(2,1)S(1)}, u32[]{:S(2)}, u32[]{:S(2)}) %collective-permute-start.2) | collective-permute-done | bytes 262176 | tf_op jit(solution)/shard_map/ppermute | solution.py:97
  12.6 0.2 collective-permute-start.3
  12.8 0.0 collective-permute-done.4.refs_0_
  12.8 0.9 %shard_map.59 = (f32[1024,128]{1,0:T(8,128)S(1)}, bf16[1024,128]{1,0:T(8,128)(2,1)S(1)}) custom-call(bf16[128,8,128]{2,1,0:T(8,128)(2,1)S(1)} %collective-permute-done.4.refs_0_, bf16[27,256,128]{2,1,0:T(8,128)(2,1)S(1)} %bitcast.11, f32[1024,128]{1,0:T(8,128)S(1)} %get-tuple-element.19.refs_2_), custom_call_target="tpu_custom_call" | custom-call | flops 268435456 | bytes 2555904 | tf_op jit(solution)/shard_map/pallas_call | solution.py:23
  13.7 0.0 copy-start.2
  13.7 3.6 %collective-permute-start.7 = (bf16[1024,128]{1,0:T(8,128)(2,1)S(1)}, bf16[1024,128]{1,0:T(8,128)(2,1)S(1)}, u32[]{:S(2)}, u32[]{:S(2)}) collective-permute-start(bf16[1024,128]{1,0:T(8,128)(2,1)S(1)} %get-tuple-element.21), channel_id=1, source_target_pairs={{2,4},{6,8},{10,12},{14,16},{18,20},{22,24},{26,28},{4,2},{8,6},{1... | collective-permute-start | bytes 786440 | tf_op jit(solution)/shard_map/ppermute | solution.py:97
  17.4 0.9 %shard_map.60.refs_2_ = f32[1024,128]{1,0:T(8,128)S(1)} custom-call(bf16[128,8,128]{2,1,0:T(8,128)(2,1)S(1)} %collective-permute-done.2.vol, bf16[27,256,128]{2,1,0:T(8,128)(2,1)S(1)} %bitcast.12, f32[1024,128]{1,0:T(8,128)S(1)} %get-tuple-element.20.sum_ref), custom_call_target="tpu_custom_call" | custom-call | tf_op jit(solution)/shard_map/pallas_call | solution.py:23
  18.3 0.0 copy-start.1
  18.3 1.7 %collective-permute-done.3.refs_0_ = bf16[128,8,128]{2,1,0:T(8,128)(2,1)S(1)} collective-permute-done((bf16[128,8,128]{2,1,0:T(8,128)(2,1)S(1)}, bf16[128,8,128]{2,1,0:T(8,128)(2,1)S(1)}, u32[]{:S(2)}, u32[]{:S(2)}) %collective-permute-start.3) | collective-permute-done | bytes 262176 | tf_op jit(solution)/shard_map/ppermute | solution.py:98
  19.9 0.0 copy-done.2
  19.9 0.9 %shard_map.61.cells = bf16[1024,128]{1,0:T(8,128)(2,1)S(1)} custom-call(bf16[128,8,128]{2,1,0:T(8,128)(2,1)S(1)} %collective-permute-done.3.refs_0_, bf16[27,256,128]{2,1,0:T(8,128)(2,1)S(1)} %bitcast.13, f32[1024,128]{1,0:T(8,128)S(1)} %shard_map.60.refs_2_, f32[1,128]{1,0:T(1,128)S(1)} %bitcast.17), custom_call_target="tpu_custom_call" | custom-call | tf_op jit(solution)/shard_map/pallas_call | solution.py:23
  20.9 0.1 collective-permute-start.5
  20.9 0.5 %collective-permute-start.6 = (bf16[512,128]{1,0:T(8,128)(2,1)S(1)}, bf16[512,128]{1,0:T(8,128)(2,1)S(1)}, u32[]{:S(2)}, u32[]{:S(2)}) collective-permute-start(bf16[512,128]{1,0:T(8,128)(2,1)S(1)} %get-tuple-element.23), channel_id=1, source_target_pairs={{0,2},{2,0},{4,6},{6,4},{8,10},{10,8},{12,14},{14,12},{16,18},{18,... | collective-permute-start | bytes 393224 | tf_op jit(solution)/shard_map/ppermute | solution.py:96
  21.4 0.0 copy-done.1
  21.4 0.9 %shard_map.62.refs_6_ = f32[1024,256]{1,0:T(8,128)S(1)} custom-call(bf16[1024,128]{1,0:T(8,128)(2,1)S(1)} %shard_map.61.cells, bf16[27,128,256]{2,1,0:T(8,128)(2,1)S(1)} %bitcast.14), custom_call_target="tpu_custom_call" | custom-call | tf_op jit(solution)/shard_map/pallas_call | solution.py:23
  22.3 0.0 collective-permute-done.5.refs_0_
  22.3 0.1 collective-permute-done.6.refs_1_
  22.5 1.3 %collective-permute-done.7.refs_2_ = bf16[1024,128]{1,0:T(8,128)(2,1)S(1)} collective-permute-done((bf16[1024,128]{1,0:T(8,128)(2,1)S(1)}, bf16[1024,128]{1,0:T(8,128)(2,1)S(1)}, u32[]{:S(2)}, u32[]{:S(2)}) %collective-permute-start.7) | collective-permute-done | bytes 262176 | tf_op jit(solution)/shard_map/ppermute | solution.py:97
  23.8 0.0 copy-start.3
  23.8 1.5 %shard_map.64 = bf16[1024,128]{1,0:T(8,128)(2,1)S(1)} custom-call(bf16[512,128]{1,0:T(8,128)(2,1)S(1)} %collective-permute-done.5.refs_0_, bf16[512,128]{1,0:T(8,128)(2,1)S(1)} %collective-permute-done.6.refs_1_, bf16[1024,128]{1,0:T(8,128)(2,1)S(1)} %collective-permute-done.7.refs_2_, f32[1024,128]{1,0:T(8,128)S(1)} %get-tuple-element.22.refs_3_, ...), custom_call_target="tpu_custom_call" | custom-call | tf_op jit(solution)/shard_map/pallas_call | solution.py:23
  25.3 0.8 %collective-permute-start.8 = (bf16[1024,128]{1,0:T(8,128)(2,1)S(1)}, bf16[1024,128]{1,0:T(8,128)(2,1)S(1)}, u32[]{:S(2)}, u32[]{:S(2)}) collective-permute-start(bf16[1024,128]{1,0:T(8,128)(2,1)S(1)} %shard_map.64), channel_id=1, source_target_pairs={{0,1},{1,0},{2,3},{3,2},{4,5},{5,4},{6,7},{7,6},{8,9},{9,8},{10,11... | collective-permute-start | bytes 786440 | tf_op jit(solution)/shard_map/ppermute | solution.py:98
  26.1 0.0 copy-done.3
  26.1 1.5 %shard_map.63.kept_ref = f32[1024,128]{1,0:T(8,128)S(1)} custom-call(bf16[512,128]{1,0:T(8,128)(2,1)S(1)} %collective-permute-done.5.refs_0_, bf16[512,128]{1,0:T(8,128)(2,1)S(1)} %collective-permute-done.6.refs_1_, bf16[1024,128]{1,0:T(8,128)(2,1)S(1)} %collective-permute-done.7.refs_2_, f32[1024,128]{1,0:T(8,128)S(1)} %get-tuple-element.22.refs_3_, ...), custom_call_target="tpu_custom_call" | custom-call | flops 603979776 | bytes 3867648 | tf_op jit(solution)/shard_map/pallas_call | solution.py:23
  27.6 5.3 %collective-permute-done.8.refs_0_ = bf16[1024,128]{1,0:T(8,128)(2,1)S(1)} collective-permute-done((bf16[1024,128]{1,0:T(8,128)(2,1)S(1)}, bf16[1024,128]{1,0:T(8,128)(2,1)S(1)}, u32[]{:S(2)}, u32[]{:S(2)}) %collective-permute-start.8) | collective-permute-done | bytes 262176 | tf_op jit(solution)/shard_map/ppermute | solution.py:98
  32.8 1.0 %shard_map.65 = bf16[128,8,128]{2,1,0:T(8,128)(2,1)} custom-call(f32[1024,128]{1,0:T(8,128)S(1)} %shard_map.63.kept_ref, bf16[1024,128]{1,0:T(8,128)(2,1)S(1)} %collective-permute-done.8.refs_0_), custom_call_target="tpu_custom_call" | custom-call | flops 262144 | bytes 786432 | tf_op jit(solution)/shard_map/pallas_call | solution.py:23
  (1 shorter events, 0.0 us)
Async XLA Ops:
  0.0 6.4 %copy-start = (bf16[256,27,128]{2,0,1:T(8,128)(2,1)S(1)}, bf16[256,27,128]{2,0,1:T(8,128)(2,1)}, u32[]{:S(2)}) copy-start(bf16[256,27,128]{2,0,1:T(8,128)(2,1)} %param.6) | copy-start | bytes 5308420
  0.0 7.3 %collective-permute-start = (bf16[128,8,128]{2,1,0:T(8,128)(2,1)}, bf16[128,8,128]{2,1,0:T(8,128)(2,1)S(1)}, u32[]{:S(2)}, u32[]{:S(2)}) collective-permute-start(bf16[128,8,128]{2,1,0:T(8,128)(2,1)} %bitcast.21), channel_id=1, source_target_pairs={{0,2},{2,0},{4,6},{6,4},{8,10},{10,8},{12,14},{14,12},{16,18},{18,... | collective-permute-start | bytes 786440 | tf_op jit(solution)/shard_map/ppermute | solution.py:96
  0.7 8.1 %collective-permute-start.1 = (bf16[128,8,128]{2,1,0:T(8,128)(2,1)}, bf16[128,8,128]{2,1,0:T(8,128)(2,1)S(1)}, u32[]{:S(2)}, u32[]{:S(2)}) collective-permute-start(bf16[128,8,128]{2,1,0:T(8,128)(2,1)} %bitcast.22), channel_id=1, source_target_pairs={{0,1},{1,0},{2,3},{3,2},{4,5},{5,4},{6,7},{7,6},{8,9},{9,8},{10,11... | collective-permute-start | bytes 786440 | tf_op jit(solution)/shard_map/ppermute | solution.py:98
  1.9 10.7 %collective-permute-start.2 = (bf16[128,8,128]{2,1,0:T(8,128)(2,1)}, bf16[128,8,128]{2,1,0:T(8,128)(2,1)S(1)}, u32[]{:S(2)}, u32[]{:S(2)}) collective-permute-start(bf16[128,8,128]{2,1,0:T(8,128)(2,1)} %bitcast.23), channel_id=1, source_target_pairs={{2,4},{6,8},{10,12},{14,16},{18,20},{22,24},{26,28},{4,2},{8,6},{1... | collective-permute-start | bytes 786440 | tf_op jit(solution)/shard_map/ppermute | solution.py:97
  5.3 1.0 %copy-start.4 = (bf16[128,1,8,128]{3,2,1,0:T(8,128)(2,1)S(1)}, bf16[128,1,8,128]{3,2,1,0:T(8,128)(2,1)}, u32[]{:S(2)}) copy-start(bf16[128,1,8,128]{3,2,1,0:T(8,128)(2,1)} %param.5) | copy-start | bytes 786436
  8.8 4.1 %collective-permute-start.4 = (bf16[128,8,128]{2,1,0:T(8,128)(2,1)S(1)}, bf16[128,8,128]{2,1,0:T(8,128)(2,1)S(1)}, u32[]{:S(2)}, u32[]{:S(2)}) collective-permute-start(bf16[128,8,128]{2,1,0:T(8,128)(2,1)S(1)} %collective-permute-done.1.refs_0_), channel_id=1, source_target_pairs={{0,2},{2,0},{4,6},{6,4},{8,10},{10,8},{12,14},{14,12},{16,18},{18,... | collective-permute-start | bytes 786440 | tf_op jit(solution)/shard_map/ppermute | solution.py:96
  12.6 7.3 %collective-permute-start.3 = (bf16[128,8,128]{2,1,0:T(8,128)(2,1)S(1)}, bf16[128,8,128]{2,1,0:T(8,128)(2,1)S(1)}, u32[]{:S(2)}, u32[]{:S(2)}) collective-permute-start(bf16[128,8,128]{2,1,0:T(8,128)(2,1)S(1)} %collective-permute-done.2.vol), channel_id=1, source_target_pairs={{0,1},{1,0},{2,3},{3,2},{4,5},{5,4},{6,7},{7,6},{8,9},{9,8},{10,11... | collective-permute-start | bytes 786440 | tf_op jit(solution)/shard_map/ppermute | solution.py:98
  13.7 6.2 %copy-start.2 = (f32[128]{0:T(128)S(1)}, f32[128]{0:T(128)}, u32[]{:S(2)}) copy-start(f32[128]{0:T(128)} %param.7) | copy-start | bytes 1540
  13.7 10.0 %collective-permute-start.7 = (bf16[1024,128]{1,0:T(8,128)(2,1)S(1)}, bf16[1024,128]{1,0:T(8,128)(2,1)S(1)}, u32[]{:S(2)}, u32[]{:S(2)}) collective-permute-start(bf16[1024,128]{1,0:T(8,128)(2,1)S(1)} %get-tuple-element.21), channel_id=1, source_target_pairs={{2,4},{6,8},{10,12},{14,16},{18,20},{22,24},{26,28},{4,2},{8,6},{1... | collective-permute-start | bytes 786440 | tf_op jit(solution)/shard_map/ppermute | solution.py:97
  18.3 3.2 %copy-start.1 = (bf16[128,27,256]{2,0,1:T(8,128)(2,1)S(1)}, bf16[128,27,256]{2,0,1:T(8,128)(2,1)}, u32[]{:S(2)}) copy-start(bf16[128,27,256]{2,0,1:T(8,128)(2,1)} %param.8) | copy-start | bytes 5308420
  20.9 1.4 %collective-permute-start.5 = (bf16[512,128]{1,0:T(8,128)(2,1)S(1)}, bf16[512,128]{1,0:T(8,128)(2,1)S(1)}, u32[]{:S(2)}, u32[]{:S(2)}) collective-permute-start(bf16[512,128]{1,0:T(8,128)(2,1)S(1)} %get-tuple-element.24), channel_id=1, source_target_pairs={{0,2},{2,0},{4,6},{6,4},{8,10},{10,8},{12,14},{14,12},{16,18},{18,... | collective-permute-start | bytes 393224 | tf_op jit(solution)/shard_map/ppermute | solution.py:96
  20.9 1.5 %collective-permute-start.6 = (bf16[512,128]{1,0:T(8,128)(2,1)S(1)}, bf16[512,128]{1,0:T(8,128)(2,1)S(1)}, u32[]{:S(2)}, u32[]{:S(2)}) collective-permute-start(bf16[512,128]{1,0:T(8,128)(2,1)S(1)} %get-tuple-element.23), channel_id=1, source_target_pairs={{0,2},{2,0},{4,6},{6,4},{8,10},{10,8},{12,14},{14,12},{16,18},{18,... | collective-permute-start | bytes 393224 | tf_op jit(solution)/shard_map/ppermute | solution.py:96
  23.8 2.3 %copy-start.3 = (f32[128]{0:T(128)S(1)}, f32[128]{0:T(128)}, u32[]{:S(2)}) copy-start(f32[128]{0:T(128)} %param.9) | copy-start | bytes 1540
  25.3 7.6 %collective-permute-start.8 = (bf16[1024,128]{1,0:T(8,128)(2,1)S(1)}, bf16[1024,128]{1,0:T(8,128)(2,1)S(1)}, u32[]{:S(2)}, u32[]{:S(2)}) collective-permute-start(bf16[1024,128]{1,0:T(8,128)(2,1)S(1)} %shard_map.64), channel_id=1, source_target_pairs={{0,1},{1,0},{2,3},{3,2},{4,5},{5,4},{6,7},{7,6},{8,9},{9,8},{10,11... | collective-permute-start | bytes 786440 | tf_op jit(solution)/shard_map/ppermute | solution.py:98

commit v4 on v3

--- a/solution.py
+++ b/solution.py
@@ -144,25 +144,20 @@
     )
     taps_first = w_first
 
-    def pair_own(vol, wt, out, framed):
-        out[...] = spread(framed, vol[...], wt, (from_pair,), 0)
-
-    pair_part = run(pair_own, part, (partner, taps_first), scratch_in, 18 * hw * cb * ob)
-
     def first_rest(*refs):
         vols, refs = refs[: nc - 1], refs[nc - 1 :]
-        wt, both_ref, pair_ref, mid_ref, onward_ref, framed = refs
+        wt, both_ref, mid_ref, onward_ref, framed = refs
         total = both_ref[...]
         for vol, k in zip(vols, others):
             total += spread(framed, vol[...], wt, (lambda: 1, to_next), k)
-        mid_ref[...] = total[:, :ob] + pair_ref[...]
+        mid_ref[...] = total[:, :ob]
         onward_ref[...] = total[:, ob:]
 
-    both, pair_part, arrived = lax.optimization_barrier((both, pair_part, arrived))
+    both, arrived = lax.optimization_barrier((both, arrived))
     mid, onward = run(
         first_rest,
         [part, part],
-        (*arrived, taps_first, both, pair_part),
+        (*arrived, taps_first, both),
         scratch_in,
         36 * hw * cb * ob,
     )
@@ -171,9 +166,10 @@
     partner_rest = [in_chip(q) for x in arrived for q in jnp.split(x, pieces)]
 
     def first_pair(*refs):
+        whole_ref, refs = refs[0], refs[1:]
         count = (nc - 1) * pieces
         parts_in, (wt, mid_ref, sum_ref, edge_ref, framed) = refs[:count], refs[count:]
-        total = mid_ref[...]
+        total = mid_ref[...] + spread(framed, whole_ref[...], wt, (from_pair,), 0)
         for k in others:
             vol = jnp.concatenate([r[...] for r in parts_in[(k - 1) * pieces : k * pieces]])
             total += spread(framed, vol, wt, (from_pair,), k)
@@ -181,7 +177,7 @@
         edge_ref[...] = total.astype(BF16)
 
     so_far, edge_sum = run(
-        first_pair, [part, half], (*partner_rest, taps_first, mid), scratch_in, PAIR_COST
+        first_pair, [part, half], (partner, *partner_rest, taps_first, mid), scratch_in, PAIR_COST
     )
     next_edge = next_chip(edge_sum)
 

time: 34 us -> 33.9 us (level)
  starting transfers between devices: 11.3 us -> 12.8 us
  waiting for transfers between devices: 11 us -> 9.67 us
    ppermute x3, waiting for transfers between devices: 7.49 us -> 5.51 us  [per_device(): lax.ppermute(x, 'chan', [(i, (i + k) % nc) for i in range(nc)])]
    ppermute x2, starting transfers between devices: 6.96 us -> 7.87 us  [per_device(): next_chip = lambda x: lax.ppermute(x, 'space', beside)]
    ppermute x2, waiting for transfers between devices: 3.36 us -> 4.01 us  [per_device(): next_chip = lambda x: lax.ppermute(x, 'space', beside)]
    ppermute x3, starting transfers between devices: 2.28 us -> 2.77 us  [per_device(): lax.ppermute(x, 'chan', [(i, (i + k) % nc) for i in range(nc)])]
    pallas_call x11 -> x10, Pallas kernels: 10.3 us -> 10.1 us  [run(): pl.pallas_call(kernel, out_shape=outs, scratch_shapes=scratch, compiler_p...]
where the time goes in v4:
time: 33.9 us; the launch traced here: 33.7 us
  starting transfers between devices  12.8 us (38%)
  Pallas kernels  10.1 us (30%)
  waiting for transfers between devices  9.67 us (29%)
  local copies, waits for them, and re-layouts  0.98 us (3%)
    pallas_call x10, Pallas kernels, run(): pl.pallas_call(kernel, out_shape=outs, scratch_shapes=scratch, compiler_p...  10.1 us
    ppermute x2, starting transfers between devices, per_device(): next_chip = lambda x: lax.ppermute(x, 'space', beside)  7.87 us
    ppermute x3, waiting for transfers between devices, per_device(): lax.ppermute(x, 'chan', [(i, (i + k) % nc) for i in range(nc)])  5.51 us
    ppermute x2, waiting for transfers between devices, per_device(): next_chip = lambda x: lax.ppermute(x, 'space', beside)  4.01 us
    ppermute x3, starting transfers between devices, per_device(): lax.ppermute(x, 'chan', [(i, (i + k) % nc) for i in range(nc)])  2.77 us
    ppermute x4, starting transfers between devices, per_device(): in_chip = lambda x: lax.ppermute(x, 'space', pairs)  2.19 us
    unnamed x10, local copies, waits for them, and re-layouts  0.96 us
  transfers between devices with their start and end apart: 9, of which 6 were waited for; matrix products, arithmetic and copies ran while one was open for 0% of the time, Pallas kernels for 23%

profile of v4, /device:TPU:9, one launch (start us, length us, event | category | flops | bytes accessed | tf_op | source)
XLA Modules:
  0.0 33.7 jit_solution(295537009078707300)
XLA Ops:
  0.0 0.0 copy-start
  0.0 1.2 %collective-permute-start = (bf16[128,8,128]{2,1,0:T(8,128)(2,1)}, bf16[128,8,128]{2,1,0:T(8,128)(2,1)S(1)}, u32[]{:S(2)}, u32[]{:S(2)}) collective-permute-start(bf16[128,8,128]{2,1,0:T(8,128)(2,1)} %bitcast.20), channel_id=1, source_target_pairs={{0,1},{1,0},{2,3},{3,2},{4,5},{5,4},{6,7},{7,6},{8,9},{9,8},{10,11... | collective-permute-start | bytes 786440 | tf_op jit(solution)/shard_map/ppermute | solution.py:98
  1.2 3.9 %collective-permute-start.1 = (bf16[128,8,128]{2,1,0:T(8,128)(2,1)}, bf16[128,8,128]{2,1,0:T(8,128)(2,1)S(1)}, u32[]{:S(2)}, u32[]{:S(2)}) collective-permute-start(bf16[128,8,128]{2,1,0:T(8,128)(2,1)} %bitcast.21), channel_id=1, source_target_pairs={{2,4},{6,8},{10,12},{14,16},{18,20},{22,24},{26,28},{4,2},{8,6},{1... | collective-permute-start | bytes 786440 | tf_op jit(solution)/shard_map/ppermute | solution.py:97
  5.2 0.1 collective-permute-start.3
  5.3 0.0 copy-start.4
  5.3 0.9 %copy-done.4 = bf16[128,1,8,128]{3,2,1,0:T(8,128)(2,1)S(1)} copy-done((bf16[128,1,8,128]{3,2,1,0:T(8,128)(2,1)S(1)}, bf16[128,1,8,128]{3,2,1,0:T(8,128)(2,1)}, u32[]{:S(2)}) %copy-start.4) | copy-done | bytes 262168
  6.2 0.2 shard_map.55.framed
  6.4 0.0 copy-done
  6.5 0.9 %shard_map.56.refs_2_ = f32[1024,256]{1,0:T(8,128)S(1)} custom-call(bf16[1280,384]{1,0:T(8,128)(2,1)S(1)} %shard_map.55.framed, bf16[27,256,128]{2,1,0:T(8,128)(2,1)S(1)} %bitcast.8), custom_call_target="tpu_custom_call" | custom-call | flops 603979776 | bytes 2752512 | tf_op jit(solution)/shard_map/pallas_call | solution.py:23
  7.3 0.1 collective-permute-done.refs_0_
  7.4 1.5 %collective-permute-start.4 = (bf16[128,8,128]{2,1,0:T(8,128)(2,1)S(1)}, bf16[128,8,128]{2,1,0:T(8,128)(2,1)S(1)}, u32[]{:S(2)}, u32[]{:S(2)}) collective-permute-start(bf16[128,8,128]{2,1,0:T(8,128)(2,1)S(1)} %collective-permute-done.refs_0_), channel_id=1, source_target_pairs={{0,2},{2,0},{4,6},{6,4},{8,10},{10,8},{12,14},{14,12},{16,18},{18,... | collective-permute-start | bytes 786440 | tf_op jit(solution)/shard_map/ppermute | solution.py:96
  8.9 0.9 %shard_map.57 = (f32[1024,128]{1,0:T(8,128)S(1)}, f32[1024,128]{1,0:T(8,128)S(1)}) custom-call(bf16[128,8,128]{2,1,0:T(8,128)(2,1)S(1)} %collective-permute-done.refs_0_, bf16[27,256,128]{2,1,0:T(8,128)(2,1)S(1)} %bitcast.9, f32[1024,256]{1,0:T(8,128)S(1)} %shard_map.56.refs_2_), custom_call_target="tpu_custom_call" | custom-call | flops 603979776 | bytes 3080192 | tf_op jit(solution)/shard_map/pallas_call | solution.py:23
  9.9 2.4 %collective-permute-done.1.vol = bf16[128,8,128]{2,1,0:T(8,128)(2,1)S(1)} collective-permute-done((bf16[128,8,128]{2,1,0:T(8,128)(2,1)}, bf16[128,8,128]{2,1,0:T(8,128)(2,1)S(1)}, u32[]{:S(2)}, u32[]{:S(2)}) %collective-permute-start.1) | collective-permute-done | bytes 262176 | tf_op jit(solution)/shard_map/ppermute | solution.py:97
  12.3 0.4 %collective-permute-start.2 = (bf16[128,8,128]{2,1,0:T(8,128)(2,1)S(1)}, bf16[128,8,128]{2,1,0:T(8,128)(2,1)S(1)}, u32[]{:S(2)}, u32[]{:S(2)}) collective-permute-start(bf16[128,8,128]{2,1,0:T(8,128)(2,1)S(1)} %collective-permute-done.1.vol), channel_id=1, source_target_pairs={{0,1},{1,0},{2,3},{3,2},{4,5},{5,4},{6,7},{7,6},{8,9},{9,8},{10,11... | collective-permute-start | bytes 786440 | tf_op jit(solution)/shard_map/ppermute | solution.py:98
  12.6 0.0 collective-permute-done.3.refs_0_
  12.6 0.0 collective-permute-done.4.refs_1_
  12.6 1.6 %shard_map.58 = (f32[1024,128]{1,0:T(8,128)S(1)}, bf16[1024,128]{1,0:T(8,128)(2,1)S(1)}) custom-call(bf16[128,8,128]{2,1,0:T(8,128)(2,1)S(1)} %collective-permute-done.3.refs_0_, bf16[128,8,128]{2,1,0:T(8,128)(2,1)S(1)} %collective-permute-done.4.refs_1_, bf16[27,256,128]{2,1,0:T(8,128)(2,1)S(1)} %bitcast.10, f32[1024,128]{1,0:T(8,128)S(1)} %get-tuple-element.17.refs_3_), custom_call_target="tpu_custom_call" | custom-call | flops 268435456 | bytes 2818048 | tf_op jit(solution)/shard_map/pallas_call | solution.py:23
  14.2 0.0 copy-start.2
  14.2 3.9 %collective-permute-start.7 = (bf16[1024,128]{1,0:T(8,128)(2,1)S(1)}, bf16[1024,128]{1,0:T(8,128)(2,1)S(1)}, u32[]{:S(2)}, u32[]{:S(2)}) collective-permute-start(bf16[1024,128]{1,0:T(8,128)(2,1)S(1)} %get-tuple-element.19), channel_id=1, source_target_pairs={{2,4},{6,8},{10,12},{14,16},{18,20},{22,24},{26,28},{4,2},{8,6},{1... | collective-permute-start | bytes 786440 | tf_op jit(solution)/shard_map/ppermute | solution.py:97
  18.1 0.9 %shard_map.59.refs_2_ = f32[1024,128]{1,0:T(8,128)S(1)} custom-call(bf16[128,8,128]{2,1,0:T(8,128)(2,1)S(1)} %collective-permute-done.1.vol, bf16[27,256,128]{2,1,0:T(8,128)(2,1)S(1)} %bitcast.11, f32[1024,128]{1,0:T(8,128)S(1)} %get-tuple-element.18.sum_ref), custom_call_target="tpu_custom_call" | custom-call | tf_op jit(solution)/shard_map/pallas_call | solution.py:23
  19.0 0.0 copy-start.1
  19.0 0.8 %collective-permute-done.2.refs_0_ = bf16[128,8,128]{2,1,0:T(8,128)(2,1)S(1)} collective-permute-done((bf16[128,8,128]{2,1,0:T(8,128)(2,1)S(1)}, bf16[128,8,128]{2,1,0:T(8,128)(2,1)S(1)}, u32[]{:S(2)}, u32[]{:S(2)}) %collective-permute-start.2) | collective-permute-done | bytes 262176 | tf_op jit(solution)/shard_map/ppermute | solution.py:98
  19.9 0.0 copy-done.2
  19.9 0.9 %shard_map.60.cells = bf16[1024,128]{1,0:T(8,128)(2,1)S(1)} custom-call(bf16[128,8,128]{2,1,0:T(8,128)(2,1)S(1)} %collective-permute-done.2.refs_0_, bf16[27,256,128]{2,1,0:T(8,128)(2,1)S(1)} %bitcast.12, f32[1024,128]{1,0:T(8,128)S(1)} %shard_map.59.refs_2_, f32[1,128]{1,0:T(1,128)S(1)} %bitcast.16), custom_call_target="tpu_custom_call" | custom-call | tf_op jit(solution)/shard_map/pallas_call | solution.py:23
  20.8 0.1 collective-permute-start.5
  20.9 0.5 %collective-permute-start.6 = (bf16[512,128]{1,0:T(8,128)(2,1)S(1)}, bf16[512,128]{1,0:T(8,128)(2,1)S(1)}, u32[]{:S(2)}, u32[]{:S(2)}) collective-permute-start(bf16[512,128]{1,0:T(8,128)(2,1)S(1)} %get-tuple-element.21), channel_id=1, source_target_pairs={{0,2},{2,0},{4,6},{6,4},{8,10},{10,8},{12,14},{14,12},{16,18},{18,... | collective-permute-start | bytes 393224 | tf_op jit(solution)/shard_map/ppermute | solution.py:96
  21.4 0.0 copy-done.1
  21.4 0.9 %shard_map.61.refs_6_ = f32[1024,256]{1,0:T(8,128)S(1)} custom-call(bf16[1024,128]{1,0:T(8,128)(2,1)S(1)} %shard_map.60.cells, bf16[27,128,256]{2,1,0:T(8,128)(2,1)S(1)} %bitcast.13), custom_call_target="tpu_custom_call" | custom-call | tf_op jit(solution)/shard_map/pallas_call | solution.py:23
  22.2 0.0 collective-permute-done.5.refs_0_
  22.3 0.1 collective-permute-done.6.refs_1_
  22.4 1.6 %collective-permute-done.7.refs_2_ = bf16[1024,128]{1,0:T(8,128)(2,1)S(1)} collective-permute-done((bf16[1024,128]{1,0:T(8,128)(2,1)S(1)}, bf16[1024,128]{1,0:T(8,128)(2,1)S(1)}, u32[]{:S(2)}, u32[]{:S(2)}) %collective-permute-start.7) | collective-permute-done | bytes 262176 | tf_op jit(solution)/shard_map/ppermute | solution.py:97
  24.0 0.0 copy-start.3
  24.0 1.5 %shard_map.63 = bf16[1024,128]{1,0:T(8,128)(2,1)S(1)} custom-call(bf16[512,128]{1,0:T(8,128)(2,1)S(1)} %collective-permute-done.5.refs_0_, bf16[512,128]{1,0:T(8,128)(2,1)S(1)} %collective-permute-done.6.refs_1_, bf16[1024,128]{1,0:T(8,128)(2,1)S(1)} %collective-permute-done.7.refs_2_, f32[1024,128]{1,0:T(8,128)S(1)} %get-tuple-element.20.refs_3_, ...), custom_call_target="tpu_custom_call" | custom-call | tf_op jit(solution)/shard_map/pallas_call | solution.py:23
  25.5 1.2 %collective-permute-start.8 = (bf16[1024,128]{1,0:T(8,128)(2,1)S(1)}, bf16[1024,128]{1,0:T(8,128)(2,1)S(1)}, u32[]{:S(2)}, u32[]{:S(2)}) collective-permute-start(bf16[1024,128]{1,0:T(8,128)(2,1)S(1)} %shard_map.63), channel_id=1, source_target_pairs={{0,1},{1,0},{2,3},{3,2},{4,5},{5,4},{6,7},{7,6},{8,9},{9,8},{10,11... | collective-permute-start | bytes 786440 | tf_op jit(solution)/shard_map/ppermute | solution.py:98
  26.7 0.0 copy-done.3
  26.7 1.5 %shard_map.62.kept_ref = f32[1024,128]{1,0:T(8,128)S(1)} custom-call(bf16[512,128]{1,0:T(8,128)(2,1)S(1)} %collective-permute-done.5.refs_0_, bf16[512,128]{1,0:T(8,128)(2,1)S(1)} %collective-permute-done.6.refs_1_, bf16[1024,128]{1,0:T(8,128)(2,1)S(1)} %collective-permute-done.7.refs_2_, f32[1024,128]{1,0:T(8,128)S(1)} %get-tuple-element.20.refs_3_, ...), custom_call_target="tpu_custom_call" | custom-call | flops 603979776 | bytes 3867648 | tf_op jit(solution)/shard_map/pallas_call | solution.py:23
  28.2 4.6 %collective-permute-done.8.refs_0_ = bf16[1024,128]{1,0:T(8,128)(2,1)S(1)} collective-permute-done((bf16[1024,128]{1,0:T(8,128)(2,1)S(1)}, bf16[1024,128]{1,0:T(8,128)(2,1)S(1)}, u32[]{:S(2)}, u32[]{:S(2)}) %collective-permute-start.8) | collective-permute-done | bytes 262176 | tf_op jit(solution)/shard_map/ppermute | solution.py:98
  32.8 1.0 %shard_map.64 = bf16[128,8,128]{2,1,0:T(8,128)(2,1)} custom-call(f32[1024,128]{1,0:T(8,128)S(1)} %shard_map.62.kept_ref, bf16[1024,128]{1,0:T(8,128)(2,1)S(1)} %collective-permute-done.8.refs_0_), custom_call_target="tpu_custom_call" | custom-call | flops 262144 | bytes 786432 | tf_op jit(solution)/shard_map/pallas_call | solution.py:23
  (1 shorter events, 0.0 us)
Async XLA Ops:
  0.0 6.4 %copy-start = (bf16[256,27,128]{2,0,1:T(8,128)(2,1)S(1)}, bf16[256,27,128]{2,0,1:T(8,128)(2,1)}, u32[]{:S(2)}) copy-start(bf16[256,27,128]{2,0,1:T(8,128)(2,1)} %param.6) | copy-start | bytes 5308420
  0.0 7.4 %collective-permute-start = (bf16[128,8,128]{2,1,0:T(8,128)(2,1)}, bf16[128,8,128]{2,1,0:T(8,128)(2,1)S(1)}, u32[]{:S(2)}, u32[]{:S(2)}) collective-permute-start(bf16[128,8,128]{2,1,0:T(8,128)(2,1)} %bitcast.20), channel_id=1, source_target_pairs={{0,1},{1,0},{2,3},{3,2},{4,5},{5,4},{6,7},{7,6},{8,9},{9,8},{10,11... | collective-permute-start | bytes 786440 | tf_op jit(solution)/shard_map/ppermute | solution.py:98
  1.2 11.0 %collective-permute-start.1 = (bf16[128,8,128]{2,1,0:T(8,128)(2,1)}, bf16[128,8,128]{2,1,0:T(8,128)(2,1)S(1)}, u32[]{:S(2)}, u32[]{:S(2)}) collective-permute-start(bf16[128,8,128]{2,1,0:T(8,128)(2,1)} %bitcast.21), channel_id=1, source_target_pairs={{2,4},{6,8},{10,12},{14,16},{18,20},{22,24},{26,28},{4,2},{8,6},{1... | collective-permute-start | bytes 786440 | tf_op jit(solution)/shard_map/ppermute | solution.py:97
  5.2 7.4 %collective-permute-start.3 = (bf16[128,8,128]{2,1,0:T(8,128)(2,1)}, bf16[128,8,128]{2,1,0:T(8,128)(2,1)S(1)}, u32[]{:S(2)}, u32[]{:S(2)}) collective-permute-start(bf16[128,8,128]{2,1,0:T(8,128)(2,1)} %bitcast.22), channel_id=1, source_target_pairs={{0,2},{2,0},{4,6},{6,4},{8,10},{10,8},{12,14},{14,12},{16,18},{18,... | collective-permute-start | bytes 786440 | tf_op jit(solution)/shard_map/ppermute | solution.py:96
  5.3 1.0 %copy-start.4 = (bf16[128,1,8,128]{3,2,1,0:T(8,128)(2,1)S(1)}, bf16[128,1,8,128]{3,2,1,0:T(8,128)(2,1)}, u32[]{:S(2)}) copy-start(bf16[128,1,8,128]{3,2,1,0:T(8,128)(2,1)} %param.5) | copy-start | bytes 786436
  7.4 5.2 %collective-permute-start.4 = (bf16[128,8,128]{2,1,0:T(8,128)(2,1)S(1)}, bf16[128,8,128]{2,1,0:T(8,128)(2,1)S(1)}, u32[]{:S(2)}, u32[]{:S(2)}) collective-permute-start(bf16[128,8,128]{2,1,0:T(8,128)(2,1)S(1)} %collective-permute-done.refs_0_), channel_id=1, source_target_pairs={{0,2},{2,0},{4,6},{6,4},{8,10},{10,8},{12,14},{14,12},{16,18},{18,... | collective-permute-start | bytes 786440 | tf_op jit(solution)/shard_map/ppermute | solution.py:96
  12.3 7.6 %collective-permute-start.2 = (bf16[128,8,128]{2,1,0:T(8,128)(2,1)S(1)}, bf16[128,8,128]{2,1,0:T(8,128)(2,1)S(1)}, u32[]{:S(2)}, u32[]{:S(2)}) collective-permute-start(bf16[128,8,128]{2,1,0:T(8,128)(2,1)S(1)} %collective-permute-done.1.vol), channel_id=1, source_target_pairs={{0,1},{1,0},{2,3},{3,2},{4,5},{5,4},{6,7},{7,6},{8,9},{9,8},{10,11... | collective-permute-start | bytes 786440 | tf_op jit(solution)/shard_map/ppermute | solution.py:98
  14.2 5.7 %copy-start.2 = (f32[128]{0:T(128)S(1)}, f32[128]{0:T(128)}, u32[]{:S(2)}) copy-start(f32[128]{0:T(128)} %param.7) | copy-start | bytes 1540
  14.2 9.8 %collective-permute-start.7 = (bf16[1024,128]{1,0:T(8,128)(2,1)S(1)}, bf16[1024,128]{1,0:T(8,128)(2,1)S(1)}, u32[]{:S(2)}, u32[]{:S(2)}) collective-permute-start(bf16[1024,128]{1,0:T(8,128)(2,1)S(1)} %get-tuple-element.19), channel_id=1, source_target_pairs={{2,4},{6,8},{10,12},{14,16},{18,20},{22,24},{26,28},{4,2},{8,6},{1... | collective-permute-start | bytes 786440 | tf_op jit(solution)/shard_map/ppermute | solution.py:97
  19.0 2.4 %copy-start.1 = (bf16[128,27,256]{2,0,1:T(8,128)(2,1)S(1)}, bf16[128,27,256]{2,0,1:T(8,128)(2,1)}, u32[]{:S(2)}) copy-start(bf16[128,27,256]{2,0,1:T(8,128)(2,1)} %param.8) | copy-start | bytes 5308420
  20.8 1.4 %collective-permute-start.5 = (bf16[512,128]{1,0:T(8,128)(2,1)S(1)}, bf16[512,128]{1,0:T(8,128)(2,1)S(1)}, u32[]{:S(2)}, u32[]{:S(2)}) collective-permute-start(bf16[512,128]{1,0:T(8,128)(2,1)S(1)} %get-tuple-element.22), channel_id=1, source_target_pairs={{0,2},{2,0},{4,6},{6,4},{8,10},{10,8},{12,14},{14,12},{16,18},{18,... | collective-permute-start | bytes 393224 | tf_op jit(solution)/shard_map/ppermute | solution.py:96
  20.9 1.5 %collective-permute-start.6 = (bf16[512,128]{1,0:T(8,128)(2,1)S(1)}, bf16[512,128]{1,0:T(8,128)(2,1)S(1)}, u32[]{:S(2)}, u32[]{:S(2)}) collective-permute-start(bf16[512,128]{1,0:T(8,128)(2,1)S(1)} %get-tuple-element.21), channel_id=1, source_target_pairs={{0,2},{2,0},{4,6},{6,4},{8,10},{10,8},{12,14},{14,12},{16,18},{18,... | collective-permute-start | bytes 393224 | tf_op jit(solution)/shard_map/ppermute | solution.py:96
  24.0 2.7 %copy-start.3 = (f32[128]{0:T(128)S(1)}, f32[128]{0:T(128)}, u32[]{:S(2)}) copy-start(f32[128]{0:T(128)} %param.9) | copy-start | bytes 1540
  25.5 7.3 %collective-permute-start.8 = (bf16[1024,128]{1,0:T(8,128)(2,1)S(1)}, bf16[1024,128]{1,0:T(8,128)(2,1)S(1)}, u32[]{:S(2)}, u32[]{:S(2)}) collective-permute-start(bf16[1024,128]{1,0:T(8,128)(2,1)S(1)} %shard_map.63), channel_id=1, source_target_pairs={{0,1},{1,0},{2,3},{3,2},{4,5},{5,4},{6,7},{7,6},{8,9},{9,8},{10,11... | collective-permute-start | bytes 786440 | tf_op jit(solution)/shard_map/ppermute | solution.py:98

commit v5 on v4

--- a/solution.py
+++ b/solution.py
@@ -56,16 +56,17 @@
     framed[w : w + hw, 2 * c : 3 * c] = right.astype(BF16)
 
 
-def nine_taps(framed, weights, h, w):
+def nine_taps(framed, weights, h, w, first=0):
     hw = h * w
     _, c, n = weights.shape
+    at = [slice((first + b) * w, (first + b) * w + hw) for b in range(3)]
     if c % 128 == 0:
-        lhs = jnp.concatenate([framed[b * w : b * w + hw] for b in range(3)], axis=1)
+        lhs = jnp.concatenate([framed[rows] for rows in at], axis=1)
         return jnp.dot(lhs, weights.reshape(9 * c, n), preferred_element_type=F32)
     total = None
     for b in range(3):
         term = jnp.dot(
-            framed[b * w : b * w + hw],
+            framed[at[b]],
             weights[3 * b : 3 * b + 3].reshape(3 * c, n),
             preferred_element_type=F32,
         )
@@ -217,43 +218,63 @@
             picked = jnp.where(owner == i, taps[:, :, i * own_out : (i + 1) * own_out], picked)
         return picked
 
-    def columns_for(ref, k):
+    def columns_for(ref, rows, k):
         if own_out % 128 == 0:
-            return ref[:, wanted(k)]
+            return ref[rows, wanted(k)]
         owner = lax.rem(lax.axis_index("chan") + k, nc)
-        cells = ref[...]
+        cells = ref[rows]
         picked = cells[:, 0:own_out]
         for i in range(1, nc):
             picked = jnp.where(owner == i, cells[:, i * own_out : (i + 1) * own_out], picked)
         return picked
 
-    def beside(top, low, edge, mine, b, wt, before, frames, ks):
+    def beside_rows(top, low, edge, mine, b, wt, before, frames, ks, start, stop):
+        first, last = max(start - 1, 0), min(stop + 1, h)
+        rows = slice(first * w, last * w)
+        count = last - first
+        pair_cells = jnp.concatenate([top[...], low[...]], axis=0)[rows].astype(F32)
         place = lax.axis_index("space")
         inside = jnp.logical_and(place > 0, place < ns - 1)
-        total = edge[...].astype(F32) + mine[...] + b[...]
+        total = edge[rows].astype(F32) + mine[rows] + b[...]
         edge_cells = jnp.where(inside, jnp.maximum(total, 0.0), 0.0)
-        pair_cells = jnp.concatenate([top[...], low[...]], axis=0).astype(F32)
-        lay_columns(pair_cells, frames.at[0], h, w)
-        lay_columns(edge_cells, frames.at[1], h, w)
+        lay_columns(pair_cells, frames.at[0], count, w)
+        lay_columns(edge_cells, frames.at[1], count, w)
+        skip = start - first
+        out = []
         for k in ks:
-            sums = nine_taps(frames.at[0], taps_for(wt, 2 - 2 * odd(), k), h, w)
-            sums += nine_taps(frames.at[1], taps_for(wt, 2 * odd(), k), h, w)
-            yield sums + columns_for(before, k)
-
-    def second_send(*refs):
-        ins, outs, frames = refs[:7], refs[7:-1], refs[-1]
-        for out, sums in zip(outs, beside(*ins, frames, others)):
-            out[...] = sums.astype(BF16)
+            sums = columns_for(before, slice(start * w, stop * w), k)
+            taps = taps_for(wt, 2 - 2 * odd(), k)
+            sums += nine_taps(frames.at[0], taps, stop - start, w, skip)
+            taps = taps_for(wt, 2 * odd(), k)
+            sums += nine_taps(frames.at[1], taps, stop - start, w, skip)
+            out.append(sums)
+        return out
+
+    def send_rows(start, stop):
+        def kernel(*refs):
+            ins, outs, frames = refs[:7], refs[7:-1], refs[-1]
+            for out, sums in zip(outs, beside_rows(*ins, frames, others, start, stop)):
+                out[...] = sums.astype(BF16)
+
+        return kernel
+
+    two_frames = [pltpu.VMEM((2, (h + 2) * w, 3 * ob), BF16)]
+    beside_in = (*pair_hidden, next_edge, onward, b_first, w_second, second)
+    chunks = [(0, h // 2), (h // 2, h)]
+    parts = []
+    for start, stop in chunks:
+        sends = run(
+            send_rows(start, stop),
+            [sds(((stop - start) * w, own_out), BF16)] * (nc - 1),
+            beside_in,
+            two_frames,
+        )
+        parts.append([round_chan(sends[k - 1], k) for k in others])
 
     def second_keep(*refs):
         ins, (b, out, frames) = refs[:7], refs[7:]
-        for sums in beside(*ins, frames, [0]):
-            out[...] = sums + b[...]
-
-    two_frames = [pltpu.VMEM((2, (h + 2) * w, 3 * ob), BF16)]
-    beside_in = (*pair_hidden, next_edge, onward, b_first, w_second, second)
-    sends = run(second_send, [sds((hw, own_out), BF16)] * (nc - 1), beside_in, two_frames)
-    parts = [round_chan(sends[k - 1], k) for k in others]
+        out[...] = beside_rows(*ins, frames, [0], 0, h)[0] + b[...]
+
     kept = run(
         second_keep,
         sds((hw, own_out), F32),
@@ -264,11 +285,17 @@
 
     def finish(kept_ref, *refs):
         total, out = kept_ref[...], refs[-1]
-        for ref in refs[:-1]:
-            total += ref[...].astype(F32)
+        for k in range(nc - 1):
+            pieces_in = [refs[i * (nc - 1) + k][...] for i in range(len(chunks))]
+            total += jnp.concatenate(pieces_in, axis=0).astype(F32)
         out[...] = channels_first(jnp.maximum(total, 0.0), h, w).astype(BF16)
 
-    result = run(finish, sds((own_out, h, w), BF16), (kept, *parts), flops=2 * hw * own_out)
+    result = run(
+        finish,
+        sds((own_out, h, w), BF16),
+        (kept, *[x for part in parts for x in part]),
+        flops=2 * hw * own_out,
+    )
     return result.reshape(own_out, 1, h, w)
 
 

time: 33.9 us -> 33.3 us (0.982)
  waiting for transfers between devices: 9.67 us -> 8.46 us
  starting transfers between devices: 12.8 us -> 13.2 us
    ppermute x3 -> x4, waiting for transfers between devices: 5.51 us -> 4.32 us  [per_device(): lax.ppermute(x, 'chan', [(i, (i + k) % nc) for i in range(nc)])]
    ppermute x3 -> x4, starting transfers between devices: 2.77 us -> 3.19 us  [per_device(): lax.ppermute(x, 'chan', [(i, (i + k) % nc) for i in range(nc)])]
    pallas_call x10 -> x11, Pallas kernels: 10.1 us -> 10.2 us  [run(): pl.pallas_call(kernel, out_shape=outs, scratch_shapes=scratch, compiler_p...]
  transfers between devices with their start and end apart: 9 -> 10, of which waited for: 6 -> 7; matrix products, arithmetic and copies ran while one was open for 0% -> 0% of each run, Pallas kernels for 23% -> 26%
where the time goes in v5:
time: 33.3 us; the launch traced here: 33.1 us
  starting transfers between devices  13.2 us (40%)
  Pallas kernels  10.2 us (31%)
  waiting for transfers between devices  8.46 us (25%)
  local copies, waits for them, and re-layouts  0.99 us (3%)
    pallas_call x11, Pallas kernels, run(): pl.pallas_call(kernel, out_shape=outs, scratch_shapes=scratch, compiler_p...  10.2 us
    ppermute x2, starting transfers between devices, per_device(): next_chip = lambda x: lax.ppermute(x, 'space', beside)  7.87 us
    ppermute x4, waiting for transfers between devices, per_device(): lax.ppermute(x, 'chan', [(i, (i + k) % nc) for i in range(nc)])  4.32 us
    ppermute x2, waiting for transfers between devices, per_device(): next_chip = lambda x: lax.ppermute(x, 'space', beside)  3.99 us
    ppermute x4, starting transfers between devices, per_device(): lax.ppermute(x, 'chan', [(i, (i + k) % nc) for i in range(nc)])  3.19 us
    ppermute x4, starting transfers between devices, per_device(): in_chip = lambda x: lax.ppermute(x, 'space', pairs)  2.19 us
    unnamed x10, local copies, waits for them, and re-layouts  0.97 us
  transfers between devices with their start and end apart: 10, of which 7 were waited for; matrix products, arithmetic and copies ran while one was open for 0% of the time, Pallas kernels for 26%

profile of v5, /device:TPU:9, one launch (start us, length us, event | category | flops | bytes accessed | tf_op | source)
XLA Modules:
  0.0 33.1 jit_solution(169100656562629652)
XLA Ops:
  0.0 0.0 copy-start
  0.0 1.2 %collective-permute-start = (bf16[128,8,128]{2,1,0:T(8,128)(2,1)}, bf16[128,8,128]{2,1,0:T(8,128)(2,1)S(1)}, u32[]{:S(2)}, u32[]{:S(2)}) collective-permute-start(bf16[128,8,128]{2,1,0:T(8,128)(2,1)} %bitcast.22), channel_id=1, source_target_pairs={{0,1},{1,0},{2,3},{3,2},{4,5},{5,4},{6,7},{7,6},{8,9},{9,8},{10,11... | collective-permute-start | bytes 786440 | tf_op jit(solution)/shard_map/ppermute | solution.py:99
  1.2 3.9 %collective-permute-start.1 = (bf16[128,8,128]{2,1,0:T(8,128)(2,1)}, bf16[128,8,128]{2,1,0:T(8,128)(2,1)S(1)}, u32[]{:S(2)}, u32[]{:S(2)}) collective-permute-start(bf16[128,8,128]{2,1,0:T(8,128)(2,1)} %bitcast.23), channel_id=1, source_target_pairs={{2,4},{6,8},{10,12},{14,16},{18,20},{22,24},{26,28},{4,2},{8,6},{1... | collective-permute-start | bytes 786440 | tf_op jit(solution)/shard_map/ppermute | solution.py:98
  5.2 0.1 collective-permute-start.3
  5.3 0.0 copy-start.4
  5.3 0.9 %copy-done.4 = bf16[128,1,8,128]{3,2,1,0:T(8,128)(2,1)S(1)} copy-done((bf16[128,1,8,128]{3,2,1,0:T(8,128)(2,1)S(1)}, bf16[128,1,8,128]{3,2,1,0:T(8,128)(2,1)}, u32[]{:S(2)}) %copy-start.4) | copy-done | bytes 262168
  6.2 0.2 shard_map.55.framed
  6.4 0.0 copy-done
  6.5 0.9 %shard_map.56.refs_2_ = f32[1024,256]{1,0:T(8,128)S(1)} custom-call(bf16[1280,384]{1,0:T(8,128)(2,1)S(1)} %shard_map.55.framed, bf16[27,256,128]{2,1,0:T(8,128)(2,1)S(1)} %bitcast.8), custom_call_target="tpu_custom_call" | custom-call | flops 603979776 | bytes 2752512 | tf_op jit(solution)/shard_map/pallas_call | solution.py:23
  7.3 0.1 collective-permute-done.refs_0_
  7.4 1.5 %collective-permute-start.4 = (bf16[128,8,128]{2,1,0:T(8,128)(2,1)S(1)}, bf16[128,8,128]{2,1,0:T(8,128)(2,1)S(1)}, u32[]{:S(2)}, u32[]{:S(2)}) collective-permute-start(bf16[128,8,128]{2,1,0:T(8,128)(2,1)S(1)} %collective-permute-done.refs_0_), channel_id=1, source_target_pairs={{0,2},{2,0},{4,6},{6,4},{8,10},{10,8},{12,14},{14,12},{16,18},{18,... | collective-permute-start | bytes 786440 | tf_op jit(solution)/shard_map/ppermute | solution.py:97
  8.9 0.9 %shard_map.57 = (f32[1024,128]{1,0:T(8,128)S(1)}, f32[1024,128]{1,0:T(8,128)S(1)}) custom-call(bf16[128,8,128]{2,1,0:T(8,128)(2,1)S(1)} %collective-permute-done.refs_0_, bf16[27,256,128]{2,1,0:T(8,128)(2,1)S(1)} %bitcast.9, f32[1024,256]{1,0:T(8,128)S(1)} %shard_map.56.refs_2_), custom_call_target="tpu_custom_call" | custom-call | flops 603979776 | bytes 3080192 | tf_op jit(solution)/shard_map/pallas_call | solution.py:23
  9.9 2.4 %collective-permute-done.1.vol = bf16[128,8,128]{2,1,0:T(8,128)(2,1)S(1)} collective-permute-done((bf16[128,8,128]{2,1,0:T(8,128)(2,1)}, bf16[128,8,128]{2,1,0:T(8,128)(2,1)S(1)}, u32[]{:S(2)}, u32[]{:S(2)}) %collective-permute-start.1) | collective-permute-done | bytes 262176 | tf_op jit(solution)/shard_map/ppermute | solution.py:98
  12.3 0.4 %collective-permute-start.2 = (bf16[128,8,128]{2,1,0:T(8,128)(2,1)S(1)}, bf16[128,8,128]{2,1,0:T(8,128)(2,1)S(1)}, u32[]{:S(2)}, u32[]{:S(2)}) collective-permute-start(bf16[128,8,128]{2,1,0:T(8,128)(2,1)S(1)} %collective-permute-done.1.vol), channel_id=1, source_target_pairs={{0,1},{1,0},{2,3},{3,2},{4,5},{5,4},{6,7},{7,6},{8,9},{9,8},{10,11... | collective-permute-start | bytes 786440 | tf_op jit(solution)/shard_map/ppermute | solution.py:99
  12.6 0.0 collective-permute-done.3.refs_0_
  12.6 0.0 collective-permute-done.4.refs_1_
  12.6 1.6 %shard_map.58 = (f32[1024,128]{1,0:T(8,128)S(1)}, bf16[1024,128]{1,0:T(8,128)(2,1)S(1)}) custom-call(bf16[128,8,128]{2,1,0:T(8,128)(2,1)S(1)} %collective-permute-done.3.refs_0_, bf16[128,8,128]{2,1,0:T(8,128)(2,1)S(1)} %collective-permute-done.4.refs_1_, bf16[27,256,128]{2,1,0:T(8,128)(2,1)S(1)} %bitcast.10, f32[1024,128]{1,0:T(8,128)S(1)} %get-tuple-element.17.refs_3_), custom_call_target="tpu_custom_call" | custom-call | flops 268435456 | bytes 2818048 | tf_op jit(solution)/shard_map/pallas_call | solution.py:23
  14.2 0.0 copy-start.2
  14.2 3.9 %collective-permute-start.7 = (bf16[1024,128]{1,0:T(8,128)(2,1)S(1)}, bf16[1024,128]{1,0:T(8,128)(2,1)S(1)}, u32[]{:S(2)}, u32[]{:S(2)}) collective-permute-start(bf16[1024,128]{1,0:T(8,128)(2,1)S(1)} %get-tuple-element.19), channel_id=1, source_target_pairs={{2,4},{6,8},{10,12},{14,16},{18,20},{22,24},{26,28},{4,2},{8,6},{1... | collective-permute-start | bytes 786440 | tf_op jit(solution)/shard_map/ppermute | solution.py:98
  18.1 0.9 %shard_map.59.refs_2_ = f32[1024,128]{1,0:T(8,128)S(1)} custom-call(bf16[128,8,128]{2,1,0:T(8,128)(2,1)S(1)} %collective-permute-done.1.vol, bf16[27,256,128]{2,1,0:T(8,128)(2,1)S(1)} %bitcast.11, f32[1024,128]{1,0:T(8,128)S(1)} %get-tuple-element.18.sum_ref), custom_call_target="tpu_custom_call" | custom-call | tf_op jit(solution)/shard_map/pallas_call | solution.py:23
  19.0 0.0 copy-start.1
  19.0 0.8 %collective-permute-done.2.refs_0_ = bf16[128,8,128]{2,1,0:T(8,128)(2,1)S(1)} collective-permute-done((bf16[128,8,128]{2,1,0:T(8,128)(2,1)S(1)}, bf16[128,8,128]{2,1,0:T(8,128)(2,1)S(1)}, u32[]{:S(2)}, u32[]{:S(2)}) %collective-permute-start.2) | collective-permute-done | bytes 262176 | tf_op jit(solution)/shard_map/ppermute | solution.py:99
  19.9 0.0 copy-done.2
  19.9 0.9 %shard_map.60.cells = bf16[1024,128]{1,0:T(8,128)(2,1)S(1)} custom-call(bf16[128,8,128]{2,1,0:T(8,128)(2,1)S(1)} %collective-permute-done.2.refs_0_, bf16[27,256,128]{2,1,0:T(8,128)(2,1)S(1)} %bitcast.12, f32[1024,128]{1,0:T(8,128)S(1)} %shard_map.59.refs_2_, f32[1,128]{1,0:T(1,128)S(1)} %bitcast.17), custom_call_target="tpu_custom_call" | custom-call | tf_op jit(solution)/shard_map/pallas_call | solution.py:23
  20.8 0.1 collective-permute-start.5
  20.9 0.5 %collective-permute-start.6 = (bf16[512,128]{1,0:T(8,128)(2,1)S(1)}, bf16[512,128]{1,0:T(8,128)(2,1)S(1)}, u32[]{:S(2)}, u32[]{:S(2)}) collective-permute-start(bf16[512,128]{1,0:T(8,128)(2,1)S(1)} %get-tuple-element.21), channel_id=1, source_target_pairs={{0,2},{2,0},{4,6},{6,4},{8,10},{10,8},{12,14},{14,12},{16,18},{18,... | collective-permute-start | bytes 393224 | tf_op jit(solution)/shard_map/ppermute | solution.py:97
  21.4 0.0 copy-done.1
  21.4 0.9 %shard_map.61.refs_6_ = f32[1024,256]{1,0:T(8,128)S(1)} custom-call(bf16[1024,128]{1,0:T(8,128)(2,1)S(1)} %shard_map.60.cells, bf16[27,128,256]{2,1,0:T(8,128)(2,1)S(1)} %bitcast.13), custom_call_target="tpu_custom_call" | custom-call | tf_op jit(solution)/shard_map/pallas_call | solution.py:23
  22.2 0.0 collective-permute-done.5.refs_0_
  22.3 0.1 collective-permute-done.6.refs_1_
  22.4 1.6 %collective-permute-done.7.refs_2_ = bf16[1024,128]{1,0:T(8,128)(2,1)S(1)} collective-permute-done((bf16[1024,128]{1,0:T(8,128)(2,1)S(1)}, bf16[1024,128]{1,0:T(8,128)(2,1)S(1)}, u32[]{:S(2)}, u32[]{:S(2)}) %collective-permute-start.7) | collective-permute-done | bytes 262176 | tf_op jit(solution)/shard_map/ppermute | solution.py:98
  24.0 0.8 %shard_map.64 = bf16[512,128]{1,0:T(8,128)(2,1)S(1)} custom-call(bf16[512,128]{1,0:T(8,128)(2,1)S(1)} %collective-permute-done.5.refs_0_, bf16[512,128]{1,0:T(8,128)(2,1)S(1)} %collective-permute-done.6.refs_1_, bf16[1024,128]{1,0:T(8,128)(2,1)S(1)} %collective-permute-done.7.refs_2_, f32[1024,128]{1,0:T(8,128)S(1)} %get-tuple-element.20.refs_3_, ...), custom_call_target="tpu_custom_call" | custom-call | tf_op jit(solution)/shard_map/pallas_call | solution.py:23
  24.9 0.0 copy-start.3
  24.9 1.2 %collective-permute-start.9 = (bf16[512,128]{1,0:T(8,128)(2,1)S(1)}, bf16[512,128]{1,0:T(8,128)(2,1)S(1)}, u32[]{:S(2)}, u32[]{:S(2)}) collective-permute-start(bf16[512,128]{1,0:T(8,128)(2,1)S(1)} %shard_map.64), channel_id=1, source_target_pairs={{0,1},{1,0},{2,3},{3,2},{4,5},{5,4},{6,7},{7,6},{8,9},{9,8},{10,11... | collective-permute-start | bytes 393224 | tf_op jit(solution)/shard_map/ppermute | solution.py:99
  26.0 0.8 %shard_map.63 = bf16[512,128]{1,0:T(8,128)(2,1)S(1)} custom-call(bf16[512,128]{1,0:T(8,128)(2,1)S(1)} %collective-permute-done.5.refs_0_, bf16[512,128]{1,0:T(8,128)(2,1)S(1)} %collective-permute-done.6.refs_1_, bf16[1024,128]{1,0:T(8,128)(2,1)S(1)} %collective-permute-done.7.refs_2_, f32[1024,128]{1,0:T(8,128)S(1)} %get-tuple-element.20.refs_3_, ...), custom_call_target="tpu_custom_call" | custom-call | tf_op jit(solution)/shard_map/pallas_call | solution.py:23
  26.8 0.4 %collective-permute-start.8 = (bf16[512,128]{1,0:T(8,128)(2,1)S(1)}, bf16[512,128]{1,0:T(8,128)(2,1)S(1)}, u32[]{:S(2)}, u32[]{:S(2)}) collective-permute-start(bf16[512,128]{1,0:T(8,128)(2,1)S(1)} %shard_map.63), channel_id=1, source_target_pairs={{0,1},{1,0},{2,3},{3,2},{4,5},{5,4},{6,7},{7,6},{8,9},{9,8},{10,11... | collective-permute-start | bytes 393224 | tf_op jit(solution)/shard_map/ppermute | solution.py:99
  27.3 0.0 copy-done.3
  27.3 1.4 %shard_map.62.kept_ref = f32[1024,128]{1,0:T(8,128)S(1)} custom-call(bf16[512,128]{1,0:T(8,128)(2,1)S(1)} %collective-permute-done.5.refs_0_, bf16[512,128]{1,0:T(8,128)(2,1)S(1)} %collective-permute-done.6.refs_1_, bf16[1024,128]{1,0:T(8,128)(2,1)S(1)} %collective-permute-done.7.refs_2_, f32[1024,128]{1,0:T(8,128)S(1)} %get-tuple-element.20.refs_3_, ...), custom_call_target="tpu_custom_call" | custom-call | flops 603979776 | bytes 3867648 | tf_op jit(solution)/shard_map/pallas_call | solution.py:23
  28.7 1.7 %collective-permute-done.9.refs_1_ = bf16[512,128]{1,0:T(8,128)(2,1)S(1)} collective-permute-done((bf16[512,128]{1,0:T(8,128)(2,1)S(1)}, bf16[512,128]{1,0:T(8,128)(2,1)S(1)}, u32[]{:S(2)}, u32[]{:S(2)}) %collective-permute-start.9) | collective-permute-done | bytes 131104 | tf_op jit(solution)/shard_map/ppermute | solution.py:99
  30.4 1.7 %collective-permute-done.8.refs_0_ = bf16[512,128]{1,0:T(8,128)(2,1)S(1)} collective-permute-done((bf16[512,128]{1,0:T(8,128)(2,1)S(1)}, bf16[512,128]{1,0:T(8,128)(2,1)S(1)}, u32[]{:S(2)}, u32[]{:S(2)}) %collective-permute-start.8) | collective-permute-done | bytes 131104 | tf_op jit(solution)/shard_map/ppermute | solution.py:99
  32.1 1.0 %shard_map.65 = bf16[128,8,128]{2,1,0:T(8,128)(2,1)} custom-call(f32[1024,128]{1,0:T(8,128)S(1)} %shard_map.62.kept_ref, bf16[512,128]{1,0:T(8,128)(2,1)S(1)} %collective-permute-done.8.refs_0_, bf16[512,128]{1,0:T(8,128)(2,1)S(1)} %collective-permute-done.9.refs_1_), custom_call_target="tpu_custom_call" | custom-call | flops 262144 | bytes 786432 | tf_op jit(solution)/shard_map/pallas_call | solution.py:23
  (1 shorter events, 0.0 us)
Async XLA Ops:
  0.0 6.4 %copy-start = (bf16[256,27,128]{2,0,1:T(8,128)(2,1)S(1)}, bf16[256,27,128]{2,0,1:T(8,128)(2,1)}, u32[]{:S(2)}) copy-start(bf16[256,27,128]{2,0,1:T(8,128)(2,1)} %param.6) | copy-start | bytes 5308420
  0.0 7.4 %collective-permute-start = (bf16[128,8,128]{2,1,0:T(8,128)(2,1)}, bf16[128,8,128]{2,1,0:T(8,128)(2,1)S(1)}, u32[]{:S(2)}, u32[]{:S(2)}) collective-permute-start(bf16[128,8,128]{2,1,0:T(8,128)(2,1)} %bitcast.22), channel_id=1, source_target_pairs={{0,1},{1,0},{2,3},{3,2},{4,5},{5,4},{6,7},{7,6},{8,9},{9,8},{10,11... | collective-permute-start | bytes 786440 | tf_op jit(solution)/shard_map/ppermute | solution.py:99
  1.2 11.0 %collective-permute-start.1 = (bf16[128,8,128]{2,1,0:T(8,128)(2,1)}, bf16[128,8,128]{2,1,0:T(8,128)(2,1)S(1)}, u32[]{:S(2)}, u32[]{:S(2)}) collective-permute-start(bf16[128,8,128]{2,1,0:T(8,128)(2,1)} %bitcast.23), channel_id=1, source_target_pairs={{2,4},{6,8},{10,12},{14,16},{18,20},{22,24},{26,28},{4,2},{8,6},{1... | collective-permute-start | bytes 786440 | tf_op jit(solution)/shard_map/ppermute | solution.py:98
  5.2 7.4 %collective-permute-start.3 = (bf16[128,8,128]{2,1,0:T(8,128)(2,1)}, bf16[128,8,128]{2,1,0:T(8,128)(2,1)S(1)}, u32[]{:S(2)}, u32[]{:S(2)}) collective-permute-start(bf16[128,8,128]{2,1,0:T(8,128)(2,1)} %bitcast.24), channel_id=1, source_target_pairs={{0,2},{2,0},{4,6},{6,4},{8,10},{10,8},{12,14},{14,12},{16,18},{18,... | collective-permute-start | bytes 786440 | tf_op jit(solution)/shard_map/ppermute | solution.py:97
  5.3 1.0 %copy-start.4 = (bf16[128,1,8,128]{3,2,1,0:T(8,128)(2,1)S(1)}, bf16[128,1,8,128]{3,2,1,0:T(8,128)(2,1)}, u32[]{:S(2)}) copy-start(bf16[128,1,8,128]{3,2,1,0:T(8,128)(2,1)} %param.5) | copy-start | bytes 786436
  7.4 5.2 %collective-permute-start.4 = (bf16[128,8,128]{2,1,0:T(8,128)(2,1)S(1)}, bf16[128,8,128]{2,1,0:T(8,128)(2,1)S(1)}, u32[]{:S(2)}, u32[]{:S(2)}) collective-permute-start(bf16[128,8,128]{2,1,0:T(8,128)(2,1)S(1)} %collective-permute-done.refs_0_), channel_id=1, source_target_pairs={{0,2},{2,0},{4,6},{6,4},{8,10},{10,8},{12,14},{14,12},{16,18},{18,... | collective-permute-start | bytes 786440 | tf_op jit(solution)/shard_map/ppermute | solution.py:97
  12.3 7.6 %collective-permute-start.2 = (bf16[128,8,128]{2,1,0:T(8,128)(2,1)S(1)}, bf16[128,8,128]{2,1,0:T(8,128)(2,1)S(1)}, u32[]{:S(2)}, u32[]{:S(2)}) collective-permute-start(bf16[128,8,128]{2,1,0:T(8,128)(2,1)S(1)} %collective-permute-done.1.vol), channel_id=1, source_target_pairs={{0,1},{1,0},{2,3},{3,2},{4,5},{5,4},{6,7},{7,6},{8,9},{9,8},{10,11... | collective-permute-start | bytes 786440 | tf_op jit(solution)/shard_map/ppermute | solution.py:99
  14.2 5.7 %copy-start.2 = (f32[128]{0:T(128)S(1)}, f32[128]{0:T(128)}, u32[]{:S(2)}) copy-start(f32[128]{0:T(128)} %param.7) | copy-start | bytes 1540
  14.2 9.8 %collective-permute-start.7 = (bf16[1024,128]{1,0:T(8,128)(2,1)S(1)}, bf16[1024,128]{1,0:T(8,128)(2,1)S(1)}, u32[]{:S(2)}, u32[]{:S(2)}) collective-permute-start(bf16[1024,128]{1,0:T(8,128)(2,1)S(1)} %get-tuple-element.19), channel_id=1, source_target_pairs={{2,4},{6,8},{10,12},{14,16},{18,20},{22,24},{26,28},{4,2},{8,6},{1... | collective-permute-start | bytes 786440 | tf_op jit(solution)/shard_map/ppermute | solution.py:98
  19.0 2.4 %copy-start.1 = (bf16[128,27,256]{2,0,1:T(8,128)(2,1)S(1)}, bf16[128,27,256]{2,0,1:T(8,128)(2,1)}, u32[]{:S(2)}) copy-start(bf16[128,27,256]{2,0,1:T(8,128)(2,1)} %param.8) | copy-start | bytes 5308420
  20.8 1.5 %collective-permute-start.5 = (bf16[512,128]{1,0:T(8,128)(2,1)S(1)}, bf16[512,128]{1,0:T(8,128)(2,1)S(1)}, u32[]{:S(2)}, u32[]{:S(2)}) collective-permute-start(bf16[512,128]{1,0:T(8,128)(2,1)S(1)} %get-tuple-element.22), channel_id=1, source_target_pairs={{0,2},{2,0},{4,6},{6,4},{8,10},{10,8},{12,14},{14,12},{16,18},{18,... | collective-permute-start | bytes 393224 | tf_op jit(solution)/shard_map/ppermute | solution.py:97
  20.9 1.5 %collective-permute-start.6 = (bf16[512,128]{1,0:T(8,128)(2,1)S(1)}, bf16[512,128]{1,0:T(8,128)(2,1)S(1)}, u32[]{:S(2)}, u32[]{:S(2)}) collective-permute-start(bf16[512,128]{1,0:T(8,128)(2,1)S(1)} %get-tuple-element.21), channel_id=1, source_target_pairs={{0,2},{2,0},{4,6},{6,4},{8,10},{10,8},{12,14},{14,12},{16,18},{18,... | collective-permute-start | bytes 393224 | tf_op jit(solution)/shard_map/ppermute | solution.py:97
  24.9 2.4 %copy-start.3 = (f32[128]{0:T(128)S(1)}, f32[128]{0:T(128)}, u32[]{:S(2)}) copy-start(f32[128]{0:T(128)} %param.9) | copy-start | bytes 1540
  24.9 5.6 %collective-permute-start.9 = (bf16[512,128]{1,0:T(8,128)(2,1)S(1)}, bf16[512,128]{1,0:T(8,128)(2,1)S(1)}, u32[]{:S(2)}, u32[]{:S(2)}) collective-permute-start(bf16[512,128]{1,0:T(8,128)(2,1)S(1)} %shard_map.64), channel_id=1, source_target_pairs={{0,1},{1,0},{2,3},{3,2},{4,5},{5,4},{6,7},{7,6},{8,9},{9,8},{10,11... | collective-permute-start | bytes 393224 | tf_op jit(solution)/shard_map/ppermute | solution.py:99
  26.8 5.3 %collective-permute-start.8 = (bf16[512,128]{1,0:T(8,128)(2,1)S(1)}, bf16[512,128]{1,0:T(8,128)(2,1)S(1)}, u32[]{:S(2)}, u32[]{:S(2)}) collective-permute-start(bf16[512,128]{1,0:T(8,128)(2,1)S(1)} %shard_map.63), channel_id=1, source_target_pairs={{0,1},{1,0},{2,3},{3,2},{4,5},{5,4},{6,7},{7,6},{8,9},{9,8},{10,11... | collective-permute-start | bytes 393224 | tf_op jit(solution)/shard_map/ppermute | solution.py:99

commit v6 on v5

--- a/solution.py
+++ b/solution.py
@@ -188,22 +188,25 @@
     side = run(first_next, part, (beyond, taps_first, so_far), scratch_in)
 
     def hidden_own(*refs):
-        vols, (wt, side_ref, b, out, framed) = refs[: nc - 1], refs[nc - 1 :]
+        vols, (wt, side_ref, b, top, low, framed) = refs[: nc - 1], refs[nc - 1 :]
         total = side_ref[...]
         for vol, k in zip(vols, others):
             total += spread(framed, vol[...], wt, (from_next,), k)
-        out[...] = jnp.maximum(total + b[...], 0.0).astype(BF16)
-
-    hidden = run(hidden_own, half, (*beyond_rest, taps_first, side, b_first), scratch_in)
-    pair_hidden = [in_chip(hidden[: hw // 2]), in_chip(hidden[hw // 2 :])]
-
-    def second_own(cells, wt, out, framed):
-        lay_columns(cells[...].astype(F32), framed, h, w)
+        cells = jnp.maximum(total + b[...], 0.0).astype(BF16)
+        top[...] = cells[: hw // 2]
+        low[...] = cells[hw // 2 :]
+
+    half_rows = sds((hw // 2, ob), BF16)
+    hidden = run(hidden_own, [half_rows, half_rows], (*beyond_rest, taps_first, side, b_first), scratch_in)
+    pair_hidden = [in_chip(x) for x in hidden]
+
+    def second_own(top, low, wt, out, framed):
+        lay_columns(jnp.concatenate([top[...], low[...]], axis=0).astype(F32), framed, h, w)
         out[...] = nine_taps(framed, depth_taps(1, wt), h, w)
 
     scratch_mid = [pltpu.VMEM(framed_mid.shape, BF16)]
     whole = sds((hw, full), F32)
-    second = run(second_own, whole, (hidden, w_second), scratch_mid)
+    second = run(second_own, whole, (*hidden, w_second), scratch_mid)
     def wanted(k):
         owner = lax.rem(lax.axis_index("chan") + k, nc)
         return pl.ds(pl.multiple_of(owner * own_out, own_out), own_out)

time: 33.3 us -> 33.3 us (level)
  no operation moved by 1% of the time
where the time goes in v6:
time: 33.3 us; the launch traced here: 33 us
  starting transfers between devices  13.2 us (40%)
  Pallas kernels  10.2 us (31%)
  waiting for transfers between devices  8.45 us (25%)
  local copies, waits for them, and re-layouts  0.97 us (3%)
    pallas_call x11, Pallas kernels, run(): pl.pallas_call(kernel, out_shape=outs, scratch_shapes=scratch, compiler_p...  10.2 us
    ppermute x2, starting transfers between devices, per_device(): next_chip = lambda x: lax.ppermute(x, 'space', beside)  7.87 us
    ppermute x4, waiting for transfers between devices, per_device(): lax.ppermute(x, 'chan', [(i, (i + k) % nc) for i in range(nc)])  4.28 us
    ppermute x2, waiting for transfers between devices, per_device(): next_chip = lambda x: lax.ppermute(x, 'space', beside)  4.02 us
    ppermute x4, starting transfers between devices, per_device(): lax.ppermute(x, 'chan', [(i, (i + k) % nc) for i in range(nc)])  3.19 us
    ppermute x4, starting transfers between devices, per_device(): in_chip = lambda x: lax.ppermute(x, 'space', pairs)  2.19 us
    unnamed x10, local copies, waits for them, and re-layouts  0.97 us
  transfers between devices with their start and end apart: 10, of which 7 were waited for; matrix products, arithmetic and copies ran while one was open for 0% of the time, Pallas kernels for 26%

profile of v6, /device:TPU:9, one launch (start us, length us, event | category | flops | bytes accessed | tf_op | source)
XLA Modules:
  0.0 33.0 jit_solution(6488874199008637257)
XLA Ops:
  0.0 0.0 copy-start
  0.0 1.2 %collective-permute-start = (bf16[128,8,128]{2,1,0:T(8,128)(2,1)}, bf16[128,8,128]{2,1,0:T(8,128)(2,1)S(1)}, u32[]{:S(2)}, u32[]{:S(2)}) collective-permute-start(bf16[128,8,128]{2,1,0:T(8,128)(2,1)} %bitcast.22), channel_id=1, source_target_pairs={{0,1},{1,0},{2,3},{3,2},{4,5},{5,4},{6,7},{7,6},{8,9},{9,8},{10,11... | collective-permute-start | bytes 786440 | tf_op jit(solution)/shard_map/ppermute | solution.py:99
  1.2 3.9 %collective-permute-start.1 = (bf16[128,8,128]{2,1,0:T(8,128)(2,1)}, bf16[128,8,128]{2,1,0:T(8,128)(2,1)S(1)}, u32[]{:S(2)}, u32[]{:S(2)}) collective-permute-start(bf16[128,8,128]{2,1,0:T(8,128)(2,1)} %bitcast.23), channel_id=1, source_target_pairs={{2,4},{6,8},{10,12},{14,16},{18,20},{22,24},{26,28},{4,2},{8,6},{1... | collective-permute-start | bytes 786440 | tf_op jit(solution)/shard_map/ppermute | solution.py:98
  5.2 0.1 collective-permute-start.3
  5.3 0.0 copy-start.4
  5.3 0.9 %copy-done.4 = bf16[128,1,8,128]{3,2,1,0:T(8,128)(2,1)S(1)} copy-done((bf16[128,1,8,128]{3,2,1,0:T(8,128)(2,1)S(1)}, bf16[128,1,8,128]{3,2,1,0:T(8,128)(2,1)}, u32[]{:S(2)}) %copy-start.4) | copy-done | bytes 262168
  6.2 0.2 shard_map.55.framed
  6.4 0.0 copy-done
  6.5 0.9 %shard_map.56.refs_2_ = f32[1024,256]{1,0:T(8,128)S(1)} custom-call(bf16[1280,384]{1,0:T(8,128)(2,1)S(1)} %shard_map.55.framed, bf16[27,256,128]{2,1,0:T(8,128)(2,1)S(1)} %bitcast.8), custom_call_target="tpu_custom_call" | custom-call | flops 603979776 | bytes 2752512 | tf_op jit(solution)/shard_map/pallas_call | solution.py:23
  7.3 0.1 collective-permute-done.refs_0_
  7.4 1.5 %collective-permute-start.4 = (bf16[128,8,128]{2,1,0:T(8,128)(2,1)S(1)}, bf16[128,8,128]{2,1,0:T(8,128)(2,1)S(1)}, u32[]{:S(2)}, u32[]{:S(2)}) collective-permute-start(bf16[128,8,128]{2,1,0:T(8,128)(2,1)S(1)} %collective-permute-done.refs_0_), channel_id=1, source_target_pairs={{0,2},{2,0},{4,6},{6,4},{8,10},{10,8},{12,14},{14,12},{16,18},{18,... | collective-permute-start | bytes 786440 | tf_op jit(solution)/shard_map/ppermute | solution.py:97
  8.9 0.9 %shard_map.57 = (f32[1024,128]{1,0:T(8,128)S(1)}, f32[1024,128]{1,0:T(8,128)S(1)}) custom-call(bf16[128,8,128]{2,1,0:T(8,128)(2,1)S(1)} %collective-permute-done.refs_0_, bf16[27,256,128]{2,1,0:T(8,128)(2,1)S(1)} %bitcast.9, f32[1024,256]{1,0:T(8,128)S(1)} %shard_map.56.refs_2_), custom_call_target="tpu_custom_call" | custom-call | flops 603979776 | bytes 3080192 | tf_op jit(solution)/shard_map/pallas_call | solution.py:23
  9.9 2.4 %collective-permute-done.1.vol = bf16[128,8,128]{2,1,0:T(8,128)(2,1)S(1)} collective-permute-done((bf16[128,8,128]{2,1,0:T(8,128)(2,1)}, bf16[128,8,128]{2,1,0:T(8,128)(2,1)S(1)}, u32[]{:S(2)}, u32[]{:S(2)}) %collective-permute-start.1) | collective-permute-done | bytes 262176 | tf_op jit(solution)/shard_map/ppermute | solution.py:98
  12.3 0.4 %collective-permute-start.2 = (bf16[128,8,128]{2,1,0:T(8,128)(2,1)S(1)}, bf16[128,8,128]{2,1,0:T(8,128)(2,1)S(1)}, u32[]{:S(2)}, u32[]{:S(2)}) collective-permute-start(bf16[128,8,128]{2,1,0:T(8,128)(2,1)S(1)} %collective-permute-done.1.vol), channel_id=1, source_target_pairs={{0,1},{1,0},{2,3},{3,2},{4,5},{5,4},{6,7},{7,6},{8,9},{9,8},{10,11... | collective-permute-start | bytes 786440 | tf_op jit(solution)/shard_map/ppermute | solution.py:99
  12.6 0.0 collective-permute-done.3.refs_0_
  12.6 0.0 collective-permute-done.4.refs_1_
  12.6 1.6 %shard_map.58 = (f32[1024,128]{1,0:T(8,128)S(1)}, bf16[1024,128]{1,0:T(8,128)(2,1)S(1)}) custom-call(bf16[128,8,128]{2,1,0:T(8,128)(2,1)S(1)} %collective-permute-done.3.refs_0_, bf16[128,8,128]{2,1,0:T(8,128)(2,1)S(1)} %collective-permute-done.4.refs_1_, bf16[27,256,128]{2,1,0:T(8,128)(2,1)S(1)} %bitcast.10, f32[1024,128]{1,0:T(8,128)S(1)} %get-tuple-element.19.refs_3_), custom_call_target="tpu_custom_call" | custom-call | flops 268435456 | bytes 2818048 | tf_op jit(solution)/shard_map/pallas_call | solution.py:23
  14.2 0.0 copy-start.2
  14.2 3.9 %collective-permute-start.7 = (bf16[1024,128]{1,0:T(8,128)(2,1)S(1)}, bf16[1024,128]{1,0:T(8,128)(2,1)S(1)}, u32[]{:S(2)}, u32[]{:S(2)}) collective-permute-start(bf16[1024,128]{1,0:T(8,128)(2,1)S(1)} %get-tuple-element.23), channel_id=1, source_target_pairs={{2,4},{6,8},{10,12},{14,16},{18,20},{22,24},{26,28},{4,2},{8,6},{1... | collective-permute-start | bytes 786440 | tf_op jit(solution)/shard_map/ppermute | solution.py:98
  18.1 0.9 %shard_map.59.refs_2_ = f32[1024,128]{1,0:T(8,128)S(1)} custom-call(bf16[128,8,128]{2,1,0:T(8,128)(2,1)S(1)} %collective-permute-done.1.vol, bf16[27,256,128]{2,1,0:T(8,128)(2,1)S(1)} %bitcast.11, f32[1024,128]{1,0:T(8,128)S(1)} %get-tuple-element.20.sum_ref), custom_call_target="tpu_custom_call" | custom-call | tf_op jit(solution)/shard_map/pallas_call | solution.py:23
  19.0 0.0 copy-start.1
  19.0 0.8 %collective-permute-done.2.refs_0_ = bf16[128,8,128]{2,1,0:T(8,128)(2,1)S(1)} collective-permute-done((bf16[128,8,128]{2,1,0:T(8,128)(2,1)S(1)}, bf16[128,8,128]{2,1,0:T(8,128)(2,1)S(1)}, u32[]{:S(2)}, u32[]{:S(2)}) %collective-permute-start.2) | collective-permute-done | bytes 262176 | tf_op jit(solution)/shard_map/ppermute | solution.py:99
  19.9 0.0 copy-done.2
  19.9 0.9 %shard_map.60 = (bf16[512,128]{1,0:T(8,128)(2,1)S(1)}, bf16[512,128]{1,0:T(8,128)(2,1)S(1)}) custom-call(bf16[128,8,128]{2,1,0:T(8,128)(2,1)S(1)} %collective-permute-done.2.refs_0_, bf16[27,256,128]{2,1,0:T(8,128)(2,1)S(1)} %bitcast.12, f32[1024,128]{1,0:T(8,128)S(1)} %shard_map.59.refs_2_, f32[1,128]{1,0:T(1,128)S(1)} %bitcast.17), custom_call_target="tpu_custom_call" | custom-call | tf_op jit(solution)/shard_map/pallas_call | solution.py:23
  20.8 0.1 collective-permute-start.5
  20.9 0.5 %collective-permute-start.6 = (bf16[512,128]{1,0:T(8,128)(2,1)S(1)}, bf16[512,128]{1,0:T(8,128)(2,1)S(1)}, u32[]{:S(2)}, u32[]{:S(2)}) collective-permute-start(bf16[512,128]{1,0:T(8,128)(2,1)S(1)} %get-tuple-element.22.low), channel_id=1, source_target_pairs={{0,2},{2,0},{4,6},{6,4},{8,10},{10,8},{12,14},{14,12},{16,18},{18,... | collective-permute-start | bytes 393224 | tf_op jit(solution)/shard_map/ppermute | solution.py:97
  21.4 0.0 copy-done.1
  21.4 0.9 %shard_map.61.refs_6_ = f32[1024,256]{1,0:T(8,128)S(1)} custom-call(bf16[512,128]{1,0:T(8,128)(2,1)S(1)} %get-tuple-element.21.top, bf16[512,128]{1,0:T(8,128)(2,1)S(1)} %get-tuple-element.22.low, bf16[27,128,256]{2,1,0:T(8,128)(2,1)S(1)} %bitcast.13), custom_call_target="tpu_custom_call" | custom-call | tf_op jit(solution)/shard_map/pallas_call | solution.py:23
  22.2 0.0 collective-permute-done.5.refs_0_
  22.2 0.1 collective-permute-done.6.refs_1_
  22.4 1.7 %collective-permute-done.7.refs_2_ = bf16[1024,128]{1,0:T(8,128)(2,1)S(1)} collective-permute-done((bf16[1024,128]{1,0:T(8,128)(2,1)S(1)}, bf16[1024,128]{1,0:T(8,128)(2,1)S(1)}, u32[]{:S(2)}, u32[]{:S(2)}) %collective-permute-start.7) | collective-permute-done | bytes 262176 | tf_op jit(solution)/shard_map/ppermute | solution.py:98
  24.0 0.8 %shard_map.64 = bf16[512,128]{1,0:T(8,128)(2,1)S(1)} custom-call(bf16[512,128]{1,0:T(8,128)(2,1)S(1)} %collective-permute-done.5.refs_0_, bf16[512,128]{1,0:T(8,128)(2,1)S(1)} %collective-permute-done.6.refs_1_, bf16[1024,128]{1,0:T(8,128)(2,1)S(1)} %collective-permute-done.7.refs_2_, f32[1024,128]{1,0:T(8,128)S(1)} %get-tuple-element.24.refs_3_, ...), custom_call_target="tpu_custom_call" | custom-call | tf_op jit(solution)/shard_map/pallas_call | solution.py:23
  24.8 0.0 copy-start.3
  24.9 1.2 %collective-permute-start.9 = (bf16[512,128]{1,0:T(8,128)(2,1)S(1)}, bf16[512,128]{1,0:T(8,128)(2,1)S(1)}, u32[]{:S(2)}, u32[]{:S(2)}) collective-permute-start(bf16[512,128]{1,0:T(8,128)(2,1)S(1)} %shard_map.64), channel_id=1, source_target_pairs={{0,1},{1,0},{2,3},{3,2},{4,5},{5,4},{6,7},{7,6},{8,9},{9,8},{10,11... | collective-permute-start | bytes 393224 | tf_op jit(solution)/shard_map/ppermute | solution.py:99
  26.0 0.8 %shard_map.63 = bf16[512,128]{1,0:T(8,128)(2,1)S(1)} custom-call(bf16[512,128]{1,0:T(8,128)(2,1)S(1)} %collective-permute-done.5.refs_0_, bf16[512,128]{1,0:T(8,128)(2,1)S(1)} %collective-permute-done.6.refs_1_, bf16[1024,128]{1,0:T(8,128)(2,1)S(1)} %collective-permute-done.7.refs_2_, f32[1024,128]{1,0:T(8,128)S(1)} %get-tuple-element.24.refs_3_, ...), custom_call_target="tpu_custom_call" | custom-call | tf_op jit(solution)/shard_map/pallas_call | solution.py:23
  26.8 0.4 %collective-permute-start.8 = (bf16[512,128]{1,0:T(8,128)(2,1)S(1)}, bf16[512,128]{1,0:T(8,128)(2,1)S(1)}, u32[]{:S(2)}, u32[]{:S(2)}) collective-permute-start(bf16[512,128]{1,0:T(8,128)(2,1)S(1)} %shard_map.63), channel_id=1, source_target_pairs={{0,1},{1,0},{2,3},{3,2},{4,5},{5,4},{6,7},{7,6},{8,9},{9,8},{10,11... | collective-permute-start | bytes 393224 | tf_op jit(solution)/shard_map/ppermute | solution.py:99
  27.3 0.0 copy-done.3
  27.3 1.4 %shard_map.62.kept_ref = f32[1024,128]{1,0:T(8,128)S(1)} custom-call(bf16[512,128]{1,0:T(8,128)(2,1)S(1)} %collective-permute-done.5.refs_0_, bf16[512,128]{1,0:T(8,128)(2,1)S(1)} %collective-permute-done.6.refs_1_, bf16[1024,128]{1,0:T(8,128)(2,1)S(1)} %collective-permute-done.7.refs_2_, f32[1024,128]{1,0:T(8,128)S(1)} %get-tuple-element.24.refs_3_, ...), custom_call_target="tpu_custom_call" | custom-call | flops 603979776 | bytes 3867648 | tf_op jit(solution)/shard_map/pallas_call | solution.py:23
  28.7 1.7 %collective-permute-done.9.refs_1_ = bf16[512,128]{1,0:T(8,128)(2,1)S(1)} collective-permute-done((bf16[512,128]{1,0:T(8,128)(2,1)S(1)}, bf16[512,128]{1,0:T(8,128)(2,1)S(1)}, u32[]{:S(2)}, u32[]{:S(2)}) %collective-permute-start.9) | collective-permute-done | bytes 131104 | tf_op jit(solution)/shard_map/ppermute | solution.py:99
  30.4 1.7 %collective-permute-done.8.refs_0_ = bf16[512,128]{1,0:T(8,128)(2,1)S(1)} collective-permute-done((bf16[512,128]{1,0:T(8,128)(2,1)S(1)}, bf16[512,128]{1,0:T(8,128)(2,1)S(1)}, u32[]{:S(2)}, u32[]{:S(2)}) %collective-permute-start.8) | collective-permute-done | bytes 131104 | tf_op jit(solution)/shard_map/ppermute | solution.py:99
  32.1 1.0 %shard_map.65 = bf16[128,8,128]{2,1,0:T(8,128)(2,1)} custom-call(f32[1024,128]{1,0:T(8,128)S(1)} %shard_map.62.kept_ref, bf16[512,128]{1,0:T(8,128)(2,1)S(1)} %collective-permute-done.8.refs_0_, bf16[512,128]{1,0:T(8,128)(2,1)S(1)} %collective-permute-done.9.refs_1_), custom_call_target="tpu_custom_call" | custom-call | flops 262144 | bytes 786432 | tf_op jit(solution)/shard_map/pallas_call | solution.py:23
Async XLA Ops:
  0.0 6.4 %copy-start = (bf16[256,27,128]{2,0,1:T(8,128)(2,1)S(1)}, bf16[256,27,128]{2,0,1:T(8,128)(2,1)}, u32[]{:S(2)}) copy-start(bf16[256,27,128]{2,0,1:T(8,128)(2,1)} %param.6) | copy-start | bytes 5308420
  0.0 7.4 %collective-permute-start = (bf16[128,8,128]{2,1,0:T(8,128)(2,1)}, bf16[128,8,128]{2,1,0:T(8,128)(2,1)S(1)}, u32[]{:S(2)}, u32[]{:S(2)}) collective-permute-start(bf16[128,8,128]{2,1,0:T(8,128)(2,1)} %bitcast.22), channel_id=1, source_target_pairs={{0,1},{1,0},{2,3},{3,2},{4,5},{5,4},{6,7},{7,6},{8,9},{9,8},{10,11... | collective-permute-start | bytes 786440 | tf_op jit(solution)/shard_map/ppermute | solution.py:99
  1.2 11.0 %collective-permute-start.1 = (bf16[128,8,128]{2,1,0:T(8,128)(2,1)}, bf16[128,8,128]{2,1,0:T(8,128)(2,1)S(1)}, u32[]{:S(2)}, u32[]{:S(2)}) collective-permute-start(bf16[128,8,128]{2,1,0:T(8,128)(2,1)} %bitcast.23), channel_id=1, source_target_pairs={{2,4},{6,8},{10,12},{14,16},{18,20},{22,24},{26,28},{4,2},{8,6},{1... | collective-permute-start | bytes 786440 | tf_op jit(solution)/shard_map/ppermute | solution.py:98
  5.2 7.4 %collective-permute-start.3 = (bf16[128,8,128]{2,1,0:T(8,128)(2,1)}, bf16[128,8,128]{2,1,0:T(8,128)(2,1)S(1)}, u32[]{:S(2)}, u32[]{:S(2)}) collective-permute-start(bf16[128,8,128]{2,1,0:T(8,128)(2,1)} %bitcast.24), channel_id=1, source_target_pairs={{0,2},{2,0},{4,6},{6,4},{8,10},{10,8},{12,14},{14,12},{16,18},{18,... | collective-permute-start | bytes 786440 | tf_op jit(solution)/shard_map/ppermute | solution.py:97
  5.3 1.0 %copy-start.4 = (bf16[128,1,8,128]{3,2,1,0:T(8,128)(2,1)S(1)}, bf16[128,1,8,128]{3,2,1,0:T(8,128)(2,1)}, u32[]{:S(2)}) copy-start(bf16[128,1,8,128]{3,2,1,0:T(8,128)(2,1)} %param.5) | copy-start | bytes 786436
  7.4 5.2 %collective-permute-start.4 = (bf16[128,8,128]{2,1,0:T(8,128)(2,1)S(1)}, bf16[128,8,128]{2,1,0:T(8,128)(2,1)S(1)}, u32[]{:S(2)}, u32[]{:S(2)}) collective-permute-start(bf16[128,8,128]{2,1,0:T(8,128)(2,1)S(1)} %collective-permute-done.refs_0_), channel_id=1, source_target_pairs={{0,2},{2,0},{4,6},{6,4},{8,10},{10,8},{12,14},{14,12},{16,18},{18,... | collective-permute-start | bytes 786440 | tf_op jit(solution)/shard_map/ppermute | solution.py:97
  12.3 7.6 %collective-permute-start.2 = (bf16[128,8,128]{2,1,0:T(8,128)(2,1)S(1)}, bf16[128,8,128]{2,1,0:T(8,128)(2,1)S(1)}, u32[]{:S(2)}, u32[]{:S(2)}) collective-permute-start(bf16[128,8,128]{2,1,0:T(8,128)(2,1)S(1)} %collective-permute-done.1.vol), channel_id=1, source_target_pairs={{0,1},{1,0},{2,3},{3,2},{4,5},{5,4},{6,7},{7,6},{8,9},{9,8},{10,11... | collective-permute-start | bytes 786440 | tf_op jit(solution)/shard_map/ppermute | solution.py:99
  14.2 5.7 %copy-start.2 = (f32[128]{0:T(128)S(1)}, f32[128]{0:T(128)}, u32[]{:S(2)}) copy-start(f32[128]{0:T(128)} %param.7) | copy-start | bytes 1540
  14.2 9.8 %collective-permute-start.7 = (bf16[1024,128]{1,0:T(8,128)(2,1)S(1)}, bf16[1024,128]{1,0:T(8,128)(2,1)S(1)}, u32[]{:S(2)}, u32[]{:S(2)}) collective-permute-start(bf16[1024,128]{1,0:T(8,128)(2,1)S(1)} %get-tuple-element.23), channel_id=1, source_target_pairs={{2,4},{6,8},{10,12},{14,16},{18,20},{22,24},{26,28},{4,2},{8,6},{1... | collective-permute-start | bytes 786440 | tf_op jit(solution)/shard_map/ppermute | solution.py:98
  19.0 2.3 %copy-start.1 = (bf16[128,27,256]{2,0,1:T(8,128)(2,1)S(1)}, bf16[128,27,256]{2,0,1:T(8,128)(2,1)}, u32[]{:S(2)}) copy-start(bf16[128,27,256]{2,0,1:T(8,128)(2,1)} %param.8) | copy-start | bytes 5308420
  20.8 1.5 %collective-permute-start.5 = (bf16[512,128]{1,0:T(8,128)(2,1)S(1)}, bf16[512,128]{1,0:T(8,128)(2,1)S(1)}, u32[]{:S(2)}, u32[]{:S(2)}) collective-permute-start(bf16[512,128]{1,0:T(8,128)(2,1)S(1)} %get-tuple-element.21.top), channel_id=1, source_target_pairs={{0,2},{2,0},{4,6},{6,4},{8,10},{10,8},{12,14},{14,12},{16,18},{18,... | collective-permute-start | bytes 393224 | tf_op jit(solution)/shard_map/ppermute | solution.py:97
  20.9 1.5 %collective-permute-start.6 = (bf16[512,128]{1,0:T(8,128)(2,1)S(1)}, bf16[512,128]{1,0:T(8,128)(2,1)S(1)}, u32[]{:S(2)}, u32[]{:S(2)}) collective-permute-start(bf16[512,128]{1,0:T(8,128)(2,1)S(1)} %get-tuple-element.22.low), channel_id=1, source_target_pairs={{0,2},{2,0},{4,6},{6,4},{8,10},{10,8},{12,14},{14,12},{16,18},{18,... | collective-permute-start | bytes 393224 | tf_op jit(solution)/shard_map/ppermute | solution.py:97
  24.8 2.4 %copy-start.3 = (f32[128]{0:T(128)S(1)}, f32[128]{0:T(128)}, u32[]{:S(2)}) copy-start(f32[128]{0:T(128)} %param.9) | copy-start | bytes 1540
  24.9 5.6 %collective-permute-start.9 = (bf16[512,128]{1,0:T(8,128)(2,1)S(1)}, bf16[512,128]{1,0:T(8,128)(2,1)S(1)}, u32[]{:S(2)}, u32[]{:S(2)}) collective-permute-start(bf16[512,128]{1,0:T(8,128)(2,1)S(1)} %shard_map.64), channel_id=1, source_target_pairs={{0,1},{1,0},{2,3},{3,2},{4,5},{5,4},{6,7},{7,6},{8,9},{9,8},{10,11... | collective-permute-start | bytes 393224 | tf_op jit(solution)/shard_map/ppermute | solution.py:99
  26.8 5.3 %collective-permute-start.8 = (bf16[512,128]{1,0:T(8,128)(2,1)S(1)}, bf16[512,128]{1,0:T(8,128)(2,1)S(1)}, u32[]{:S(2)}, u32[]{:S(2)}) collective-permute-start(bf16[512,128]{1,0:T(8,128)(2,1)S(1)} %shard_map.63), channel_id=1, source_target_pairs={{0,1},{1,0},{2,3},{3,2},{4,5},{5,4},{6,7},{7,6},{8,9},{9,8},{10,11... | collective-permute-start | bytes 393224 | tf_op jit(solution)/shard_map/ppermute | solution.py:99
